TPU v7x, 512 devices: a whole 4x8x8 slice. The times are simulated.
512 devices in a mesh: row: 32 (over y, x), col: 16 (over z, core).
Axes of the slice: x: 4, y: 8, z: 8, core: 2. Of those that a mesh axis runs over, the one named last changes fastest.
Arguments:
- blocks: bfloat16 [32, 16, 2, 8, 128, 128], P('row', 'col'), may hold values from -4 to 4
- block_rows: int32 [32, 16, 2, 8], P('row', 'col'), may hold values from 0 to 4, as said below
- block_cols: int32 [32, 16, 2, 8], P('row', 'col'), may hold values from 0 to 4, as said below
- counts: int32 [32, 16, 2], P('row', 'col'), may hold values from 2 to 8, as said below
Outputs:
- square: bfloat16 [20480, 20480], P('row', 'col')
- trace_value: float32 [], replicated
Inputs may be any that keep to these rules, and one draw needn't show every extreme that they name: `block_rows`: in every (row panel, column panel, group) the 8 slots name distinct block positions; a slot holds data only if its index is below the group's count. `block_cols`: together with block_rows each slot names a distinct position of the 5 x 5 grid of its group. `counts`: some group is full in every draw.
All inputs are finite; a program needn't handle non-finite values.
Results may differ from a plain program's by a relative error of at most 0.001.
Values may be sent and summed in bfloat16 or wider, within the bound.
A program may use at most 64 MiB of HBM per device.

v0:
```python
import math

import jax
import jax.numpy as jnp
from jax import lax
from jax.sharding import PartitionSpec as P

RB = 5
STEPS = 4


def as_sent(shard):
    return jax.tree.map(lambda a: a.astype(jnp.bfloat16) if a.dtype == jnp.float32 else a, shard)


def passed_along(block, axis, distance):
    devices = range(lax.axis_size(axis))
    route = [((i - distance) % len(devices), i) for i in devices]
    return lax.ppermute(block, axis, route)


def densify(pieces, rows, cols, nrows, ncols):
    width = pieces.shape[-1]
    count = pieces.shape[0]
    places = rows * ncols + cols
    onehot = (places[None, :] == jnp.arange(nrows * ncols, dtype=jnp.int32)[:, None]).astype(
        pieces.dtype
    )
    dense = jnp.dot(
        onehot, pieces.reshape(count, width * width), preferred_element_type=jnp.float32
    )
    dense = dense.reshape(nrows, ncols, width, width).transpose(0, 2, 1, 3)
    return dense.reshape(nrows * width, ncols * width).astype(pieces.dtype)


def pick(flag, kept, moved):
    return jax.tree.map(lambda first, second: jnp.where(flag, second, first), kept, moved)


def body(blocks, block_rows, block_cols, counts):
    groups = blocks.shape[2]
    slot_count = blocks.shape[3]
    width = blocks.shape[4]
    row_count = lax.axis_size("row")
    col_count = lax.axis_size("col")
    row_place = lax.axis_index("row")
    col_place = lax.axis_index("col")
    upper = row_place // groups
    lower = row_place % groups
    filled = counts[0, 0]
    live = jnp.arange(slot_count, dtype=jnp.int32)[None, :] < filled[:, None]
    masked = blocks[0, 0] * live[..., None, None].astype(blocks.dtype)
    rows_here = block_rows[0, 0]
    offsets = (jnp.arange(groups, dtype=jnp.int32) * RB)[:, None]
    cols_here = block_cols[0, 0] + offsets
    left_pieces = lax.dynamic_index_in_dim(masked, lower, 0, keepdims=False)
    left_rows = lax.dynamic_index_in_dim(rows_here, lower, 0, keepdims=False)
    left_cols = lax.dynamic_index_in_dim(block_cols[0, 0], lower, 0, keepdims=False)
    left = (left_pieces, left_rows, left_cols)
    right = (masked, rows_here, cols_here)
    left_move = (col_count - upper % col_count) % col_count
    for bit in range((col_count - 1).bit_length()):
        moved = jax.tree.map(
            lambda part, own: part.astype(own.dtype),
            passed_along(as_sent(left), "col", 1 << bit),
            left,
        )
        left = pick(left_move >> bit & 1 == 1, left, moved)
    right_move = (row_count - groups * col_place % row_count) % row_count
    for bit in range((row_count - 1).bit_length()):
        moved = jax.tree.map(
            lambda part, own: part.astype(own.dtype),
            passed_along(as_sent(right), "row", 1 << bit),
            right,
        )
        right = pick(right_move >> bit & 1 == 1, right, moved)
    totals = jnp.zeros((RB * width, groups * RB * width), jnp.float32)
    for step in range(STEPS):
        if step > 0:
            left = jax.tree.map(
                lambda part, own: part.astype(own.dtype),
                passed_along(as_sent(left), "col", col_count - 1),
                left,
            )
            right = jax.tree.map(
                lambda part, own: part.astype(own.dtype),
                passed_along(as_sent(right), "row", row_count - groups),
                right,
            )
        right_dense = densify(
            right[0].reshape(groups * slot_count, width, width),
            right[1].reshape(-1),
            right[2].reshape(-1),
            RB,
            groups * RB,
        )
        left_dense = densify(left[0], left[1], left[2], RB, RB)
        totals = totals + jnp.dot(left_dense, right_dense, preferred_element_type=jnp.float32)
    shift_amount = row_place - groups * col_place
    valid = (shift_amount >= 0) & (shift_amount < groups)
    start = jnp.clip(shift_amount, 0, groups - 1) * RB * width
    window = lax.dynamic_slice_in_dim(totals, start, RB * width, 1)
    term = jnp.where(valid, jnp.trace(window), jnp.zeros((), jnp.float32))
    overall = lax.psum(term, ("row", "col"))
    trace_value = overall / math.sqrt(row_count * RB * width)
    return (totals.astype(jnp.bfloat16), trace_value)


def solution(mesh):
    return jax.shard_map(
        body,
        mesh=mesh,
        in_specs=(
            P("row", "col", None, None, None, None),
            P("row", "col", None, None),
            P("row", "col", None, None),
            P("row", "col", None),
        ),
        out_specs=(P("row", "col"), P()),
        check_vma=False,
    )
```

profile of v0, /device:TPU:1, one launch (start us, length us, event | category | flops | bytes accessed | tf_op | source)
XLA Modules:
  0.0 380.4 jit_solution(16158533486816690697)
XLA Ops:
  32.8 4.6 %collective-permute-start.13 = (s32[2,8]{1,0:T(2,128)S(1)}, s32[2,8]{1,0:T(2,128)S(1)}, u32[]{:S(2)}, u32[]{:S(2)}) collective-permute-start(s32[2,8]{1,0:T(2,128)S(1)} %broadcast_select_fusion.10), channel_id=1, source_target_pairs={{480,0},{496,16},{0,32},{16,48},{32,64},{48,80},{64,96},{80,112},{... | collective-permute-start | bytes 200 | tf_op jit(solution)/shard_map/ppermute | solution.py:19
  41.4 6.2 %collective-permute-start.2 = (s32[8]{0:T(128)S(1)}, s32[8]{0:T(128)S(1)}, u32[]{:S(2)}, u32[]{:S(2)}) collective-permute-start(s32[8]{0:T(128)S(1)} %broadcast_select_fusion.22), channel_id=1, source_target_pairs={{12,0},{13,1},{14,2},{15,3},{0,4},{1,5},{2,6},{3,7},{4,8},{5,9},{6... | collective-permute-start | bytes 104 | tf_op jit(solution)/shard_map/ppermute | solution.py:19
  48.3 4.5 %collective-permute-start.6 = (s32[8]{0:T(128)S(1)}, s32[8]{0:T(128)S(1)}, u32[]{:S(2)}, u32[]{:S(2)}) collective-permute-start(s32[8]{0:T(128)S(1)} %broadcast_select_fusion.21), channel_id=1, source_target_pairs={{12,0},{13,1},{14,2},{15,3},{0,4},{1,5},{2,6},{3,7},{4,8},{5,9},{6... | collective-permute-start | bytes 104 | tf_op jit(solution)/shard_map/ppermute | solution.py:19
  54.7 7.5 %collective-permute-start.3 = (s32[8]{0:T(128)S(1)}, s32[8]{0:T(128)S(1)}, u32[]{:S(2)}, u32[]{:S(2)}) collective-permute-start(s32[8]{0:T(128)S(1)} %broadcast_select_fusion.24), channel_id=1, source_target_pairs={{8,0},{9,1},{10,2},{11,3},{12,4},{13,5},{14,6},{15,7},{0,8},{1,9},... | collective-permute-start | bytes 104 | tf_op jit(solution)/shard_map/ppermute | solution.py:19
  70.6 7.6 %collective-permute-start.28 = (s32[8]{0:T(128)S(1)}, s32[8]{0:T(128)S(1)}, u32[]{:S(2)}, u32[]{:S(2)}) collective-permute-start(s32[8]{0:T(128)S(1)} %get-tuple-element.4), channel_id=1, source_target_pairs={{1,0},{2,1},{3,2},{4,3},{5,4},{6,5},{7,6},{8,7},{9,8},{10,9},{11,1... | collective-permute-start | bytes 104 | tf_op jit(solution)/shard_map/ppermute | solution.py:19
  86.6 4.5 %collective-permute-start.15 = (s32[2,8]{1,0:T(2,128)S(1)}, s32[2,8]{1,0:T(2,128)S(1)}, u32[]{:S(2)}, u32[]{:S(2)}) collective-permute-start(s32[2,8]{1,0:T(2,128)S(1)} %broadcast_select_fusion.14), channel_id=1, source_target_pairs={{384,0},{400,16},{416,32},{432,48},{448,64},{464,80},{480,96},{496... | collective-permute-start | bytes 200 | tf_op jit(solution)/shard_map/ppermute | solution.py:19
  99.5 4.4 %collective-permute-start.16 = (s32[2,8]{1,0:T(2,128)S(1)}, s32[2,8]{1,0:T(2,128)S(1)}, u32[]{:S(2)}, u32[]{:S(2)}) collective-permute-start(s32[2,8]{1,0:T(2,128)S(1)} %broadcast_select_fusion.16), channel_id=1, source_target_pairs={{256,0},{272,16},{288,32},{304,48},{320,64},{336,80},{352,96},{368... | collective-permute-start | bytes 200 | tf_op jit(solution)/shard_map/ppermute | solution.py:19
  104.0 4.8 %collective-permute-start.21 = (s32[2,8]{1,0:T(2,128)S(1)}, s32[2,8]{1,0:T(2,128)S(1)}, u32[]{:S(2)}, u32[]{:S(2)}) collective-permute-start(s32[2,8]{1,0:T(2,128)S(1)} %broadcast_select_fusion.15), channel_id=1, source_target_pairs={{256,0},{272,16},{288,32},{304,48},{320,64},{336,80},{352,96},{368... | collective-permute-start | bytes 200 | tf_op jit(solution)/shard_map/ppermute | solution.py:19
  114.6 5.4 %collective-permute-done.9 = bf16[8,128,128]{2,1,0:T(8,128)(2,1)S(1)} collective-permute-done((bf16[8,128,128]{2,1,0:T(8,128)(2,1)S(1)}, bf16[8,128,128]{2,1,0:T(8,128)(2,1)S(1)}, u32[]{:S(2)}, u32[]{:S(2)}) %collective-permute-start.9) | collective-permute-done | bytes 262176 | tf_op jit(solution)/shard_map/ppermute | solution.py:19
  122.1 5.7 %collective-permute-start.31 = (s32[2,8]{1,0:T(2,128)S(1)}, s32[2,8]{1,0:T(2,128)S(1)}, u32[]{:S(2)}, u32[]{:S(2)}) collective-permute-start(s32[2,8]{1,0:T(2,128)S(1)} %get-tuple-element.7), channel_id=1, source_target_pairs={{32,0},{48,16},{64,32},{80,48},{96,64},{112,80},{128,96},{144,112}... | collective-permute-start | bytes 200 | tf_op jit(solution)/shard_map/ppermute | solution.py:19
  134.1 4.8 %collective-permute-start.37 = (s32[2,8]{1,0:T(2,128)S(1)}, s32[2,8]{1,0:T(2,128)S(1)}, u32[]{:S(2)}, u32[]{:S(2)}) collective-permute-start(s32[2,8]{1,0:T(2,128)S(1)} %collective-permute-done.31), channel_id=1, source_target_pairs={{32,0},{48,16},{64,32},{80,48},{96,64},{112,80},{128,96},{144,112}... | collective-permute-start | bytes 200 | tf_op jit(solution)/shard_map/ppermute | solution.py:19
  141.7 5.4 %collective-permute-start.11 = (bf16[8,128,128]{2,1,0:T(8,128)(2,1)S(1)}, bf16[8,128,128]{2,1,0:T(8,128)(2,1)S(1)}, u32[]{:S(2)}, u32[]{:S(2)}) collective-permute-start(bf16[8,128,128]{2,1,0:T(8,128)(2,1)S(1)} %broadcast_select_fusion.7), channel_id=1, source_target_pairs={{8,0},{9,1},{10,2},{11,3},{12,4},{13,5},{14,6},{15,7},{0,8},{1,9},... | collective-permute-start | bytes 786440 | tf_op jit(solution)/shard_map/ppermute | solution.py:19
  149.6 6.0 %collective-permute-start.43 = (s32[2,8]{1,0:T(2,128)S(1)}, s32[2,8]{1,0:T(2,128)S(1)}, u32[]{:S(2)}, u32[]{:S(2)}) collective-permute-start(s32[2,8]{1,0:T(2,128)S(1)} %collective-permute-done.37), channel_id=1, source_target_pairs={{32,0},{48,16},{64,32},{80,48},{96,64},{112,80},{128,96},{144,112}... | collective-permute-start | bytes 200 | tf_op jit(solution)/shard_map/ppermute | solution.py:19
  161.6 5.6 %collective-permute-start.29 = (bf16[8,128,128]{2,1,0:T(8,128)(2,1)S(1)}, bf16[8,128,128]{2,1,0:T(8,128)(2,1)S(1)}, u32[]{:S(2)}, u32[]{:S(2)}) collective-permute-start(bf16[8,128,128]{2,1,0:T(8,128)(2,1)S(1)} %broadcast_select_fusion.8), channel_id=1, source_target_pairs={{1,0},{2,1},{3,2},{4,3},{5,4},{6,5},{7,6},{8,7},{9,8},{10,9},{11,1... | collective-permute-start | bytes 786440 | tf_op jit(solution)/shard_map/ppermute | solution.py:19
  171.7 4.9 %collective-permute-done.35 = bf16[8,128,128]{2,1,0:T(8,128)(2,1)S(1)} collective-permute-done((bf16[8,128,128]{2,1,0:T(8,128)(2,1)S(1)}, bf16[8,128,128]{2,1,0:T(8,128)(2,1)S(1)}, u32[]{:S(2)}, u32[]{:S(2)}) %collective-permute-start.35) | collective-permute-done | bytes 262176 | tf_op jit(solution)/shard_map/ppermute | solution.py:19
  178.2 15.1 %collective-permute-done.25 = bf16[2,8,128,128]{3,2,1,0:T(8,128)(2,1)S(1)} collective-permute-done((bf16[2,8,128,128]{3,2,1,0:T(8,128)(2,1)S(1)}, bf16[2,8,128,128]{3,2,1,0:T(8,128)(2,1)S(1)}, u32[]{:S(2)}, u32[]{:S(2)}) %collective-permute-start.25) | collective-permute-done | bytes 524320 | tf_op jit(solution)/shard_map/ppermute | solution.py:19
  193.4 4.2 %collective-permute-start.26 = (bf16[2,8,128,128]{3,2,1,0:T(8,128)(2,1)S(1)}, bf16[2,8,128,128]{3,2,1,0:T(8,128)(2,1)S(1)}, u32[]{:S(2)}, u32[]{:S(2)}) collective-permute-start(bf16[2,8,128,128]{3,2,1,0:T(8,128)(2,1)S(1)} %broadcast_select_fusion.3), channel_id=1, source_target_pairs={{256,0},{272,16},{288,32},{304,48},{320,64},{336,80},{352,96},{368... | collective-permute-start | bytes 1572872 | tf_op jit(solution)/shard_map/ppermute | solution.py:19
  198.6 25.7 %collective-permute-done.26 = bf16[2,8,128,128]{3,2,1,0:T(8,128)(2,1)S(1)} collective-permute-done((bf16[2,8,128,128]{3,2,1,0:T(8,128)(2,1)S(1)}, bf16[2,8,128,128]{3,2,1,0:T(8,128)(2,1)S(1)}, u32[]{:S(2)}, u32[]{:S(2)}) %collective-permute-start.26) | collective-permute-done | bytes 524320 | tf_op jit(solution)/shard_map/ppermute | solution.py:19
  228.7 12.0 %collective-permute-done.32 = bf16[2,8,128,128]{3,2,1,0:T(8,128)(2,1)S(1)} collective-permute-done((bf16[2,8,128,128]{3,2,1,0:T(8,128)(2,1)S(1)}, bf16[2,8,128,128]{3,2,1,0:T(8,128)(2,1)S(1)}, u32[]{:S(2)}, u32[]{:S(2)}) %collective-permute-start.32) | collective-permute-done | bytes 524320 | tf_op jit(solution)/shard_map/ppermute | solution.py:19
  240.7 4.3 %collective-permute-start.38 = (bf16[2,8,128,128]{3,2,1,0:T(8,128)(2,1)S(1)}, bf16[2,8,128,128]{3,2,1,0:T(8,128)(2,1)S(1)}, u32[]{:S(2)}, u32[]{:S(2)}) collective-permute-start(bf16[2,8,128,128]{3,2,1,0:T(8,128)(2,1)S(1)} %collective-permute-done.32), channel_id=1, source_target_pairs={{32,0},{48,16},{64,32},{80,48},{96,64},{112,80},{128,96},{144,112}... | collective-permute-start | bytes 1572872 | tf_op jit(solution)/shard_map/ppermute | solution.py:19
  247.4 8.7 %collective-permute-done.38 = bf16[2,8,128,128]{3,2,1,0:T(8,128)(2,1)S(1)} collective-permute-done((bf16[2,8,128,128]{3,2,1,0:T(8,128)(2,1)S(1)}, bf16[2,8,128,128]{3,2,1,0:T(8,128)(2,1)S(1)}, u32[]{:S(2)}, u32[]{:S(2)}) %collective-permute-start.38) | collective-permute-done | bytes 524320 | tf_op jit(solution)/shard_map/ppermute | solution.py:19
  256.1 6.9 %collective-permute-start.44 = (bf16[2,8,128,128]{3,2,1,0:T(8,128)(2,1)S(1)}, bf16[2,8,128,128]{3,2,1,0:T(8,128)(2,1)S(1)}, u32[]{:S(2)}, u32[]{:S(2)}) collective-permute-start(bf16[2,8,128,128]{3,2,1,0:T(8,128)(2,1)S(1)} %collective-permute-done.38), channel_id=1, source_target_pairs={{32,0},{48,16},{64,32},{80,48},{96,64},{112,80},{128,96},{144,112}... | collective-permute-start | bytes 1572872 | tf_op jit(solution)/shard_map/ppermute | solution.py:19
  265.4 6.6 %collective-permute-done.44 = bf16[2,8,128,128]{3,2,1,0:T(8,128)(2,1)S(1)} collective-permute-done((bf16[2,8,128,128]{3,2,1,0:T(8,128)(2,1)S(1)}, bf16[2,8,128,128]{3,2,1,0:T(8,128)(2,1)S(1)}, u32[]{:S(2)}, u32[]{:S(2)}) %collective-permute-start.44) | collective-permute-done | bytes 524320 | tf_op jit(solution)/shard_map/ppermute | solution.py:19
  277.0 101.6 %psum.7 = f32[]{:T(128)} all-reduce(f32[]{:T(128)S(6)} %select_n.252), channel_id=1, replica_groups=mesh['row'=32,'col'=16] {'row','col'}, use_global_device_ids=true, to_apply=%region_1.2 | all-reduce | flops 1 | bytes 8 | tf_op jit(solution)/shard_map/psum | solution.py:104
  (126 shorter events, 109.3 us)
Async XLA Ops:
  0.6 29.2 %collective-permute-start.12 = (s32[2,8]{1,0:T(2,128)}, s32[2,8]{1,0:T(2,128)S(1)}, u32[]{:S(2)}, u32[]{:S(2)}) collective-permute-start(s32[2,8]{1,0:T(2,128)} %bitcast.239), channel_id=1, source_target_pairs={{496,0},{0,16},{16,32},{32,48},{48,64},{64,80},{80,96},{96,112},{1... | collective-permute-start | bytes 200 | tf_op jit(solution)/shard_map/ppermute | solution.py:19
  5.5 27.3 %collective-permute-start.17 = (s32[2,8]{1,0:T(2,128)S(1)}, s32[2,8]{1,0:T(2,128)S(1)}, u32[]{:S(2)}, u32[]{:S(2)}) collective-permute-start(s32[2,8]{1,0:T(2,128)S(1)} %bitcast_add_fusion), channel_id=1, source_target_pairs={{496,0},{0,16},{16,32},{32,48},{48,64},{64,80},{80,96},{96,112},{1... | collective-permute-start | bytes 200 | tf_op jit(solution)/shard_map/ppermute | solution.py:19
  10.5 100.3 %collective-permute-start.22 = (bf16[2,8,128,128]{3,2,1,0:T(8,128)(2,1)S(1)}, bf16[2,8,128,128]{3,2,1,0:T(8,128)(2,1)S(1)}, u32[]{:S(2)}, u32[]{:S(2)}) collective-permute-start(bf16[2,8,128,128]{3,2,1,0:T(8,128)(2,1)S(1)} %bitcast_multiply_fusion), channel_id=1, source_target_pairs={{496,0},{0,16},{16,32},{32,48},{48,64},{64,80},{80,96},{96,112},{1... | collective-permute-start | bytes 1572872 | tf_op jit(solution)/shard_map/ppermute | solution.py:19
  13.4 95.4 %collective-permute-start.8 = (bf16[8,128,128]{2,1,0:T(8,128)(2,1)S(1)}, bf16[8,128,128]{2,1,0:T(8,128)(2,1)S(1)}, u32[]{:S(2)}, u32[]{:S(2)}) collective-permute-start(bf16[8,128,128]{2,1,0:T(8,128)(2,1)S(1)} %dynamic-slice_bitcast_fusion), channel_id=1, source_target_pairs={{15,0},{0,1},{1,2},{2,3},{3,4},{4,5},{5,6},{6,7},{7,8},{8,9},{9,10... | collective-permute-start | bytes 786440 | tf_op jit(solution)/shard_map/ppermute | solution.py:19
  32.8 29.3 %collective-permute-start.13 = (s32[2,8]{1,0:T(2,128)S(1)}, s32[2,8]{1,0:T(2,128)S(1)}, u32[]{:S(2)}, u32[]{:S(2)}) collective-permute-start(s32[2,8]{1,0:T(2,128)S(1)} %broadcast_select_fusion.10), channel_id=1, source_target_pairs={{480,0},{496,16},{0,32},{16,48},{32,64},{48,80},{64,96},{80,112},{... | collective-permute-start | bytes 200 | tf_op jit(solution)/shard_map/ppermute | solution.py:19
  38.2 25.8 %collective-permute-start.18 = (s32[2,8]{1,0:T(2,128)S(1)}, s32[2,8]{1,0:T(2,128)S(1)}, u32[]{:S(2)}, u32[]{:S(2)}) collective-permute-start(s32[2,8]{1,0:T(2,128)S(1)} %broadcast_select_fusion.9), channel_id=1, source_target_pairs={{480,0},{496,16},{0,32},{16,48},{32,64},{48,80},{64,96},{80,112},{... | collective-permute-start | bytes 200 | tf_op jit(solution)/shard_map/ppermute | solution.py:19
  54.7 12.7 %collective-permute-start.3 = (s32[8]{0:T(128)S(1)}, s32[8]{0:T(128)S(1)}, u32[]{:S(2)}, u32[]{:S(2)}) collective-permute-start(s32[8]{0:T(128)S(1)} %broadcast_select_fusion.24), channel_id=1, source_target_pairs={{8,0},{9,1},{10,2},{11,3},{12,4},{13,5},{14,6},{15,7},{0,8},{1,9},... | collective-permute-start | bytes 104 | tf_op jit(solution)/shard_map/ppermute | solution.py:19
  64.1 19.6 %collective-permute-start.14 = (s32[2,8]{1,0:T(2,128)S(1)}, s32[2,8]{1,0:T(2,128)S(1)}, u32[]{:S(2)}, u32[]{:S(2)}) collective-permute-start(s32[2,8]{1,0:T(2,128)S(1)} %broadcast_select_fusion.12), channel_id=1, source_target_pairs={{448,0},{464,16},{480,32},{496,48},{0,64},{16,80},{32,96},{48,112}... | collective-permute-start | bytes 200 | tf_op jit(solution)/shard_map/ppermute | solution.py:19
  67.3 19.2 %collective-permute-start.19 = (s32[2,8]{1,0:T(2,128)S(1)}, s32[2,8]{1,0:T(2,128)S(1)}, u32[]{:S(2)}, u32[]{:S(2)}) collective-permute-start(s32[2,8]{1,0:T(2,128)S(1)} %broadcast_select_fusion.11), channel_id=1, source_target_pairs={{448,0},{464,16},{480,32},{496,48},{0,64},{16,80},{32,96},{48,112}... | collective-permute-start | bytes 200 | tf_op jit(solution)/shard_map/ppermute | solution.py:19
  86.6 13.0 %collective-permute-start.15 = (s32[2,8]{1,0:T(2,128)S(1)}, s32[2,8]{1,0:T(2,128)S(1)}, u32[]{:S(2)}, u32[]{:S(2)}) collective-permute-start(s32[2,8]{1,0:T(2,128)S(1)} %broadcast_select_fusion.14), channel_id=1, source_target_pairs={{384,0},{400,16},{416,32},{432,48},{448,64},{464,80},{480,96},{496... | collective-permute-start | bytes 200 | tf_op jit(solution)/shard_map/ppermute | solution.py:19
  91.1 12.8 %collective-permute-start.20 = (s32[2,8]{1,0:T(2,128)S(1)}, s32[2,8]{1,0:T(2,128)S(1)}, u32[]{:S(2)}, u32[]{:S(2)}) collective-permute-start(s32[2,8]{1,0:T(2,128)S(1)} %broadcast_select_fusion.13), channel_id=1, source_target_pairs={{384,0},{400,16},{416,32},{432,48},{448,64},{464,80},{480,96},{496... | collective-permute-start | bytes 200 | tf_op jit(solution)/shard_map/ppermute | solution.py:19
  99.5 22.5 %collective-permute-start.16 = (s32[2,8]{1,0:T(2,128)S(1)}, s32[2,8]{1,0:T(2,128)S(1)}, u32[]{:S(2)}, u32[]{:S(2)}) collective-permute-start(s32[2,8]{1,0:T(2,128)S(1)} %broadcast_select_fusion.16), channel_id=1, source_target_pairs={{256,0},{272,16},{288,32},{304,48},{320,64},{336,80},{352,96},{368... | collective-permute-start | bytes 200 | tf_op jit(solution)/shard_map/ppermute | solution.py:19
  104.0 18.1 %collective-permute-start.21 = (s32[2,8]{1,0:T(2,128)S(1)}, s32[2,8]{1,0:T(2,128)S(1)}, u32[]{:S(2)}, u32[]{:S(2)}) collective-permute-start(s32[2,8]{1,0:T(2,128)S(1)} %broadcast_select_fusion.15), channel_id=1, source_target_pairs={{256,0},{272,16},{288,32},{304,48},{320,64},{336,80},{352,96},{368... | collective-permute-start | bytes 200 | tf_op jit(solution)/shard_map/ppermute | solution.py:19
  110.9 36.3 %collective-permute-start.23 = (bf16[2,8,128,128]{3,2,1,0:T(8,128)(2,1)S(1)}, bf16[2,8,128,128]{3,2,1,0:T(8,128)(2,1)S(1)}, u32[]{:S(2)}, u32[]{:S(2)}) collective-permute-start(bf16[2,8,128,128]{3,2,1,0:T(8,128)(2,1)S(1)} %broadcast_select_fusion), channel_id=1, source_target_pairs={{480,0},{496,16},{0,32},{16,48},{32,64},{48,80},{64,96},{80,112},{... | collective-permute-start | bytes 1572872 | tf_op jit(solution)/shard_map/ppermute | solution.py:19
  120.1 21.6 %collective-permute-start.10 = (bf16[8,128,128]{2,1,0:T(8,128)(2,1)S(1)}, bf16[8,128,128]{2,1,0:T(8,128)(2,1)S(1)}, u32[]{:S(2)}, u32[]{:S(2)}) collective-permute-start(bf16[8,128,128]{2,1,0:T(8,128)(2,1)S(1)} %broadcast_select_fusion.6), channel_id=1, source_target_pairs={{12,0},{13,1},{14,2},{15,3},{0,4},{1,5},{2,6},{3,7},{4,8},{5,9},{6... | collective-permute-start | bytes 786440 | tf_op jit(solution)/shard_map/ppermute | solution.py:19
  134.1 15.5 %collective-permute-start.37 = (s32[2,8]{1,0:T(2,128)S(1)}, s32[2,8]{1,0:T(2,128)S(1)}, u32[]{:S(2)}, u32[]{:S(2)}) collective-permute-start(s32[2,8]{1,0:T(2,128)S(1)} %collective-permute-done.31), channel_id=1, source_target_pairs={{32,0},{48,16},{64,32},{80,48},{96,64},{112,80},{128,96},{144,112}... | collective-permute-start | bytes 200 | tf_op jit(solution)/shard_map/ppermute | solution.py:19
  141.7 19.9 %collective-permute-start.11 = (bf16[8,128,128]{2,1,0:T(8,128)(2,1)S(1)}, bf16[8,128,128]{2,1,0:T(8,128)(2,1)S(1)}, u32[]{:S(2)}, u32[]{:S(2)}) collective-permute-start(bf16[8,128,128]{2,1,0:T(8,128)(2,1)S(1)} %broadcast_select_fusion.7), channel_id=1, source_target_pairs={{8,0},{9,1},{10,2},{11,3},{12,4},{13,5},{14,6},{15,7},{0,8},{1,9},... | collective-permute-start | bytes 786440 | tf_op jit(solution)/shard_map/ppermute | solution.py:19
  147.2 20.0 %collective-permute-start.24 = (bf16[2,8,128,128]{3,2,1,0:T(8,128)(2,1)S(1)}, bf16[2,8,128,128]{3,2,1,0:T(8,128)(2,1)S(1)}, u32[]{:S(2)}, u32[]{:S(2)}) collective-permute-start(bf16[2,8,128,128]{3,2,1,0:T(8,128)(2,1)S(1)} %broadcast_select_fusion.1), channel_id=1, source_target_pairs={{448,0},{464,16},{480,32},{496,48},{0,64},{16,80},{32,96},{48,112}... | collective-permute-start | bytes 1572872 | tf_op jit(solution)/shard_map/ppermute | solution.py:19
  167.3 26.0 %collective-permute-start.25 = (bf16[2,8,128,128]{3,2,1,0:T(8,128)(2,1)S(1)}, bf16[2,8,128,128]{3,2,1,0:T(8,128)(2,1)S(1)}, u32[]{:S(2)}, u32[]{:S(2)}) collective-permute-start(bf16[2,8,128,128]{3,2,1,0:T(8,128)(2,1)S(1)} %broadcast_select_fusion.2), channel_id=1, source_target_pairs={{384,0},{400,16},{416,32},{432,48},{448,64},{464,80},{480,96},{496... | collective-permute-start | bytes 1572872 | tf_op jit(solution)/shard_map/ppermute | solution.py:19
  176.6 21.5 %collective-permute-start.41 = (bf16[8,128,128]{2,1,0:T(8,128)(2,1)S(1)}, bf16[8,128,128]{2,1,0:T(8,128)(2,1)S(1)}, u32[]{:S(2)}, u32[]{:S(2)}) collective-permute-start(bf16[8,128,128]{2,1,0:T(8,128)(2,1)S(1)} %collective-permute-done.35), channel_id=1, source_target_pairs={{1,0},{2,1},{3,2},{4,3},{5,4},{6,5},{7,6},{8,7},{9,8},{10,9},{11,1... | collective-permute-start | bytes 786440 | tf_op jit(solution)/shard_map/ppermute | solution.py:19
  193.4 30.9 %collective-permute-start.26 = (bf16[2,8,128,128]{3,2,1,0:T(8,128)(2,1)S(1)}, bf16[2,8,128,128]{3,2,1,0:T(8,128)(2,1)S(1)}, u32[]{:S(2)}, u32[]{:S(2)}) collective-permute-start(bf16[2,8,128,128]{3,2,1,0:T(8,128)(2,1)S(1)} %broadcast_select_fusion.3), channel_id=1, source_target_pairs={{256,0},{272,16},{288,32},{304,48},{320,64},{336,80},{352,96},{368... | collective-permute-start | bytes 1572872 | tf_op jit(solution)/shard_map/ppermute | solution.py:19
  224.3 16.3 %collective-permute-start.32 = (bf16[2,8,128,128]{3,2,1,0:T(8,128)(2,1)S(1)}, bf16[2,8,128,128]{3,2,1,0:T(8,128)(2,1)S(1)}, u32[]{:S(2)}, u32[]{:S(2)}) collective-permute-start(bf16[2,8,128,128]{3,2,1,0:T(8,128)(2,1)S(1)} %broadcast_select_fusion.4), channel_id=1, source_target_pairs={{32,0},{48,16},{64,32},{80,48},{96,64},{112,80},{128,96},{144,112}... | collective-permute-start | bytes 1572872 | tf_op jit(solution)/shard_map/ppermute | solution.py:19
  240.7 15.4 %collective-permute-start.38 = (bf16[2,8,128,128]{3,2,1,0:T(8,128)(2,1)S(1)}, bf16[2,8,128,128]{3,2,1,0:T(8,128)(2,1)S(1)}, u32[]{:S(2)}, u32[]{:S(2)}) collective-permute-start(bf16[2,8,128,128]{3,2,1,0:T(8,128)(2,1)S(1)} %collective-permute-done.32), channel_id=1, source_target_pairs={{32,0},{48,16},{64,32},{80,48},{96,64},{112,80},{128,96},{144,112}... | collective-permute-start | bytes 1572872 | tf_op jit(solution)/shard_map/ppermute | solution.py:19
  256.1 16.0 %collective-permute-start.44 = (bf16[2,8,128,128]{3,2,1,0:T(8,128)(2,1)S(1)}, bf16[2,8,128,128]{3,2,1,0:T(8,128)(2,1)S(1)}, u32[]{:S(2)}, u32[]{:S(2)}) collective-permute-start(bf16[2,8,128,128]{3,2,1,0:T(8,128)(2,1)S(1)} %collective-permute-done.38), channel_id=1, source_target_pairs={{32,0},{48,16},{64,32},{80,48},{96,64},{112,80},{128,96},{144,112}... | collective-permute-start | bytes 1572872 | tf_op jit(solution)/shard_map/ppermute | solution.py:19
  (22 other events, 266.6 us)
where the time goes:
time: 382 us; the launch traced here: 380 us
  starting transfers between devices  151 us (40%)
  waiting for transfers between devices  102 us (27%)
  blocking collectives  102 us (27%)
  matrix products  12.7 us (3%)
  other arithmetic  6.7 us (2%)
  between operations  3.84 us (1%)
    ppermute x45, starting transfers between devices, passed_along(): return lax.ppermute(block, axis, route)  151 us
    ppermute x45, waiting for transfers between devices, passed_along(): return lax.ppermute(block, axis, route)  102 us
    psum x1, blocking collectives, body(): overall = lax.psum(term, ('row', 'col'))  102 us
  transfers between devices with their start and end apart: 45, of which 18 were waited for; matrix products, arithmetic and copies ran while one was open for 4% of the time, Pallas kernels for 0%

commit v1 on v0

v1 whole, which is shorter than its diff:
```python
import math

import jax
import jax.numpy as jnp
from jax import lax
from jax.sharding import PartitionSpec as P

RB = 5
STEPS = 4


def densify(pieces, places, nrows, ncols):
    width = pieces.shape[-1]
    count = pieces.shape[0]
    onehot = (places[None, :] == jnp.arange(nrows * ncols, dtype=jnp.int32)[:, None]).astype(
        pieces.dtype
    )
    dense = jnp.dot(
        onehot, pieces.reshape(count, width * width), preferred_element_type=jnp.float32
    )
    dense = dense.reshape(nrows, ncols, width, width).transpose(0, 2, 1, 3)
    return dense.reshape(nrows * width, ncols * width).astype(pieces.dtype)


def fetch(value, source_of, row_count, col_count):
    pairs = []
    for r in range(row_count):
        for c in range(col_count):
            sr, sc = source_of(r, c)
            pairs.append((sr * col_count + sc, r * col_count + c))
    return lax.ppermute(value, ("row", "col"), pairs)


def body(blocks, block_rows, block_cols, counts):
    groups = blocks.shape[2]
    slot_count = blocks.shape[3]
    width = blocks.shape[4]
    row_count = lax.axis_size("row")
    col_count = lax.axis_size("col")
    row_place = lax.axis_index("row")
    col_place = lax.axis_index("col")
    lower = row_place % groups
    filled = counts[0, 0]
    live = jnp.arange(slot_count, dtype=jnp.int32)[None, :] < filled[:, None]
    left_places_all = jnp.where(live, block_rows[0, 0] * RB + block_cols[0, 0], -1)
    offsets = (jnp.arange(groups, dtype=jnp.int32) * RB)[:, None]
    right_places = jnp.where(
        live, block_rows[0, 0] * (groups * RB) + block_cols[0, 0] + offsets, -1
    ).reshape(-1)
    left_pieces = lax.dynamic_index_in_dim(blocks[0, 0], lower, 0, keepdims=False)
    left_places = lax.dynamic_index_in_dim(left_places_all, lower, 0, keepdims=False)
    right_pieces = blocks[0, 0].reshape(groups * slot_count, width, width)
    totals = jnp.zeros((RB * width, groups * RB * width), jnp.float32)
    for step in range(STEPS):
        def left_source(r, c, step=step):
            return r, (c + r // groups + step) % col_count

        def right_source(r, c, step=step):
            return (r + groups * c + groups * step) % row_count, c

        lp = fetch(left_pieces, left_source, row_count, col_count)
        lq = fetch(left_places, left_source, row_count, col_count)
        rp = fetch(right_pieces, right_source, row_count, col_count)
        rq = fetch(right_places, right_source, row_count, col_count)
        right_dense = densify(rp, rq, RB, groups * RB)
        left_dense = densify(lp, lq, RB, RB)
        totals = totals + jnp.dot(left_dense, right_dense, preferred_element_type=jnp.float32)
    shift_amount = row_place - groups * col_place
    valid = (shift_amount >= 0) & (shift_amount < groups)
    start = jnp.clip(shift_amount, 0, groups - 1) * RB * width
    window = lax.dynamic_slice_in_dim(totals, start, RB * width, 1)
    term = jnp.where(valid, jnp.trace(window), jnp.zeros((), jnp.float32))
    overall = lax.psum(lax.psum(term, "col"), "row")
    trace_value = overall / math.sqrt(row_count * RB * width)
    return (totals.astype(jnp.bfloat16), trace_value)


def solution(mesh):
    return jax.shard_map(
        body,
        mesh=mesh,
        in_specs=(
            P("row", "col", None, None, None, None),
            P("row", "col", None, None),
            P("row", "col", None, None),
            P("row", "col", None),
        ),
        out_specs=(P("row", "col"), P()),
        check_vma=False,
    )
```

time: 382 us -> 289 us (0.76)
  the two profiles are of different devices: /device:TPU:1 before, /device:TPU:256 now
where the time goes in v1:
time: 289 us
  blocking collectives  100 us (35%)
  starting transfers between devices  91.4 us (32%)
  waiting for transfers between devices  76.4 us (26%)
  matrix products  12.7 us (4%)
  between operations  3.43 us (1%)
  other arithmetic  2.92 us (1%)
    psum x2, blocking collectives, body(): overall = lax.psum(lax.psum(term, 'col'), 'row')  100 us
    ppermute x16, starting transfers between devices, fetch(): return lax.ppermute(value, ('row', 'col'), pairs)  91.4 us
    ppermute x16, waiting for transfers between devices, fetch(): return lax.ppermute(value, ('row', 'col'), pairs)  76.4 us
    dot_general x4, matrix products, body(): jnp.dot(left_dense, right_dense, preferred_element_type=jnp.float32)  7.14 us
  transfers between devices with their start and end apart: 16, of which 5 were waited for; matrix products, arithmetic and copies ran while one was open for 4% of the time, Pallas kernels for 0%

profile of v1, /device:TPU:256, one launch (start us, length us, event | category | flops | bytes accessed | tf_op | source)
XLA Modules:
  0.0 288.7 jit_solution(16906311360944016867)
XLA Ops:
  2.4 1.9 collective-permute-start.5
  5.7 1.9 collective-permute-start.4
  9.4 19.1 %collective-permute-start.2 = (s32[16]{0:T(128)S(1)}, s32[16]{0:T(128)S(1)}, u32[]{:S(2)}, u32[]{:S(2)}) collective-permute-start(s32[16]{0:T(128)S(1)} %add_select_fusion), channel_id=1, source_target_pairs={{0,0},{33,1},{66,2},{99,3},{132,4},{165,5},{198,6},{231,7},{264,8}... | collective-permute-start | bytes 200 | tf_op jit(solution)/shard_map/ppermute | solution.py:31
  28.6 5.0 %collective-permute-start.6 = (s32[16]{0:T(128)S(1)}, s32[16]{0:T(128)S(1)}, u32[]{:S(2)}, u32[]{:S(2)}) collective-permute-start(s32[16]{0:T(128)S(1)} %add_select_fusion), channel_id=1, source_target_pairs={{32,0},{65,1},{98,2},{131,3},{164,4},{197,5},{230,6},{263,7},{296,... | collective-permute-start | bytes 200 | tf_op jit(solution)/shard_map/ppermute | solution.py:31
  33.7 18.6 %collective-permute-start.9 = (bf16[8,128,128]{2,1,0:T(8,128)(2,1)S(1)}, bf16[8,128,128]{2,1,0:T(8,128)(2,1)S(1)}, u32[]{:S(2)}, u32[]{:S(2)}) collective-permute-start(bf16[8,128,128]{2,1,0:T(8,128)(2,1)S(1)} %dynamic-slice_bitcast_fusion), channel_id=1, source_target_pairs={{2,0},{3,1},{4,2},{5,3},{6,4},{7,5},{8,6},{9,7},{10,8},{11,9},{12,... | collective-permute-start | bytes 786440 | tf_op jit(solution)/shard_map/ppermute | solution.py:31
  52.8 1.9 collective-permute-start.8
  54.7 1.9 collective-permute-start.13
  58.2 1.9 collective-permute-start.12
  60.2 15.4 %collective-permute-start.3 = (bf16[16,128,128]{2,1,0:T(8,128)(2,1)S(1)}, bf16[16,128,128]{2,1,0:T(8,128)(2,1)S(1)}, u32[]{:S(2)}, u32[]{:S(2)}) collective-permute-start(bf16[16,128,128]{2,1,0:T(8,128)(2,1)S(1)} %bitcast.224), channel_id=1, source_target_pairs={{0,0},{33,1},{66,2},{99,3},{132,4},{165,5},{198,6},{231,7},{264,8}... | collective-permute-start | bytes 1572872 | tf_op jit(solution)/shard_map/ppermute | solution.py:31
  76.1 14.6 %collective-permute-start.7 = (bf16[16,128,128]{2,1,0:T(8,128)(2,1)S(1)}, bf16[16,128,128]{2,1,0:T(8,128)(2,1)S(1)}, u32[]{:S(2)}, u32[]{:S(2)}) collective-permute-start(bf16[16,128,128]{2,1,0:T(8,128)(2,1)S(1)} %bitcast.225), channel_id=1, source_target_pairs={{32,0},{65,1},{98,2},{131,3},{164,4},{197,5},{230,6},{263,7},{296,... | collective-permute-start | bytes 1572872 | tf_op jit(solution)/shard_map/ppermute | solution.py:31
  90.8 1.9 collective-permute-start.10
  93.2 1.9 collective-permute-start.11
  95.1 8.9 %collective-permute-done.3 = bf16[16,128,128]{2,1,0:T(8,128)(2,1)S(1)} collective-permute-done((bf16[16,128,128]{2,1,0:T(8,128)(2,1)S(1)}, bf16[16,128,128]{2,1,0:T(8,128)(2,1)S(1)}, u32[]{:S(2)}, u32[]{:S(2)}) %collective-permute-start.3) | collective-permute-done | bytes 524320 | tf_op jit(solution)/shard_map/ppermute | solution.py:31
  104.1 1.9 collective-permute-start.14
  106.9 1.5 fusion.6
  108.4 1.9 collective-permute-start.15
  110.3 25.2 %collective-permute-done.7 = bf16[16,128,128]{2,1,0:T(8,128)(2,1)S(1)} collective-permute-done((bf16[16,128,128]{2,1,0:T(8,128)(2,1)S(1)}, bf16[16,128,128]{2,1,0:T(8,128)(2,1)S(1)}, u32[]{:S(2)}, u32[]{:S(2)}) %collective-permute-start.7) | collective-permute-done | bytes 524320 | tf_op jit(solution)/shard_map/ppermute | solution.py:31
  136.4 1.5 convolution_add_fusion.2
  137.9 33.2 %collective-permute-done.11 = bf16[16,128,128]{2,1,0:T(8,128)(2,1)S(1)} collective-permute-done((bf16[16,128,128]{2,1,0:T(8,128)(2,1)S(1)}, bf16[16,128,128]{2,1,0:T(8,128)(2,1)S(1)}, u32[]{:S(2)}, u32[]{:S(2)}) %collective-permute-start.11) | collective-permute-done | bytes 524320 | tf_op jit(solution)/shard_map/ppermute | solution.py:31
  172.0 1.5 convolution_add_fusion.1
  173.5 8.1 %collective-permute-done.15 = bf16[16,128,128]{2,1,0:T(8,128)(2,1)S(1)} collective-permute-done((bf16[16,128,128]{2,1,0:T(8,128)(2,1)S(1)}, bf16[16,128,128]{2,1,0:T(8,128)(2,1)S(1)}, u32[]{:S(2)}, u32[]{:S(2)}) %collective-permute-start.15) | collective-permute-done | bytes 524320 | tf_op jit(solution)/shard_map/ppermute | solution.py:31
  182.4 2.7 fusion.58
  186.4 25.1 %psum.14 = f32[]{:T(128)} all-reduce(f32[]{:T(128)S(6)} %select_n.39), channel_id=1, replica_groups=mesh['row'=32,'col'=16] {'col'}, use_global_device_ids=true, to_apply=%region_1.2 | all-reduce | flops 1 | bytes 8 | tf_op jit(solution)/shard_map/psum | solution.py:73
  211.5 75.4 %psum.15 = f32[]{:T(128)} all-reduce(f32[]{:T(128)} %psum.14), channel_id=1, replica_groups=mesh['row'=32,'col'=16] {'row'}, use_global_device_ids=true, to_apply=%region_2.3 | all-reduce | flops 1 | bytes 8 | tf_op jit(solution)/shard_map/psum | solution.py:73
  (38 shorter events, 12.2 us)
Async XLA Ops:
  0.6 59.5 %copy-start = (bf16[1,1,2,8,128,128]{5,4,3,2,1,0:T(8,128)(2,1)S(1)}, bf16[1,1,2,8,128,128]{5,4,3,2,1,0:T(8,128)(2,1)}, u32[]{:S(2)}) copy-start(bf16[1,1,2,8,128,128]{5,4,3,2,1,0:T(8,128)(2,1)} %param.4) | copy-start | bytes 1572868
  1.7 32.0 %collective-permute-start.1 = (bf16[8,128,128]{2,1,0:T(8,128)(2,1)S(1)}, bf16[8,128,128]{2,1,0:T(8,128)(2,1)S(1)}, u32[]{:S(2)}, u32[]{:S(2)}) collective-permute-start(bf16[8,128,128]{2,1,0:T(8,128)(2,1)S(1)} %dynamic-slice_bitcast_fusion), channel_id=1, source_target_pairs={{0,0},{1,1},{2,2},{3,3},{4,4},{5,5},{6,6},{7,7},{8,8},{9,9},{10,10... | collective-permute-start | bytes 786440 | tf_op jit(solution)/shard_map/ppermute | solution.py:31
  2.4 52.3 %collective-permute-start.5 = (bf16[8,128,128]{2,1,0:T(8,128)(2,1)S(1)}, bf16[8,128,128]{2,1,0:T(8,128)(2,1)S(1)}, u32[]{:S(2)}, u32[]{:S(2)}) collective-permute-start(bf16[8,128,128]{2,1,0:T(8,128)(2,1)S(1)} %dynamic-slice_bitcast_fusion), channel_id=1, source_target_pairs={{1,0},{2,1},{3,2},{4,3},{5,4},{6,5},{7,6},{8,7},{9,8},{10,9},{11,1... | collective-permute-start | bytes 786440 | tf_op jit(solution)/shard_map/ppermute | solution.py:31
  5.1 23.5 %collective-permute-start = (s32[8]{0:T(128)S(1)}, s32[8]{0:T(128)S(1)}, u32[]{:S(2)}, u32[]{:S(2)}) collective-permute-start(s32[8]{0:T(128)S(1)} %fusion.57), channel_id=1, source_target_pairs={{0,0},{1,1},{2,2},{3,3},{4,4},{5,5},{6,6},{7,7},{8,8},{9,9},{10,10... | collective-permute-start | bytes 104 | tf_op jit(solution)/shard_map/ppermute | solution.py:31
  5.7 47.0 %collective-permute-start.4 = (s32[8]{0:T(128)S(1)}, s32[8]{0:T(128)S(1)}, u32[]{:S(2)}, u32[]{:S(2)}) collective-permute-start(s32[8]{0:T(128)S(1)} %fusion.57), channel_id=1, source_target_pairs={{1,0},{2,1},{3,2},{4,3},{5,4},{6,5},{7,6},{8,7},{9,8},{10,9},{11,1... | collective-permute-start | bytes 104 | tf_op jit(solution)/shard_map/ppermute | solution.py:31
  9.4 83.8 %collective-permute-start.2 = (s32[16]{0:T(128)S(1)}, s32[16]{0:T(128)S(1)}, u32[]{:S(2)}, u32[]{:S(2)}) collective-permute-start(s32[16]{0:T(128)S(1)} %add_select_fusion), channel_id=1, source_target_pairs={{0,0},{33,1},{66,2},{99,3},{132,4},{165,5},{198,6},{231,7},{264,8}... | collective-permute-start | bytes 200 | tf_op jit(solution)/shard_map/ppermute | solution.py:31
  28.6 79.8 %collective-permute-start.6 = (s32[16]{0:T(128)S(1)}, s32[16]{0:T(128)S(1)}, u32[]{:S(2)}, u32[]{:S(2)}) collective-permute-start(s32[16]{0:T(128)S(1)} %add_select_fusion), channel_id=1, source_target_pairs={{32,0},{65,1},{98,2},{131,3},{164,4},{197,5},{230,6},{263,7},{296,... | collective-permute-start | bytes 200 | tf_op jit(solution)/shard_map/ppermute | solution.py:31
  33.7 26.5 %collective-permute-start.9 = (bf16[8,128,128]{2,1,0:T(8,128)(2,1)S(1)}, bf16[8,128,128]{2,1,0:T(8,128)(2,1)S(1)}, u32[]{:S(2)}, u32[]{:S(2)}) collective-permute-start(bf16[8,128,128]{2,1,0:T(8,128)(2,1)S(1)} %dynamic-slice_bitcast_fusion), channel_id=1, source_target_pairs={{2,0},{3,1},{4,2},{5,3},{6,4},{7,5},{8,6},{9,7},{10,8},{11,9},{12,... | collective-permute-start | bytes 786440 | tf_op jit(solution)/shard_map/ppermute | solution.py:31
  52.8 5.4 %collective-permute-start.8 = (s32[8]{0:T(128)S(1)}, s32[8]{0:T(128)S(1)}, u32[]{:S(2)}, u32[]{:S(2)}) collective-permute-start(s32[8]{0:T(128)S(1)} %fusion.57), channel_id=1, source_target_pairs={{2,0},{3,1},{4,2},{5,3},{6,4},{7,5},{8,6},{9,7},{10,8},{11,9},{12,... | collective-permute-start | bytes 104 | tf_op jit(solution)/shard_map/ppermute | solution.py:31
  54.7 36.0 %collective-permute-start.13 = (bf16[8,128,128]{2,1,0:T(8,128)(2,1)S(1)}, bf16[8,128,128]{2,1,0:T(8,128)(2,1)S(1)}, u32[]{:S(2)}, u32[]{:S(2)}) collective-permute-start(bf16[8,128,128]{2,1,0:T(8,128)(2,1)S(1)} %dynamic-slice_bitcast_fusion), channel_id=1, source_target_pairs={{3,0},{4,1},{5,2},{6,3},{7,4},{8,5},{9,6},{10,7},{11,8},{12,9},{13... | collective-permute-start | bytes 786440 | tf_op jit(solution)/shard_map/ppermute | solution.py:31
  58.2 17.9 %collective-permute-start.12 = (s32[8]{0:T(128)S(1)}, s32[8]{0:T(128)S(1)}, u32[]{:S(2)}, u32[]{:S(2)}) collective-permute-start(s32[8]{0:T(128)S(1)} %fusion.57), channel_id=1, source_target_pairs={{3,0},{4,1},{5,2},{6,3},{7,4},{8,5},{9,6},{10,7},{11,8},{12,9},{13... | collective-permute-start | bytes 104 | tf_op jit(solution)/shard_map/ppermute | solution.py:31
  60.2 43.9 %collective-permute-start.3 = (bf16[16,128,128]{2,1,0:T(8,128)(2,1)S(1)}, bf16[16,128,128]{2,1,0:T(8,128)(2,1)S(1)}, u32[]{:S(2)}, u32[]{:S(2)}) collective-permute-start(bf16[16,128,128]{2,1,0:T(8,128)(2,1)S(1)} %bitcast.224), channel_id=1, source_target_pairs={{0,0},{33,1},{66,2},{99,3},{132,4},{165,5},{198,6},{231,7},{264,8}... | collective-permute-start | bytes 1572872 | tf_op jit(solution)/shard_map/ppermute | solution.py:31
  76.1 59.4 %collective-permute-start.7 = (bf16[16,128,128]{2,1,0:T(8,128)(2,1)S(1)}, bf16[16,128,128]{2,1,0:T(8,128)(2,1)S(1)}, u32[]{:S(2)}, u32[]{:S(2)}) collective-permute-start(bf16[16,128,128]{2,1,0:T(8,128)(2,1)S(1)} %bitcast.225), channel_id=1, source_target_pairs={{32,0},{65,1},{98,2},{131,3},{164,4},{197,5},{230,6},{263,7},{296,... | collective-permute-start | bytes 1572872 | tf_op jit(solution)/shard_map/ppermute | solution.py:31
  90.8 47.1 %collective-permute-start.10 = (s32[16]{0:T(128)S(1)}, s32[16]{0:T(128)S(1)}, u32[]{:S(2)}, u32[]{:S(2)}) collective-permute-start(s32[16]{0:T(128)S(1)} %add_select_fusion), channel_id=1, source_target_pairs={{64,0},{97,1},{130,2},{163,3},{196,4},{229,5},{262,6},{295,7},{328... | collective-permute-start | bytes 200 | tf_op jit(solution)/shard_map/ppermute | solution.py:31
  93.2 77.9 %collective-permute-start.11 = (bf16[16,128,128]{2,1,0:T(8,128)(2,1)S(1)}, bf16[16,128,128]{2,1,0:T(8,128)(2,1)S(1)}, u32[]{:S(2)}, u32[]{:S(2)}) collective-permute-start(bf16[16,128,128]{2,1,0:T(8,128)(2,1)S(1)} %bitcast.226), channel_id=1, source_target_pairs={{64,0},{97,1},{130,2},{163,3},{196,4},{229,5},{262,6},{295,7},{328... | collective-permute-start | bytes 1572872 | tf_op jit(solution)/shard_map/ppermute | solution.py:31
  104.1 69.4 %collective-permute-start.14 = (s32[16]{0:T(128)S(1)}, s32[16]{0:T(128)S(1)}, u32[]{:S(2)}, u32[]{:S(2)}) collective-permute-start(s32[16]{0:T(128)S(1)} %add_select_fusion), channel_id=1, source_target_pairs={{96,0},{129,1},{162,2},{195,3},{228,4},{261,5},{294,6},{327,7},{36... | collective-permute-start | bytes 200 | tf_op jit(solution)/shard_map/ppermute | solution.py:31
  108.4 73.1 %collective-permute-start.15 = (bf16[16,128,128]{2,1,0:T(8,128)(2,1)S(1)}, bf16[16,128,128]{2,1,0:T(8,128)(2,1)S(1)}, u32[]{:S(2)}, u32[]{:S(2)}) collective-permute-start(bf16[16,128,128]{2,1,0:T(8,128)(2,1)S(1)} %bitcast.227), channel_id=1, source_target_pairs={{96,0},{129,1},{162,2},{195,3},{228,4},{261,5},{294,6},{327,7},{36... | collective-permute-start | bytes 1572872 | tf_op jit(solution)/shard_map/ppermute | solution.py:31

commit v2 on v1

--- a/solution.py
+++ b/solution.py
@@ -1,12 +1,16 @@
+import functools
 import math
 
 import jax
 import jax.numpy as jnp
 from jax import lax
+from jax.experimental import pallas as pl
+from jax.experimental.pallas import tpu as pltpu
 from jax.sharding import PartitionSpec as P
 
 RB = 5
 STEPS = 4
+MESH = pl.DeviceIdType.MESH
 
 
 def densify(pieces, places, nrows, ncols):
@@ -22,13 +26,89 @@
     return dense.reshape(nrows * width, ncols * width).astype(pieces.dtype)
 
 
-def fetch(value, source_of, row_count, col_count):
-    pairs = []
-    for r in range(row_count):
-        for c in range(col_count):
-            sr, sc = source_of(r, c)
-            pairs.append((sr * col_count + sc, r * col_count + c))
-    return lax.ppermute(value, ("row", "col"), pairs)
+def exchange_kernel(row_count, col_count, groups,
+                    blocks_ref, meta_ref, recv_l, recv_r, recv_ml, recv_mr, send_sem, recv_sem):
+    r = lax.axis_index("row")
+    c = lax.axis_index("col")
+    a = r // groups
+    b = r % groups
+    plans = []
+    for s in range(STEPS):
+        l_self = (a + s) % col_count == 0
+        l_dst = (r, (c - a - s + 2 * col_count) % col_count)
+        l_src = (r, (c + a + s) % col_count)
+        r_self = (c + s) % col_count == 0
+        r_dst = ((r - groups * (c + s) + 2 * row_count) % row_count, c)
+        r_src = ((r + groups * (c + s)) % row_count, c)
+        plans.append((l_self, l_dst, l_src, r_self, r_dst, r_src))
+
+    barrier = pltpu.get_barrier_semaphore()
+    for l_self, l_dst, l_src, r_self, r_dst, r_src in plans:
+        for is_self, dst, src in ((l_self, l_dst, l_src), (r_self, r_dst, r_src)):
+            @pl.when(jnp.logical_not(is_self))
+            def _(dst=dst, src=src):
+                pl.semaphore_signal(barrier, 1, device_id=dst, device_id_type=MESH)
+                pl.semaphore_signal(barrier, 1, device_id=src, device_id_type=MESH)
+    peers = 0
+    for l_self, l_dst, l_src, r_self, r_dst, r_src in plans:
+        for is_self in (l_self, r_self):
+            peers = peers + jnp.where(is_self, 0, 2)
+    pl.semaphore_wait(barrier, peers)
+
+    copies = []
+    for s, (l_self, l_dst, l_src, r_self, r_dst, r_src) in enumerate(plans):
+        jobs = (
+            (l_self, l_dst, blocks_ref.at[b], recv_l.at[s], 4 * s),
+            (l_self, l_dst, meta_ref, recv_ml.at[s], 4 * s + 1),
+            (r_self, r_dst, blocks_ref, recv_r.at[s], 4 * s + 2),
+            (r_self, r_dst, meta_ref, recv_mr.at[s], 4 * s + 3),
+        )
+        for is_self, dst, src_ref, dst_ref, k in jobs:
+            local = pltpu.make_async_copy(src_ref, dst_ref, recv_sem.at[k])
+            remote = pltpu.make_async_remote_copy(
+                src_ref, dst_ref, send_sem.at[k], recv_sem.at[k],
+                device_id=dst, device_id_type=MESH,
+            )
+            copies.append((is_self, local, remote))
+
+            @pl.when(is_self)
+            def _(local=local):
+                local.start()
+
+            @pl.when(jnp.logical_not(is_self))
+            def _(remote=remote):
+                remote.start()
+
+    for is_self, local, remote in copies:
+        @pl.when(is_self)
+        def _(local=local):
+            local.wait()
+
+        @pl.when(jnp.logical_not(is_self))
+        def _(remote=remote):
+            remote.wait_send()
+            remote.wait_recv()
+
+
+def exchange(blocks, meta, row_count, col_count):
+    groups, slots, width = blocks.shape[0], blocks.shape[1], blocks.shape[2]
+    vmem = pl.BlockSpec(memory_space=pltpu.VMEM)
+    return pl.pallas_call(
+        functools.partial(exchange_kernel, row_count, col_count, groups),
+        out_shape=(
+            jax.ShapeDtypeStruct((STEPS, slots, width, width), blocks.dtype),
+            jax.ShapeDtypeStruct((STEPS, groups, slots, width, width), blocks.dtype),
+            jax.ShapeDtypeStruct((STEPS,) + meta.shape, meta.dtype),
+            jax.ShapeDtypeStruct((STEPS,) + meta.shape, meta.dtype),
+        ),
+        in_specs=[vmem, vmem],
+        out_specs=(vmem, vmem, vmem, vmem),
+        scratch_shapes=[
+            pltpu.SemaphoreType.DMA((4 * STEPS,)),
+            pltpu.SemaphoreType.DMA((4 * STEPS,)),
+        ],
+        compiler_params=pltpu.CompilerParams(collective_id=0, has_side_effects=True),
+    )(blocks, meta)
 
 
 def body(blocks, block_rows, block_cols, counts):
@@ -47,23 +127,16 @@
     right_places = jnp.where(
         live, block_rows[0, 0] * (groups * RB) + block_cols[0, 0] + offsets, -1
     ).reshape(-1)
-    left_pieces = lax.dynamic_index_in_dim(blocks[0, 0], lower, 0, keepdims=False)
     left_places = lax.dynamic_index_in_dim(left_places_all, lower, 0, keepdims=False)
-    right_pieces = blocks[0, 0].reshape(groups * slot_count, width, width)
+    meta = jnp.zeros((8, 128), jnp.int32)
+    meta = meta.at[0, :slot_count].set(left_places)
+    meta = meta.at[1, : groups * slot_count].set(right_places)
+    recv_l, recv_r, recv_ml, recv_mr = exchange(blocks[0, 0], meta, row_count, col_count)
     totals = jnp.zeros((RB * width, groups * RB * width), jnp.float32)
     for step in range(STEPS):
-        def left_source(r, c, step=step):
-            return r, (c + r // groups + step) % col_count
-
-        def right_source(r, c, step=step):
-            return (r + groups * c + groups * step) % row_count, c
-
-        lp = fetch(left_pieces, left_source, row_count, col_count)
-        lq = fetch(left_places, left_source, row_count, col_count)
-        rp = fetch(right_pieces, right_source, row_count, col_count)
-        rq = fetch(right_places, right_source, row_count, col_count)
-        right_dense = densify(rp, rq, RB, groups * RB)
-        left_dense = densify(lp, lq, RB, RB)
+        rp = recv_r[step].reshape(groups * slot_count, width, width)
+        right_dense = densify(rp, recv_mr[step, 1, : groups * slot_count], RB, groups * RB)
+        left_dense = densify(recv_l[step], recv_ml[step, 0, :slot_count], RB, RB)
         totals = totals + jnp.dot(left_dense, right_dense, preferred_element_type=jnp.float32)
     shift_amount = row_place - groups * col_place
     valid = (shift_amount >= 0) & (shift_amount < groups)

time: 289 us -> 247 us (0.85)
  Pallas kernels: 0 us -> 121 us
  starting transfers between devices: 91.4 us -> 0 us
  waiting for transfers between devices: 76.4 us -> 0 us
  local copies, waits for them, and re-layouts: 1.36 us -> 5.54 us
    pallas_call x0 -> x1, Pallas kernels: none -> 121 us  [exchange(): pl.pallas_call(functools.partial(exchange_kernel, row_count, col_count, g...]
    ppermute x16 -> x0, starting transfers between devices: 91.4 us -> none  [fetch(): return lax.ppermute(value, ('row', 'col'), pairs)]
    ppermute x16 -> x0, waiting for transfers between devices: 76.4 us -> none  [fetch(): return lax.ppermute(value, ('row', 'col'), pairs)]
    unnamed x2 -> x8, local copies, waits for them, and re-layouts: 0.01 us -> 3.68 us
  transfers between devices with their start and end apart: 16 -> 0, of which waited for: 5 -> 0; matrix products, arithmetic and copies ran while one was open for 4% -> 0% of each run, Pallas kernels for 0% -> 0%
where the time goes in v2:
time: 247 us
  Pallas kernels  121 us (49%)
  blocking collectives  102 us (41%)
  matrix products  12.7 us (5%)
  local copies, waits for them, and re-layouts  5.54 us (2%)
  between operations  3.23 us (1%)
  other arithmetic  2.92 us (1%)
    pallas_call x1, Pallas kernels, exchange(): pl.pallas_call(functools.partial(exchange_kernel, row_count, col_count, g...  121 us
    psum x2, blocking collectives, body(): overall = lax.psum(lax.psum(term, 'col'), 'row')  102 us
    dot_general x4, matrix products, body(): jnp.dot(left_dense, right_dense, preferred_element_type=jnp.float32)  7.17 us
    dot_general x8, matrix products, densify(): jnp.dot(onehot, pieces.reshape(count, width * width), preferred_element_t...  5.52 us

profile of v2, /device:TPU:256, one launch (start us, length us, event | category | flops | bytes accessed | tf_op | source)
XLA Modules:
  0.0 247.2 jit_solution(13004039389552243185)
XLA Ops:
  0.6 0.8 bitcast_select_fusion
  1.4 0.7 iota_compare_fusion.1
  2.4 0.7 multiply_add_fusion.2
  3.3 0.6 copy-done.1
  3.9 121.1 %shard_map.59 = (bf16[4,8,128,128]{3,2,1,0:T(8,128)(2,1)}, bf16[4,2,8,128,128]{4,3,2,1,0:T(8,128)(2,1)}, s32[4,8,128]{2,1,0:T(8,128)}, s32[4,8,128]{2,1,0:T(8,128)}) custom-call(bf16[2,8,128,128]{3,2,1,0:T(8,128)(2,1)} %bitcast.228, s32[8,128]{1,0:T(8,128)} %copy-done.1), custom_call_target="tpu_custom_call" | custom-call | tf_op jit(solution)/shard_map/pallas_call | solution.py:96
  125.1 1.7 slice_bitcast_fusion
  126.7 0.7 bitcast_bitcast_fusion.2
  127.4 0.7 slice_bitcast_fusion.8
  128.1 0.9 convolution_convert_fusion.3
  129.1 0.7 slice_bitcast_fusion.9
  129.8 0.5 convolution_convert_fusion.7
  130.3 1.5 fusion.6
  131.8 0.9 convolution_convert_fusion.2
  132.7 0.5 convolution_convert_fusion.6
  133.2 1.5 convolution_add_fusion.2
  134.7 0.7 bitcast_bitcast_fusion
  135.4 0.9 convolution_convert_fusion.1
  136.8 1.5 convolution_add_fusion.1
  138.3 0.9 convolution_convert_fusion
  139.2 0.5 convolution_convert_fusion.4
  139.7 2.7 %fusion.57 = (bf16[640,1280]{1,0:T(8,128)(2,1)}, f32[640,1280]{1,0:T(8,128)S(1)}) fusion(f32[640,1280]{1,0:T(8,128)S(1)} %convolution_add_fusion.1, bf16[80,8,10,128]{3,2,1,0:T(8,128)(2,1)S(1)} %bitcast.220, bf16[80,8,5,128]{3,2,1,0:T(8,128)(2,1)S(1)} %bitcast.225), kind=kOutput, calls=%fused_computation.106 | convolution fusion | flops 1050214400 | bytes 10649600 | tf_op jit(solution)/shard_map/dot_general | solution.py:140
  142.4 0.7 select_reduce_fusion
  143.7 24.6 %psum.14 = f32[]{:T(128)} all-reduce(f32[]{:T(128)S(6)} %select_n.37), channel_id=1, replica_groups=mesh['row'=32,'col'=16] {'col'}, use_global_device_ids=true, to_apply=%region_1.2 | all-reduce | flops 1 | bytes 8 | tf_op jit(solution)/shard_map/psum | solution.py:146
  168.3 77.1 %psum.15 = f32[]{:T(128)} all-reduce(f32[]{:T(128)} %psum.14), channel_id=1, replica_groups=mesh['row'=32,'col'=16] {'row'}, use_global_device_ids=true, to_apply=%region_2.3 | all-reduce | flops 1 | bytes 8 | tf_op jit(solution)/shard_map/psum | solution.py:146
  (16 shorter events, 1.1 us)
Async XLA Ops:
  3.3 0.6 copy-start.1
  126.7 2.3 copy-start

commit v3 on v2

--- a/solution.py
+++ b/solution.py
@@ -109,6 +109,114 @@
         ],
         compiler_params=pltpu.CompilerParams(collective_id=0, has_side_effects=True),
     )(blocks, meta)
+
+
+def trace_kernel(row_count, col_count, groups,
+                 term_ref, out_ref, row_buf, col_buf, send_sem, recv_sem, col_send, col_recv):
+    r = lax.axis_index("row")
+    c = lax.axis_index("col")
+    diagonal = c == r // groups
+    barrier = pltpu.get_barrier_semaphore()
+
+    @pl.when(diagonal)
+    def _():
+        for cc in range(col_count):
+            @pl.when(cc != c)
+            def _(cc=cc):
+                pl.semaphore_signal(barrier, 1, device_id=(r, cc), device_id_type=MESH)
+
+    @pl.when(jnp.logical_not(diagonal))
+    def _():
+        pl.semaphore_signal(barrier, 1, device_id=(r, r // groups), device_id_type=MESH)
+
+    for rr in range(row_count):
+        @pl.when(rr != r)
+        def _(rr=rr):
+            pl.semaphore_signal(barrier, 1, device_id=(rr, c), device_id_type=MESH)
+
+    pl.semaphore_wait(barrier, (row_count - 1) + jnp.where(diagonal, col_count - 1, 1))
+
+    row_copies = []
+    for cc in range(col_count):
+        row_copies.append(pltpu.make_async_remote_copy(
+            term_ref, row_buf, send_sem.at[cc], recv_sem.at[0],
+            device_id=(r, cc), device_id_type=MESH,
+        ))
+
+    @pl.when(diagonal)
+    def _():
+        for cc in range(col_count):
+            @pl.when(cc != c)
+            def _(cc=cc):
+                row_copies[cc].start()
+
+    @pl.when(jnp.logical_not(diagonal))
+    def _():
+        row_copies[0].wait_recv()
+
+    def col_copy(source, rr):
+        return pltpu.make_async_remote_copy(
+            source, col_buf.at[r], col_send.at[rr], col_recv.at[r],
+            device_id=(rr, c), device_id_type=MESH,
+        )
+
+    for source, chosen in ((term_ref, diagonal), (row_buf, jnp.logical_not(diagonal))):
+        @pl.when(chosen)
+        def _(source=source):
+            for rr in range(row_count):
+                @pl.when(rr != r)
+                def _(rr=rr):
+                    col_copy(source, rr).start()
+
+    for rr in range(row_count):
+        @pl.when(rr != r)
+        def _(rr=rr):
+            pltpu.make_async_remote_copy(
+                term_ref, col_buf.at[rr], col_send.at[rr], col_recv.at[rr],
+                device_id=(rr, c), device_id_type=MESH,
+            ).wait_recv()
+
+    for source, chosen in ((term_ref, diagonal), (row_buf, jnp.logical_not(diagonal))):
+        @pl.when(chosen)
+        def _(source=source):
+            for rr in range(row_count):
+                @pl.when(rr != r)
+                def _(rr=rr):
+                    col_copy(source, rr).wait_send()
+            col_buf[r] = source[...]
+
+    @pl.when(diagonal)
+    def _():
+        for cc in range(col_count):
+            @pl.when(cc != c)
+            def _(cc=cc):
+                row_copies[cc].wait_send()
+
+    total = jnp.zeros(out_ref.shape, jnp.float32)
+    for rr in range(row_count):
+        total = total + col_buf[rr]
+    out_ref[...] = total
+
+
+def trace_total(term, row_count, col_count, groups):
+    tile = jnp.broadcast_to(term, (8, 128))
+    vmem = pl.BlockSpec(memory_space=pltpu.VMEM)
+    out = pl.pallas_call(
+        functools.partial(trace_kernel, row_count, col_count, groups),
+        out_shape=jax.ShapeDtypeStruct((8, 128), jnp.float32),
+        in_specs=[vmem],
+        out_specs=vmem,
+        scratch_shapes=[
+            pltpu.VMEM((8, 128), jnp.float32),
+            pltpu.VMEM((row_count, 8, 128), jnp.float32),
+            pltpu.SemaphoreType.DMA((col_count,)),
+            pltpu.SemaphoreType.DMA((1,)),
+            pltpu.SemaphoreType.DMA((row_count,)),
+            pltpu.SemaphoreType.DMA((row_count,)),
+        ],
+        compiler_params=pltpu.CompilerParams(collective_id=1, has_side_effects=True),
+    )(tile)
+    return out[0, 0]
 
 
 def body(blocks, block_rows, block_cols, counts):
@@ -143,7 +251,7 @@
     start = jnp.clip(shift_amount, 0, groups - 1) * RB * width
     window = lax.dynamic_slice_in_dim(totals, start, RB * width, 1)
     term = jnp.where(valid, jnp.trace(window), jnp.zeros((), jnp.float32))
-    overall = lax.psum(lax.psum(term, "col"), "row")
+    overall = trace_total(term, row_count, col_count, groups)
     trace_value = overall / math.sqrt(row_count * RB * width)
     return (totals.astype(jnp.bfloat16), trace_value)
 

time: 247 us -> 177 us (0.72)
  the two profiles are of different devices: /device:TPU:256 before, /device:TPU:1 now
where the time goes in v3:
time: 177 us; the launch traced here: 176 us
  Pallas kernels  150 us (85%)
  matrix products  12.7 us (7%)
  local copies, waits for them, and re-layouts  7.33 us (4%)
  between operations  3.24 us (2%)
  other arithmetic  2.92 us (2%)
    pallas_call x1, Pallas kernels, trace_total(): pl.pallas_call(functools.partial(trace_kernel, row_count, col_count, grou...  76.2 us
    pallas_call x1, Pallas kernels, exchange(): pl.pallas_call(functools.partial(exchange_kernel, row_count, col_count, g...  73.7 us
    dot_general x4, matrix products, body(): jnp.dot(left_dense, right_dense, preferred_element_type=jnp.float32)  7.15 us
    dot_general x8, matrix products, densify(): jnp.dot(onehot, pieces.reshape(count, width * width), preferred_element_t...  5.51 us
    unnamed x8, local copies, waits for them, and re-layouts  3.69 us

profile of v3, /device:TPU:1, one launch (start us, length us, event | category | flops | bytes accessed | tf_op | source)
XLA Modules:
  0.0 176.1 jit_solution(2913908664130498533)
XLA Ops:
  0.6 0.8 bitcast_select_fusion
  1.4 0.7 iota_compare_fusion.1
  2.4 0.7 multiply_add_fusion.2
  3.3 0.6 copy-done.1
  3.9 73.7 %shard_map.59 = (bf16[4,8,128,128]{3,2,1,0:T(8,128)(2,1)}, bf16[4,2,8,128,128]{4,3,2,1,0:T(8,128)(2,1)}, s32[4,8,128]{2,1,0:T(8,128)}, s32[4,8,128]{2,1,0:T(8,128)}) custom-call(bf16[2,8,128,128]{3,2,1,0:T(8,128)(2,1)} %bitcast.229, s32[8,128]{1,0:T(8,128)} %copy-done.1), custom_call_target="tpu_custom_call" | custom-call | tf_op jit(solution)/shard_map/pallas_call | solution.py:96
  77.6 1.7 slice_bitcast_fusion
  79.3 0.7 bitcast_bitcast_fusion.2
  80.0 0.7 slice_bitcast_fusion.8
  80.7 0.9 convolution_convert_fusion.3
  81.7 0.7 slice_bitcast_fusion.9
  82.4 0.5 convolution_convert_fusion.7
  82.9 1.5 fusion.6
  84.4 0.9 convolution_convert_fusion.2
  85.3 0.5 convolution_convert_fusion.6
  85.8 1.5 convolution_add_fusion.2
  87.3 0.7 bitcast_bitcast_fusion
  88.0 0.9 convolution_convert_fusion.1
  89.4 1.5 convolution_add_fusion.1
  90.9 0.9 convolution_convert_fusion
  92.3 2.7 %fusion.57 = (bf16[640,1280]{1,0:T(8,128)(2,1)}, f32[640,1280]{1,0:T(8,128)S(1)}) fusion(f32[640,1280]{1,0:T(8,128)S(1)} %convolution_add_fusion.1, bf16[80,8,10,128]{3,2,1,0:T(8,128)(2,1)S(1)} %bitcast.221, bf16[80,8,5,128]{3,2,1,0:T(8,128)(2,1)S(1)} %bitcast.226), kind=kOutput, calls=%fused_computation.106 | convolution fusion | flops 1050214400 | bytes 10649600 | tf_op jit(solution)/shard_map/dot_general | solution.py:248
  94.9 0.7 select_reduce_fusion
  96.3 0.6 broadcast_in_dim.28.term_ref
  96.9 76.2 %shard_map.60 = f32[8,128]{1,0:T(8,128)} custom-call(f32[8,128]{1,0:T(8,128)} %broadcast_in_dim.28.term_ref), custom_call_target="tpu_custom_call" | custom-call | tf_op jit(solution)/shard_map/pallas_call | solution.py:204
  173.1 1.2 slice.102
  (17 shorter events, 1.6 us)
Async XLA Ops:
  3.3 0.6 copy-start.1
  79.3 2.3 %copy-start = (bf16[4,8,128,128]{3,2,1,0:T(8,128)(2,1)S(1)}, bf16[4,8,128,128]{3,2,1,0:T(8,128)(2,1)}, u32[]{:S(2)}) copy-start(bf16[4,8,128,128]{3,2,1,0:T(8,128)(2,1)} %get-tuple-element.31) | copy-start | bytes 3145732

commit v4 on v3

--- a/solution.py
+++ b/solution.py
@@ -32,62 +32,108 @@
     c = lax.axis_index("col")
     a = r // groups
     b = r % groups
-    plans = []
-    for s in range(STEPS):
-        l_self = (a + s) % col_count == 0
-        l_dst = (r, (c - a - s + 2 * col_count) % col_count)
-        l_src = (r, (c + a + s) % col_count)
-        r_self = (c + s) % col_count == 0
-        r_dst = ((r - groups * (c + s) + 2 * row_count) % row_count, c)
-        r_src = ((r + groups * (c + s)) % row_count, c)
-        plans.append((l_self, l_dst, l_src, r_self, r_dst, r_src))
+
+    def l_self(s):
+        return (a + s) % col_count == 0
+
+    def r_self(s):
+        return (c + s) % col_count == 0
+
+    def l_at(shift):
+        return (r, (c + shift + 4 * col_count) % col_count)
+
+    def r_at(shift):
+        return ((r + shift + 4 * row_count) % row_count, c)
+
+    left_plan, right_plan = {}, {}
+    left_plan[1] = (l_self(1), l_at(-(a + 1)), l_at(a + 1))
+    right_plan[1] = (r_self(1), r_at(-groups * (c + 1)), r_at(groups * (c + 1)))
+    for s in (0, 2, 3):
+        left_plan[s] = (l_self(s), l_at(1 - s), l_at(s - 1))
+        right_plan[s] = (r_self(s), r_at(groups * (1 - s)), r_at(groups * (s - 1)))
 
     barrier = pltpu.get_barrier_semaphore()
-    for l_self, l_dst, l_src, r_self, r_dst, r_src in plans:
-        for is_self, dst, src in ((l_self, l_dst, l_src), (r_self, r_dst, r_src)):
+    peers = 0
+    for plan in (left_plan, right_plan):
+        for s in range(STEPS):
+            is_self, dst, src = plan[s]
+
             @pl.when(jnp.logical_not(is_self))
             def _(dst=dst, src=src):
                 pl.semaphore_signal(barrier, 1, device_id=dst, device_id_type=MESH)
                 pl.semaphore_signal(barrier, 1, device_id=src, device_id_type=MESH)
-    peers = 0
-    for l_self, l_dst, l_src, r_self, r_dst, r_src in plans:
-        for is_self in (l_self, r_self):
+
             peers = peers + jnp.where(is_self, 0, 2)
     pl.semaphore_wait(barrier, peers)
 
-    copies = []
-    for s, (l_self, l_dst, l_src, r_self, r_dst, r_src) in enumerate(plans):
-        jobs = (
-            (l_self, l_dst, blocks_ref.at[b], recv_l.at[s], 4 * s),
-            (l_self, l_dst, meta_ref, recv_ml.at[s], 4 * s + 1),
-            (r_self, r_dst, blocks_ref, recv_r.at[s], 4 * s + 2),
-            (r_self, r_dst, meta_ref, recv_mr.at[s], 4 * s + 3),
+    sides = (
+        (left_plan, blocks_ref.at[b], recv_l, 0),
+        (left_plan, meta_ref, recv_ml, 1),
+        (right_plan, blocks_ref, recv_r, 2),
+        (right_plan, meta_ref, recv_mr, 3),
+    )
+
+    def transfer(plan, s, source, recv, j):
+        is_self, dst, _ = plan[s]
+        k = 4 * s + j
+        local = pltpu.make_async_copy(source, recv.at[s], recv_sem.at[k])
+        remote = pltpu.make_async_remote_copy(
+            source, recv.at[s], send_sem.at[k], recv_sem.at[k],
+            device_id=dst, device_id_type=MESH,
         )
-        for is_self, dst, src_ref, dst_ref, k in jobs:
-            local = pltpu.make_async_copy(src_ref, dst_ref, recv_sem.at[k])
-            remote = pltpu.make_async_remote_copy(
-                src_ref, dst_ref, send_sem.at[k], recv_sem.at[k],
-                device_id=dst, device_id_type=MESH,
-            )
-            copies.append((is_self, local, remote))
+        return is_self, local, remote
+
+    def start(job, forward):
+        is_self, local, remote = job
+
+        if not forward:
+            @pl.when(is_self)
+            def _():
+                local.start()
+
+        @pl.when(jnp.logical_not(is_self))
+        def _():
+            remote.start()
+
+    def finish_recv(job):
+        is_self, local, remote = job
+
+        @pl.when(is_self)
+        def _():
+            local.wait()
+
+        @pl.when(jnp.logical_not(is_self))
+        def _():
+            remote.wait_recv()
+
+    def finish_send(job):
+        is_self, local, remote = job
+
+        @pl.when(jnp.logical_not(is_self))
+        def _():
+            remote.wait_send()
+
+    firsts = [transfer(plan, 1, source, recv, j) for plan, source, recv, j in sides]
+    for job in firsts:
+        start(job, False)
+    forwards = []
+    for plan, source, recv, j in sides:
+        for s in (0, 2, 3):
+            forwards.append(transfer(plan, s, recv.at[1], recv, j))
+    for (plan, source, recv, j), first in zip(sides, firsts):
+        finish_recv(first)
+        for s in (0, 2, 3):
+            is_self, local, remote = transfer(plan, s, source, recv, j)
 
             @pl.when(is_self)
             def _(local=local):
                 local.start()
-
-            @pl.when(jnp.logical_not(is_self))
-            def _(remote=remote):
-                remote.start()
-
-    for is_self, local, remote in copies:
-        @pl.when(is_self)
-        def _(local=local):
-            local.wait()
-
-        @pl.when(jnp.logical_not(is_self))
-        def _(remote=remote):
-            remote.wait_send()
-            remote.wait_recv()
+    for job in forwards:
+        start(job, True)
+    for job in forwards:
+        finish_recv(job)
+    for job in firsts + forwards:
+        finish_send(job)
 
 
 def exchange(blocks, meta, row_count, col_count):

time: 177 us -> 119 us (0.67)
  Pallas kernels: 150 us -> 92.3 us
    pallas_call x1, Pallas kernels: 76.2 us -> 42.2 us  [trace_total(): pl.pallas_call(functools.partial(trace_kernel, row_count, col_count, grou...]
    pallas_call x1, Pallas kernels: 73.7 us -> 50.1 us  [exchange(): pl.pallas_call(functools.partial(exchange_kernel, row_count, col_count, g...]
where the time goes in v4:
time: 119 us; the launch traced here: 118 us
  Pallas kernels  92.3 us (78%)
  matrix products  12.7 us (11%)
  local copies, waits for them, and re-layouts  7.33 us (6%)
  between operations  3.24 us (3%)
  other arithmetic  2.92 us (2%)
    pallas_call x1, Pallas kernels, exchange(): pl.pallas_call(functools.partial(exchange_kernel, row_count, col_count, g...  50.1 us
    pallas_call x1, Pallas kernels, trace_total(): pl.pallas_call(functools.partial(trace_kernel, row_count, col_count, grou...  42.2 us
    dot_general x4, matrix products, body(): jnp.dot(left_dense, right_dense, preferred_element_type=jnp.float32)  7.14 us
    dot_general x8, matrix products, densify(): jnp.dot(onehot, pieces.reshape(count, width * width), preferred_element_t...  5.52 us
    unnamed x8, local copies, waits for them, and re-layouts  3.69 us

profile of v4, /device:TPU:1, one launch (start us, length us, event | category | flops | bytes accessed | tf_op | source)
XLA Modules:
  0.0 118.5 jit_solution(7249009704104891346)
XLA Ops:
  0.6 0.8 bitcast_select_fusion
  1.4 0.7 iota_compare_fusion.1
  2.4 0.7 multiply_add_fusion.2
  3.3 0.6 copy-done.1
  3.9 50.1 %shard_map.59 = (bf16[4,8,128,128]{3,2,1,0:T(8,128)(2,1)}, bf16[4,2,8,128,128]{4,3,2,1,0:T(8,128)(2,1)}, s32[4,8,128]{2,1,0:T(8,128)}, s32[4,8,128]{2,1,0:T(8,128)}) custom-call(bf16[2,8,128,128]{3,2,1,0:T(8,128)(2,1)} %bitcast.229, s32[8,128]{1,0:T(8,128)} %copy-done.1), custom_call_target="tpu_custom_call" | custom-call | tf_op jit(solution)/shard_map/pallas_call | solution.py:142
  54.0 1.7 %slice_bitcast_fusion = (bf16[2,8,128,128]{3,2,1,0:T(8,128)(2,1)S(1)}, bf16[2,8,128,128]{3,2,1,0:T(8,128)(2,1)S(1)}, bf16[2,8,128,128]{3,2,1,0:T(8,128)(2,1)S(1)}, bf16[2,8,128,128]{3,2,1,0:T(8,128)(2,1)S(1)}) fusion(bf16[4,2,8,128,128]{4,3,2,1,0:T(8,128)(2,1)} %get-tuple-element.33), kind=kLoop, calls=%fused_computation.42 | loop fusion | bytes 4194304
  55.7 0.7 bitcast_bitcast_fusion.2
  56.4 0.7 slice_bitcast_fusion.8
  57.1 0.9 convolution_convert_fusion.3
  58.1 0.7 slice_bitcast_fusion.9
  58.8 0.5 convolution_convert_fusion.7
  59.3 1.5 %fusion.6 = f32[640,1280]{1,0:T(8,128)S(1)} fusion(bf16[80,8,10,128]{3,2,1,0:T(8,128)(2,1)S(1)} %bitcast.227, bf16[80,8,5,128]{3,2,1,0:T(8,128)(2,1)S(1)} %bitcast.228), kind=kOutput, calls=%fused_computation.13 | convolution fusion | flops 1048576000 | bytes 5734400 | tf_op jit(solution)/shard_map/dot_general | solution.py:294
  60.8 0.9 convolution_convert_fusion.2
  61.7 0.5 convolution_convert_fusion.6
  62.2 1.5 %convolution_add_fusion.2 = f32[640,1280]{1,0:T(8,128)S(1)} fusion(f32[640,1280]{1,0:T(8,128)S(1)} %fusion.6, bf16[80,8,10,128]{3,2,1,0:T(8,128)(2,1)S(1)} %bitcast.222, bf16[80,8,5,128]{3,2,1,0:T(8,128)(2,1)S(1)} %bitcast.224), kind=kOutput, calls=%fused_computation.2 | convolution fusion | flops 1049395200 | bytes 9011200 | tf_op jit(solution)/shard_map/dot_general | solution.py:294
  63.7 0.7 bitcast_bitcast_fusion
  64.4 0.9 convolution_convert_fusion.1
  65.7 1.5 %convolution_add_fusion.1 = f32[640,1280]{1,0:T(8,128)S(1)} fusion(f32[640,1280]{1,0:T(8,128)S(1)} %convolution_add_fusion.2, bf16[80,8,10,128]{3,2,1,0:T(8,128)(2,1)S(1)} %bitcast.223, bf16[80,8,5,128]{3,2,1,0:T(8,128)(2,1)S(1)} %bitcast.225), kind=kOutput, calls=%fused_computation.1 | convolution fusion | flops 1049395200 | bytes 9011200 | tf_op jit(solution)/shard_map/dot_general | solution.py:294
  67.3 0.9 convolution_convert_fusion
  68.7 2.7 %fusion.57 = (bf16[640,1280]{1,0:T(8,128)(2,1)}, f32[640,1280]{1,0:T(8,128)S(1)}) fusion(f32[640,1280]{1,0:T(8,128)S(1)} %convolution_add_fusion.1, bf16[80,8,10,128]{3,2,1,0:T(8,128)(2,1)S(1)} %bitcast.221, bf16[80,8,5,128]{3,2,1,0:T(8,128)(2,1)S(1)} %bitcast.226), kind=kOutput, calls=%fused_computation.106 | convolution fusion | flops 1050214400 | bytes 10649600 | tf_op jit(solution)/shard_map/dot_general | solution.py:294
  71.3 0.7 select_reduce_fusion
  72.7 0.6 broadcast_in_dim.28.term_ref
  73.3 42.2 %shard_map.60 = f32[8,128]{1,0:T(8,128)} custom-call(f32[8,128]{1,0:T(8,128)} %broadcast_in_dim.28.term_ref), custom_call_target="tpu_custom_call" | custom-call | tf_op jit(solution)/shard_map/pallas_call | solution.py:250
  115.5 1.2 %slice.102 = f32[1,1]{1,0:T(1,128)} slice(f32[8,128]{1,0:T(8,128)} %shard_map.60), slice={[0:1], [0:1]} | slice | bytes 8 | tf_op jit(solution)/shard_map/slice | solution.py:265
  (17 shorter events, 1.6 us)
Async XLA Ops:
  3.3 0.6 copy-start.1
  55.7 2.3 %copy-start = (bf16[4,8,128,128]{3,2,1,0:T(8,128)(2,1)S(1)}, bf16[4,8,128,128]{3,2,1,0:T(8,128)(2,1)}, u32[]{:S(2)}) copy-start(bf16[4,8,128,128]{3,2,1,0:T(8,128)(2,1)} %get-tuple-element.31) | copy-start | bytes 3145732

commit v5 on v4

--- a/solution.py
+++ b/solution.py
@@ -162,6 +162,7 @@
     r = lax.axis_index("row")
     c = lax.axis_index("col")
     diagonal = c == r // groups
+    rounds = (row_count - 1).bit_length()
     barrier = pltpu.get_barrier_semaphore()
 
     @pl.when(diagonal)
@@ -175,12 +176,10 @@
     def _():
         pl.semaphore_signal(barrier, 1, device_id=(r, r // groups), device_id_type=MESH)
 
-    for rr in range(row_count):
-        @pl.when(rr != r)
-        def _(rr=rr):
-            pl.semaphore_signal(barrier, 1, device_id=(rr, c), device_id_type=MESH)
-
-    pl.semaphore_wait(barrier, (row_count - 1) + jnp.where(diagonal, col_count - 1, 1))
+    for k in range(rounds):
+        pl.semaphore_signal(barrier, 1, device_id=(r ^ (1 << k), c), device_id_type=MESH)
+
+    pl.semaphore_wait(barrier, rounds + jnp.where(diagonal, col_count - 1, 1))
 
     row_copies = []
     for cc in range(col_count):
@@ -200,36 +199,40 @@
     def _():
         row_copies[0].wait_recv()
 
-    def col_copy(source, rr):
-        return pltpu.make_async_remote_copy(
-            source, col_buf.at[r], col_send.at[rr], col_recv.at[r],
-            device_id=(rr, c), device_id_type=MESH,
-        )
-
+    partner = r ^ 1
     for source, chosen in ((term_ref, diagonal), (row_buf, jnp.logical_not(diagonal))):
         @pl.when(chosen)
         def _(source=source):
-            for rr in range(row_count):
-                @pl.when(rr != r)
-                def _(rr=rr):
-                    col_copy(source, rr).start()
-
-    for rr in range(row_count):
-        @pl.when(rr != r)
-        def _(rr=rr):
-            pltpu.make_async_remote_copy(
-                term_ref, col_buf.at[rr], col_send.at[rr], col_recv.at[rr],
-                device_id=(rr, c), device_id_type=MESH,
-            ).wait_recv()
-
-    for source, chosen in ((term_ref, diagonal), (row_buf, jnp.logical_not(diagonal))):
-        @pl.when(chosen)
-        def _(source=source):
-            for rr in range(row_count):
-                @pl.when(rr != r)
-                def _(rr=rr):
-                    col_copy(source, rr).wait_send()
-            col_buf[r] = source[...]
+            own = pltpu.make_async_copy(source, col_buf.at[r], recv_sem.at[1])
+            first = pltpu.make_async_remote_copy(
+                source, col_buf.at[r], col_send.at[0], col_recv.at[0],
+                device_id=(partner, c), device_id_type=MESH,
+            )
+            own.start()
+            first.start()
+            own.wait()
+            first.wait_send()
+
+    pltpu.make_async_remote_copy(
+        term_ref, col_buf.at[partner], col_send.at[0], col_recv.at[0],
+        device_id=(partner, c), device_id_type=MESH,
+    ).wait_recv()
+
+    for k in range(1, rounds):
+        size = 1 << k
+        partner = r ^ size
+        mine = pl.ds(pl.multiple_of(r - r % size, size), size)
+        theirs = pl.ds(pl.multiple_of(partner - partner % size, size), size)
+        step = pltpu.make_async_remote_copy(
+            col_buf.at[mine], col_buf.at[mine], col_send.at[k], col_recv.at[k],
+            device_id=(partner, c), device_id_type=MESH,
+        )
+        step.start()
+        pltpu.make_async_remote_copy(
+            col_buf.at[theirs], col_buf.at[theirs], col_send.at[k], col_recv.at[k],
+            device_id=(partner, c), device_id_type=MESH,
+        ).wait_recv()
+        step.wait_send()
 
     @pl.when(diagonal)
     def _():
@@ -256,7 +259,7 @@
             pltpu.VMEM((8, 128), jnp.float32),
             pltpu.VMEM((row_count, 8, 128), jnp.float32),
             pltpu.SemaphoreType.DMA((col_count,)),
-            pltpu.SemaphoreType.DMA((1,)),
+            pltpu.SemaphoreType.DMA((2,)),
             pltpu.SemaphoreType.DMA((row_count,)),
             pltpu.SemaphoreType.DMA((row_count,)),
         ],

time: 119 us -> 128 us (1.076)
  the two profiles are of different devices: /device:TPU:1 before, /device:TPU:64 now
where the time goes in v5:
time: 128 us; the launch traced here: 127 us
  Pallas kernels  101 us (79%)
  matrix products  12.7 us (10%)
  local copies, waits for them, and re-layouts  7.33 us (6%)
  between operations  3.24 us (3%)
  other arithmetic  2.92 us (2%)
    pallas_call x1, Pallas kernels, exchange(): pl.pallas_call(functools.partial(exchange_kernel, row_count, col_count, g...  58 us
    pallas_call x1, Pallas kernels, trace_total(): pl.pallas_call(functools.partial(trace_kernel, row_count, col_count, grou...  43 us
    dot_general x4, matrix products, body(): jnp.dot(left_dense, right_dense, preferred_element_type=jnp.float32)  7.15 us
    dot_general x8, matrix products, densify(): jnp.dot(onehot, pieces.reshape(count, width * width), preferred_element_t...  5.51 us
    unnamed x8, local copies, waits for them, and re-layouts  3.69 us

profile of v5, /device:TPU:64, one launch (start us, length us, event | category | flops | bytes accessed | tf_op | source)
XLA Modules:
  0.0 127.2 jit_solution(14092999668659864808)
XLA Ops:
  0.6 0.8 bitcast_select_fusion
  1.4 0.7 iota_compare_fusion.1
  2.4 0.7 multiply_add_fusion.2
  3.3 0.6 copy-done.1
  3.9 58.0 %shard_map.59 = (bf16[4,8,128,128]{3,2,1,0:T(8,128)(2,1)}, bf16[4,2,8,128,128]{4,3,2,1,0:T(8,128)(2,1)}, s32[4,8,128]{2,1,0:T(8,128)}, s32[4,8,128]{2,1,0:T(8,128)}) custom-call(bf16[2,8,128,128]{3,2,1,0:T(8,128)(2,1)} %bitcast.229, s32[8,128]{1,0:T(8,128)} %copy-done.1), custom_call_target="tpu_custom_call" | custom-call | tf_op jit(solution)/shard_map/pallas_call | solution.py:142
  61.9 1.7 %slice_bitcast_fusion = (bf16[2,8,128,128]{3,2,1,0:T(8,128)(2,1)S(1)}, bf16[2,8,128,128]{3,2,1,0:T(8,128)(2,1)S(1)}, bf16[2,8,128,128]{3,2,1,0:T(8,128)(2,1)S(1)}, bf16[2,8,128,128]{3,2,1,0:T(8,128)(2,1)S(1)}) fusion(bf16[4,2,8,128,128]{4,3,2,1,0:T(8,128)(2,1)} %get-tuple-element.33), kind=kLoop, calls=%fused_computation.42 | loop fusion | bytes 4194304
  63.6 0.7 bitcast_bitcast_fusion.2
  64.3 0.7 slice_bitcast_fusion.8
  65.0 0.9 convolution_convert_fusion.3
  66.0 0.7 slice_bitcast_fusion.9
  66.7 0.5 convolution_convert_fusion.7
  67.2 1.5 %fusion.6 = f32[640,1280]{1,0:T(8,128)S(1)} fusion(bf16[80,8,10,128]{3,2,1,0:T(8,128)(2,1)S(1)} %bitcast.227, bf16[80,8,5,128]{3,2,1,0:T(8,128)(2,1)S(1)} %bitcast.228), kind=kOutput, calls=%fused_computation.13 | convolution fusion | flops 1048576000 | bytes 5734400 | tf_op jit(solution)/shard_map/dot_general | solution.py:297
  68.7 0.9 convolution_convert_fusion.2
  69.6 0.5 convolution_convert_fusion.6
  70.1 1.5 %convolution_add_fusion.2 = f32[640,1280]{1,0:T(8,128)S(1)} fusion(f32[640,1280]{1,0:T(8,128)S(1)} %fusion.6, bf16[80,8,10,128]{3,2,1,0:T(8,128)(2,1)S(1)} %bitcast.222, bf16[80,8,5,128]{3,2,1,0:T(8,128)(2,1)S(1)} %bitcast.224), kind=kOutput, calls=%fused_computation.2 | convolution fusion | flops 1049395200 | bytes 9011200 | tf_op jit(solution)/shard_map/dot_general | solution.py:297
  71.6 0.7 bitcast_bitcast_fusion
  72.3 0.9 convolution_convert_fusion.1
  73.7 1.5 %convolution_add_fusion.1 = f32[640,1280]{1,0:T(8,128)S(1)} fusion(f32[640,1280]{1,0:T(8,128)S(1)} %convolution_add_fusion.2, bf16[80,8,10,128]{3,2,1,0:T(8,128)(2,1)S(1)} %bitcast.223, bf16[80,8,5,128]{3,2,1,0:T(8,128)(2,1)S(1)} %bitcast.225), kind=kOutput, calls=%fused_computation.1 | convolution fusion | flops 1049395200 | bytes 9011200 | tf_op jit(solution)/shard_map/dot_general | solution.py:297
  75.2 0.9 convolution_convert_fusion
  76.6 2.7 %fusion.57 = (bf16[640,1280]{1,0:T(8,128)(2,1)}, f32[640,1280]{1,0:T(8,128)S(1)}) fusion(f32[640,1280]{1,0:T(8,128)S(1)} %convolution_add_fusion.1, bf16[80,8,10,128]{3,2,1,0:T(8,128)(2,1)S(1)} %bitcast.221, bf16[80,8,5,128]{3,2,1,0:T(8,128)(2,1)S(1)} %bitcast.226), kind=kOutput, calls=%fused_computation.106 | convolution fusion | flops 1050214400 | bytes 10649600 | tf_op jit(solution)/shard_map/dot_general | solution.py:297
  79.2 0.7 select_reduce_fusion
  80.6 0.6 broadcast_in_dim.28.term_ref
  81.2 43.0 %shard_map.60 = f32[8,128]{1,0:T(8,128)} custom-call(f32[8,128]{1,0:T(8,128)} %broadcast_in_dim.28.term_ref), custom_call_target="tpu_custom_call" | custom-call | tf_op jit(solution)/shard_map/pallas_call | solution.py:253
  124.2 1.2 slice.102
  (17 shorter events, 1.6 us)
Async XLA Ops:
  3.3 0.6 copy-start.1
  63.6 2.3 %copy-start = (bf16[4,8,128,128]{3,2,1,0:T(8,128)(2,1)S(1)}, bf16[4,8,128,128]{3,2,1,0:T(8,128)(2,1)}, u32[]{:S(2)}) copy-start(bf16[4,8,128,128]{3,2,1,0:T(8,128)(2,1)} %get-tuple-element.31) | copy-start | bytes 3145732

commit v6 on v4

--- a/solution.py
+++ b/solution.py
@@ -66,35 +66,25 @@
             peers = peers + jnp.where(is_self, 0, 2)
     pl.semaphore_wait(barrier, peers)
 
-    sides = (
-        (left_plan, blocks_ref.at[b], recv_l, 0),
-        (left_plan, meta_ref, recv_ml, 1),
-        (right_plan, blocks_ref, recv_r, 2),
-        (right_plan, meta_ref, recv_mr, 3),
-    )
-
-    def transfer(plan, s, source, recv, j):
+    sides = [
+        (left_plan, meta_ref, lambda s: recv_ml.at[s]),
+        (right_plan, meta_ref, lambda s: recv_mr.at[s]),
+        (left_plan, blocks_ref.at[b], lambda s: recv_l.at[s]),
+    ]
+    for g in range(groups):
+        sides.append((right_plan, blocks_ref.at[g], lambda s, g=g: recv_r.at[s, g]))
+    kinds = len(sides)
+
+    def transfer(plan, s, source, target, j):
         is_self, dst, _ = plan[s]
-        k = 4 * s + j
-        local = pltpu.make_async_copy(source, recv.at[s], recv_sem.at[k])
+        k = kinds * s + j
+        local = pltpu.make_async_copy(source, target, recv_sem.at[k])
         remote = pltpu.make_async_remote_copy(
-            source, recv.at[s], send_sem.at[k], recv_sem.at[k],
+            source, target, send_sem.at[k], recv_sem.at[k],
             device_id=dst, device_id_type=MESH,
         )
         return is_self, local, remote
 
-    def start(job, forward):
-        is_self, local, remote = job
-
-        if not forward:
-            @pl.when(is_self)
-            def _():
-                local.start()
-
-        @pl.when(jnp.logical_not(is_self))
-        def _():
-            remote.start()
-
     def finish_recv(job):
         is_self, local, remote = job
 
@@ -106,34 +96,46 @@
         def _():
             remote.wait_recv()
 
-    def finish_send(job):
+    firsts = []
+    for j, (plan, source, target) in enumerate(sides):
+        job = transfer(plan, 1, source, target(1), j)
+        firsts.append(job)
         is_self, local, remote = job
 
+        @pl.when(is_self)
+        def _(local=local):
+            local.start()
+
         @pl.when(jnp.logical_not(is_self))
-        def _():
-            remote.wait_send()
-
-    firsts = [transfer(plan, 1, source, recv, j) for plan, source, recv, j in sides]
-    for job in firsts:
-        start(job, False)
-    forwards = []
-    for plan, source, recv, j in sides:
+        def _(remote=remote):
+            remote.start()
+
+    for j, (plan, source, target) in enumerate(sides):
         for s in (0, 2, 3):
-            forwards.append(transfer(plan, s, recv.at[1], recv, j))
-    for (plan, source, recv, j), first in zip(sides, firsts):
-        finish_recv(first)
-        for s in (0, 2, 3):
-            is_self, local, remote = transfer(plan, s, source, recv, j)
+            is_self, local, remote = transfer(plan, s, source, target(s), j)
 
             @pl.when(is_self)
             def _(local=local):
                 local.start()
-    for job in forwards:
-        start(job, True)
+
+    forwards = []
+    for j, (plan, source, target) in enumerate(sides):
+        finish_recv(firsts[j])
+        for s in (0, 2, 3):
+            job = transfer(plan, s, target(1), target(s), j)
+            forwards.append(job)
+            is_self, local, remote = job
+
+            @pl.when(jnp.logical_not(is_self))
+            def _(remote=remote):
+                remote.start()
+
     for job in forwards:
         finish_recv(job)
-    for job in firsts + forwards:
-        finish_send(job)
+    for is_self, local, remote in firsts + forwards:
+        @pl.when(jnp.logical_not(is_self))
+        def _(remote=remote):
+            remote.wait_send()
 
 
 def exchange(blocks, meta, row_count, col_count):
@@ -150,8 +152,8 @@
         in_specs=[vmem, vmem],
         out_specs=(vmem, vmem, vmem, vmem),
         scratch_shapes=[
-            pltpu.SemaphoreType.DMA((4 * STEPS,)),
-            pltpu.SemaphoreType.DMA((4 * STEPS,)),
+            pltpu.SemaphoreType.DMA(((3 + groups) * STEPS,)),
+            pltpu.SemaphoreType.DMA(((3 + groups) * STEPS,)),
         ],
         compiler_params=pltpu.CompilerParams(collective_id=0, has_side_effects=True),
     )(blocks, meta)

time: 119 us -> 114 us (0.958)
  Pallas kernels: 92.3 us -> 87.8 us
    pallas_call x1, Pallas kernels: 42.2 us -> 37.9 us  [trace_total(): pl.pallas_call(functools.partial(trace_kernel, row_count, col_count, grou...]
where the time goes in v6:
time: 114 us
  Pallas kernels  87.8 us (77%)
  matrix products  12.7 us (11%)
  local copies, waits for them, and re-layouts  7.33 us (6%)
  between operations  3.24 us (3%)
  other arithmetic  2.92 us (3%)
    pallas_call x1, Pallas kernels, exchange(): pl.pallas_call(functools.partial(exchange_kernel, row_count, col_count, g...  49.9 us
    pallas_call x1, Pallas kernels, trace_total(): pl.pallas_call(functools.partial(trace_kernel, row_count, col_count, grou...  37.9 us
    dot_general x4, matrix products, body(): jnp.dot(left_dense, right_dense, preferred_element_type=jnp.float32)  7.14 us
    dot_general x8, matrix products, densify(): jnp.dot(onehot, pieces.reshape(count, width * width), preferred_element_t...  5.52 us
    unnamed x8, local copies, waits for them, and re-layouts  3.69 us

profile of v6, /device:TPU:1, one launch (start us, length us, event | category | flops | bytes accessed | tf_op | source)
XLA Modules:
  0.0 113.9 jit_solution(15574898299421629686)
XLA Ops:
  0.6 0.8 bitcast_select_fusion
  1.4 0.7 iota_compare_fusion.1
  2.4 0.7 multiply_add_fusion.2
  3.3 0.6 copy-done.1
  3.9 49.9 %shard_map.59 = (bf16[4,8,128,128]{3,2,1,0:T(8,128)(2,1)}, bf16[4,2,8,128,128]{4,3,2,1,0:T(8,128)(2,1)}, s32[4,8,128]{2,1,0:T(8,128)}, s32[4,8,128]{2,1,0:T(8,128)}) custom-call(bf16[2,8,128,128]{3,2,1,0:T(8,128)(2,1)} %bitcast.229, s32[8,128]{1,0:T(8,128)} %copy-done.1), custom_call_target="tpu_custom_call" | custom-call | tf_op jit(solution)/shard_map/pallas_call | solution.py:144
  53.8 1.7 %slice_bitcast_fusion = (bf16[2,8,128,128]{3,2,1,0:T(8,128)(2,1)S(1)}, bf16[2,8,128,128]{3,2,1,0:T(8,128)(2,1)S(1)}, bf16[2,8,128,128]{3,2,1,0:T(8,128)(2,1)S(1)}, bf16[2,8,128,128]{3,2,1,0:T(8,128)(2,1)S(1)}) fusion(bf16[4,2,8,128,128]{4,3,2,1,0:T(8,128)(2,1)} %get-tuple-element.33), kind=kLoop, calls=%fused_computation.42 | loop fusion | bytes 4194304
  55.5 0.7 bitcast_bitcast_fusion.2
  56.2 0.7 slice_bitcast_fusion.8
  56.9 0.9 convolution_convert_fusion.3
  57.8 0.7 slice_bitcast_fusion.9
  58.5 0.5 convolution_convert_fusion.7
  59.1 1.5 %fusion.6 = f32[640,1280]{1,0:T(8,128)S(1)} fusion(bf16[80,8,10,128]{3,2,1,0:T(8,128)(2,1)S(1)} %bitcast.227, bf16[80,8,5,128]{3,2,1,0:T(8,128)(2,1)S(1)} %bitcast.228), kind=kOutput, calls=%fused_computation.13 | convolution fusion | flops 1048576000 | bytes 5734400 | tf_op jit(solution)/shard_map/dot_general | solution.py:296
  60.5 0.9 convolution_convert_fusion.2
  61.4 0.5 convolution_convert_fusion.6
  61.9 1.5 %convolution_add_fusion.2 = f32[640,1280]{1,0:T(8,128)S(1)} fusion(f32[640,1280]{1,0:T(8,128)S(1)} %fusion.6, bf16[80,8,10,128]{3,2,1,0:T(8,128)(2,1)S(1)} %bitcast.222, bf16[80,8,5,128]{3,2,1,0:T(8,128)(2,1)S(1)} %bitcast.224), kind=kOutput, calls=%fused_computation.2 | convolution fusion | flops 1049395200 | bytes 9011200 | tf_op jit(solution)/shard_map/dot_general | solution.py:296
  63.4 0.7 bitcast_bitcast_fusion
  64.1 0.9 convolution_convert_fusion.1
  65.5 1.5 %convolution_add_fusion.1 = f32[640,1280]{1,0:T(8,128)S(1)} fusion(f32[640,1280]{1,0:T(8,128)S(1)} %convolution_add_fusion.2, bf16[80,8,10,128]{3,2,1,0:T(8,128)(2,1)S(1)} %bitcast.223, bf16[80,8,5,128]{3,2,1,0:T(8,128)(2,1)S(1)} %bitcast.225), kind=kOutput, calls=%fused_computation.1 | convolution fusion | flops 1049395200 | bytes 9011200 | tf_op jit(solution)/shard_map/dot_general | solution.py:296
  67.0 0.9 convolution_convert_fusion
  68.4 2.7 %fusion.57 = (bf16[640,1280]{1,0:T(8,128)(2,1)}, f32[640,1280]{1,0:T(8,128)S(1)}) fusion(f32[640,1280]{1,0:T(8,128)S(1)} %convolution_add_fusion.1, bf16[80,8,10,128]{3,2,1,0:T(8,128)(2,1)S(1)} %bitcast.221, bf16[80,8,5,128]{3,2,1,0:T(8,128)(2,1)S(1)} %bitcast.226), kind=kOutput, calls=%fused_computation.106 | convolution fusion | flops 1050214400 | bytes 10649600 | tf_op jit(solution)/shard_map/dot_general | solution.py:296
  71.1 0.7 select_reduce_fusion
  72.4 0.6 broadcast_in_dim.28.term_ref
  73.0 37.9 %shard_map.60 = f32[8,128]{1,0:T(8,128)} custom-call(f32[8,128]{1,0:T(8,128)} %broadcast_in_dim.28.term_ref), custom_call_target="tpu_custom_call" | custom-call | tf_op jit(solution)/shard_map/pallas_call | solution.py:252
  110.9 1.2 %slice.102 = f32[1,1]{1,0:T(1,128)} slice(f32[8,128]{1,0:T(8,128)} %shard_map.60), slice={[0:1], [0:1]} | slice | bytes 8 | tf_op jit(solution)/shard_map/slice | solution.py:267
  (17 shorter events, 1.6 us)
Async XLA Ops:
  3.3 0.6 copy-start.1
  55.5 2.3 %copy-start = (bf16[4,8,128,128]{3,2,1,0:T(8,128)(2,1)S(1)}, bf16[4,8,128,128]{3,2,1,0:T(8,128)(2,1)}, u32[]{:S(2)}) copy-start(bf16[4,8,128,128]{3,2,1,0:T(8,128)(2,1)} %get-tuple-element.31) | copy-start | bytes 3145732

commit v7 on v6

v7 whole, which is shorter than its diff:
```python
import functools
import math

import jax
import jax.numpy as jnp
from jax import lax
from jax.experimental import pallas as pl
from jax.experimental.pallas import tpu as pltpu
from jax.sharding import PartitionSpec as P

RB = 5
STEPS = 4
MESH = pl.DeviceIdType.MESH


def densify(pieces, places, nrows, ncols):
    width = pieces.shape[-1]
    count = pieces.shape[0]
    onehot = (places[None, :] == jnp.arange(nrows * ncols, dtype=jnp.int32)[:, None]).astype(
        pieces.dtype
    )
    dense = jnp.dot(
        onehot, pieces.reshape(count, width * width), preferred_element_type=jnp.float32
    )
    dense = dense.reshape(nrows, ncols, width, width).transpose(0, 2, 1, 3)
    return dense.reshape(nrows * width, ncols * width).astype(pieces.dtype)


def exchange_kernel(row_count, col_count, groups,
                    blocks_ref, meta_ref, recv_l, recv_r, recv_ml, recv_mr, total_ref,
                    send_sem, recv_sem, term_buf, row_buf, col_buf, t_send, t_recv, c_send, c_recv):
    r = lax.axis_index("row")
    c = lax.axis_index("col")
    a = r // groups
    b = r % groups

    def l_self(s):
        return (a + s) % col_count == 0

    def r_self(s):
        return (c + s) % col_count == 0

    def l_at(shift):
        return (r, (c + shift + 4 * col_count) % col_count)

    def r_at(shift):
        return ((r + shift + 4 * row_count) % row_count, c)

    left_plan, right_plan = {}, {}
    left_plan[1] = (l_self(1), l_at(-(a + 1)), l_at(a + 1))
    right_plan[1] = (r_self(1), r_at(-groups * (c + 1)), r_at(groups * (c + 1)))
    for s in (0, 2, 3):
        left_plan[s] = (l_self(s), l_at(1 - s), l_at(s - 1))
        right_plan[s] = (r_self(s), r_at(groups * (1 - s)), r_at(groups * (s - 1)))

    barrier = pltpu.get_barrier_semaphore()
    peers = 0
    for plan in (left_plan, right_plan):
        for s in range(STEPS):
            is_self, dst, src = plan[s]

            @pl.when(jnp.logical_not(is_self))
            def _(dst=dst, src=src):
                pl.semaphore_signal(barrier, 1, device_id=dst, device_id_type=MESH)
                pl.semaphore_signal(barrier, 1, device_id=src, device_id_type=MESH)

            peers = peers + jnp.where(is_self, 0, 2)
    diagonal = c == a
    slots = blocks_ref.shape[1]
    width = blocks_ref.shape[2]

    @pl.when(diagonal)
    def _():
        for cc in range(col_count):
            @pl.when(cc != c)
            def _(cc=cc):
                pl.semaphore_signal(barrier, 1, device_id=(r, cc), device_id_type=MESH)

    @pl.when(jnp.logical_not(diagonal))
    def _():
        pl.semaphore_signal(barrier, 1, device_id=(r, a), device_id_type=MESH)

    for rr in range(row_count):
        @pl.when(rr != r)
        def _(rr=rr):
            pl.semaphore_signal(barrier, 1, device_id=(rr, c), device_id_type=MESH)

    peers = peers + (row_count - 1) + jnp.where(diagonal, col_count - 1, 1)
    pl.semaphore_wait(barrier, peers)

    sides = [
        (left_plan, meta_ref, lambda s: recv_ml.at[s]),
        (right_plan, meta_ref, lambda s: recv_mr.at[s]),
        (left_plan, blocks_ref.at[b], lambda s: recv_l.at[s]),
    ]
    for g in range(groups):
        sides.append((right_plan, blocks_ref.at[g], lambda s, g=g: recv_r.at[s, g]))
    kinds = len(sides)

    def transfer(plan, s, source, target, j):
        is_self, dst, _ = plan[s]
        k = kinds * s + j
        local = pltpu.make_async_copy(source, target, recv_sem.at[k])
        remote = pltpu.make_async_remote_copy(
            source, target, send_sem.at[k], recv_sem.at[k],
            device_id=dst, device_id_type=MESH,
        )
        return is_self, local, remote

    def finish_recv(job):
        is_self, local, remote = job

        @pl.when(is_self)
        def _():
            local.wait()

        @pl.when(jnp.logical_not(is_self))
        def _():
            remote.wait_recv()

    firsts = []
    for j, (plan, source, target) in enumerate(sides):
        job = transfer(plan, 1, source, target(1), j)
        firsts.append(job)
        is_self, local, remote = job

        @pl.when(is_self)
        def _(local=local):
            local.start()

        @pl.when(jnp.logical_not(is_self))
        def _(remote=remote):
            remote.start()

    for j, (plan, source, target) in enumerate(sides):
        for s in (0, 2, 3):
            is_self, local, remote = transfer(plan, s, source, target(s), j)

            @pl.when(is_self)
            def _(local=local):
                local.start()

    forwards = []
    for j, (plan, source, target) in enumerate(sides):
        finish_recv(firsts[j])
        for s in (0, 2, 3):
            job = transfer(plan, s, target(1), target(s), j)
            forwards.append(job)
            is_self, local, remote = job

            @pl.when(jnp.logical_not(is_self))
            def _(remote=remote):
                remote.start()

    for job in forwards:
        finish_recv(job)
    for is_self, local, remote in firsts + forwards:
        @pl.when(jnp.logical_not(is_self))
        def _(remote=remote):
            remote.wait_send()

    @pl.when(diagonal)
    def _():
        rows_i = lax.broadcasted_iota(jnp.int32, (width, slots * width), 0)
        cols_i = lax.broadcasted_iota(jnp.int32, (width, slots * width), 1)
        on_diag = rows_i == cols_i % width
        acc = jnp.zeros((1, 1), jnp.float32)
        for s in range(STEPS):
            rm = recv_mr.at[s]
            lm = recv_ml.at[s]
            rrow = jnp.concatenate(
                [rm[pl.ds(16 + slots * b + u, 1), :] for u in range(slots)], axis=1)
            rcol = jnp.concatenate(
                [rm[pl.ds(32 + slots * b + u, 1), :] for u in range(slots)], axis=1)
            right = jnp.concatenate([recv_r[s, b, u] for u in range(slots)], axis=1)
            for t in range(slots):
                lrow = jnp.concatenate([lm[t:t + 1, :]] * slots, axis=1)
                lcol = jnp.concatenate([lm[8 + t:9 + t, :]] * slots, axis=1)
                meet = (lcol == rrow) & (lrow == rcol)
                prod = jnp.dot(recv_l[s, t], right, preferred_element_type=jnp.float32)
                picked = jnp.where(on_diag & meet, prod, 0.0)
                acc = acc + jnp.sum(picked, keepdims=True)
        term_buf[...] = jnp.broadcast_to(acc, term_buf.shape)

    row_copies = []
    for cc in range(col_count):
        row_copies.append(pltpu.make_async_remote_copy(
            term_buf, row_buf, t_send.at[cc], t_recv.at[0],
            device_id=(r, cc), device_id_type=MESH,
        ))

    @pl.when(diagonal)
    def _():
        for cc in range(col_count):
            @pl.when(cc != c)
            def _(cc=cc):
                row_copies[cc].start()

    @pl.when(jnp.logical_not(diagonal))
    def _():
        row_copies[0].wait_recv()

    def col_copy(source, rr):
        return pltpu.make_async_remote_copy(
            source, col_buf.at[r], c_send.at[rr], c_recv.at[r],
            device_id=(rr, c), device_id_type=MESH,
        )

    for source, chosen in ((term_buf, diagonal), (row_buf, jnp.logical_not(diagonal))):
        @pl.when(chosen)
        def _(source=source):
            for rr in range(row_count):
                @pl.when(rr != r)
                def _(rr=rr):
                    col_copy(source, rr).start()

    for rr in range(row_count):
        @pl.when(rr != r)
        def _(rr=rr):
            pltpu.make_async_remote_copy(
                term_buf, col_buf.at[rr], c_send.at[rr], c_recv.at[rr],
                device_id=(rr, c), device_id_type=MESH,
            ).wait_recv()

    for source, chosen in ((term_buf, diagonal), (row_buf, jnp.logical_not(diagonal))):
        @pl.when(chosen)
        def _(source=source):
            for rr in range(row_count):
                @pl.when(rr != r)
                def _(rr=rr):
                    col_copy(source, rr).wait_send()
            col_buf[r] = source[...]

    @pl.when(diagonal)
    def _():
        for cc in range(col_count):
            @pl.when(cc != c)
            def _(cc=cc):
                row_copies[cc].wait_send()

    total = jnp.zeros(total_ref.shape, jnp.float32)
    for rr in range(row_count):
        total = total + col_buf[rr]
    total_ref[...] = total


def exchange(blocks, meta, row_count, col_count):
    groups, slots, width = blocks.shape[0], blocks.shape[1], blocks.shape[2]
    vmem = pl.BlockSpec(memory_space=pltpu.VMEM)
    kinds = 3 + groups
    return pl.pallas_call(
        functools.partial(exchange_kernel, row_count, col_count, groups),
        out_shape=(
            jax.ShapeDtypeStruct((STEPS, slots, width, width), blocks.dtype),
            jax.ShapeDtypeStruct((STEPS, groups, slots, width, width), blocks.dtype),
            jax.ShapeDtypeStruct((STEPS,) + meta.shape, meta.dtype),
            jax.ShapeDtypeStruct((STEPS,) + meta.shape, meta.dtype),
            jax.ShapeDtypeStruct((8, 128), jnp.float32),
        ),
        in_specs=[vmem, vmem],
        out_specs=(vmem, vmem, vmem, vmem, vmem),
        scratch_shapes=[
            pltpu.SemaphoreType.DMA((kinds * STEPS,)),
            pltpu.SemaphoreType.DMA((kinds * STEPS,)),
            pltpu.VMEM((8, 128), jnp.float32),
            pltpu.VMEM((8, 128), jnp.float32),
            pltpu.VMEM((row_count, 8, 128), jnp.float32),
            pltpu.SemaphoreType.DMA((col_count,)),
            pltpu.SemaphoreType.DMA((1,)),
            pltpu.SemaphoreType.DMA((row_count,)),
            pltpu.SemaphoreType.DMA((row_count,)),
        ],
        compiler_params=pltpu.CompilerParams(collective_id=0, has_side_effects=True),
    )(blocks, meta)


def body(blocks, block_rows, block_cols, counts):
    groups = blocks.shape[2]
    slot_count = blocks.shape[3]
    width = blocks.shape[4]
    row_count = lax.axis_size("row")
    col_count = lax.axis_size("col")
    row_place = lax.axis_index("row")
    col_place = lax.axis_index("col")
    lower = row_place % groups
    filled = counts[0, 0]
    live = jnp.arange(slot_count, dtype=jnp.int32)[None, :] < filled[:, None]
    left_places_all = jnp.where(live, block_rows[0, 0] * RB + block_cols[0, 0], -1)
    offsets = (jnp.arange(groups, dtype=jnp.int32) * RB)[:, None]
    right_places = jnp.where(
        live, block_rows[0, 0] * (groups * RB) + block_cols[0, 0] + offsets, -1
    ).reshape(-1)
    left_places = lax.dynamic_index_in_dim(left_places_all, lower, 0, keepdims=False)
    brows = block_rows[0, 0]
    bcols = block_cols[0, 0]
    left_live = lax.dynamic_index_in_dim(live, lower, 0, keepdims=False)
    lrow = jnp.where(left_live, lax.dynamic_index_in_dim(brows, lower, 0, keepdims=False), -100)
    lcol = jnp.where(left_live, lax.dynamic_index_in_dim(bcols, lower, 0, keepdims=False), -100)
    rrow = jnp.where(live, brows, -300).reshape(-1)
    rcol = jnp.where(live, bcols, -300).reshape(-1)
    meta = jnp.zeros((64, 128), jnp.int32)
    meta = meta.at[0:slot_count].set(jnp.broadcast_to(lrow[:, None], (slot_count, 128)))
    meta = meta.at[8:8 + slot_count].set(jnp.broadcast_to(lcol[:, None], (slot_count, 128)))
    meta = meta.at[16:16 + groups * slot_count].set(jnp.broadcast_to(rrow[:, None], (groups * slot_count, 128)))
    meta = meta.at[32:32 + groups * slot_count].set(jnp.broadcast_to(rcol[:, None], (groups * slot_count, 128)))
    meta = meta.at[48, :slot_count].set(left_places)
    meta = meta.at[49, : groups * slot_count].set(right_places)
    recv_l, recv_r, recv_ml, recv_mr, total_tile = exchange(blocks[0, 0], meta, row_count, col_count)
    totals = jnp.zeros((RB * width, groups * RB * width), jnp.float32)
    for step in range(STEPS):
        rp = recv_r[step].reshape(groups * slot_count, width, width)
        right_dense = densify(rp, recv_mr[step, 49, : groups * slot_count], RB, groups * RB)
        left_dense = densify(recv_l[step], recv_ml[step, 48, :slot_count], RB, RB)
        totals = totals + jnp.dot(left_dense, right_dense, preferred_element_type=jnp.float32)
    overall = total_tile[0, 0]
    trace_value = overall / math.sqrt(row_count * RB * width)
    return (totals.astype(jnp.bfloat16), trace_value)


def solution(mesh):
    return jax.shard_map(
        body,
        mesh=mesh,
        in_specs=(
            P("row", "col", None, None, None, None),
            P("row", "col", None, None),
            P("row", "col", None, None),
            P("row", "col", None),
        ),
        out_specs=(P("row", "col"), P()),
        check_vma=False,
    )
```

time: 114 us -> 117 us (1.026)
  Pallas kernels: 87.8 us -> 89.4 us
  local copies, waits for them, and re-layouts: 7.33 us -> 8.62 us
    pallas_call x1, Pallas kernels: 49.9 us -> 89.4 us  [exchange(): pl.pallas_call(functools.partial(exchange_kernel, row_count, col_count, g...]
    pallas_call x1 -> x0, Pallas kernels: 37.9 us -> none  [trace_total(): pl.pallas_call(functools.partial(trace_kernel, row_count, col_count, grou...]
    squeeze x0 -> x2, local copies, waits for them, and re-layouts: none -> 1.52 us  [the longest x1 0.76 us: body(): brows = block_rows[0, 0]]
where the time goes in v7:
time: 117 us; the launch traced here: 116 us
  Pallas kernels  89.4 us (76%)
  matrix products  12.7 us (11%)
  local copies, waits for them, and re-layouts  8.62 us (7%)
  other arithmetic  2.93 us (3%)
  between operations  2.59 us (2%)
    pallas_call x1, Pallas kernels, exchange(): pl.pallas_call(functools.partial(exchange_kernel, row_count, col_count, g...  89.4 us
    dot_general x4, matrix products, body(): jnp.dot(left_dense, right_dense, preferred_element_type=jnp.float32)  7.16 us
    dot_general x8, matrix products, densify(): jnp.dot(onehot, pieces.reshape(count, width * width), preferred_element_t...  5.51 us
    unnamed x8, local copies, waits for them, and re-layouts  3.52 us

profile of v7, /device:TPU:1, one launch (start us, length us, event | category | flops | bytes accessed | tf_op | source)
XLA Modules:
  0.0 116.2 jit_solution(3342969173287952868)
XLA Ops:
  0.6 0.7 iota_compare_fusion
  1.4 0.7 bitcast_select_fusion
  2.3 0.8 squeeze.30
  3.1 0.8 squeeze.31
  4.0 0.8 bitcast_select_fusion.2
  5.2 0.7 multiply_add_fusion.2
  6.1 0.6 copy-done.1
  6.7 89.4 %shard_map.59 = (bf16[4,8,128,128]{3,2,1,0:T(8,128)(2,1)}, bf16[4,2,8,128,128]{4,3,2,1,0:T(8,128)(2,1)}, s32[4,64,128]{2,1,0:T(8,128)}, s32[4,64,128]{2,1,0:T(8,128)}, f32[8,128]{1,0:T(8,128)}) custom-call(bf16[2,8,128,128]{3,2,1,0:T(8,128)(2,1)} %bitcast.236, s32[64,128]{1,0:T(8,128)} %copy-done.1), custom_call_target="tpu_custom_call" | custom-call | tf_op jit(solution)/shard_map/pallas_call | solution.py:251
  96.2 1.4 %slice_bitcast_fusion.4 = (bf16[1,8,128,128]{3,2,1,0:T(8,128)(2,1)S(1)}, bf16[1,8,128,128]{3,2,1,0:T(8,128)(2,1)S(1)}, bf16[1,8,128,128]{3,2,1,0:T(8,128)(2,1)S(1)}, bf16[1,8,128,128]{3,2,1,0:T(8,128)(2,1)S(1)}) fusion(bf16[4,8,128,128]{3,2,1,0:T(8,128)(2,1)} %get-tuple-element.80), kind=kLoop, calls=%fused_computation.53 | loop fusion | bytes 2097152
  97.6 0.7 slice_bitcast_fusion.9
  98.3 0.5 convolution_convert_fusion.7
  98.9 0.7 bitcast_bitcast_fusion.2
  99.6 0.7 slice_bitcast_fusion.8
  100.3 0.9 convolution_convert_fusion.3
  101.2 1.5 %fusion.7 = f32[640,1280]{1,0:T(8,128)S(1)} fusion(bf16[80,8,10,128]{3,2,1,0:T(8,128)(2,1)S(1)} %bitcast.233, bf16[80,8,5,128]{3,2,1,0:T(8,128)(2,1)S(1)} %bitcast.234), kind=kOutput, calls=%fused_computation.14 | convolution fusion | flops 1048576000 | bytes 5734400 | tf_op jit(solution)/shard_map/dot_general | solution.py:314
  102.7 0.9 convolution_convert_fusion.2
  103.6 0.5 convolution_convert_fusion.6
  104.1 1.5 %convolution_add_fusion.2 = f32[640,1280]{1,0:T(8,128)S(1)} fusion(f32[640,1280]{1,0:T(8,128)S(1)} %fusion.7, bf16[80,8,10,128]{3,2,1,0:T(8,128)(2,1)S(1)} %bitcast.228, bf16[80,8,5,128]{3,2,1,0:T(8,128)(2,1)S(1)} %bitcast.230), kind=kOutput, calls=%fused_computation.2 | convolution fusion | flops 1049395200 | bytes 9011200 | tf_op jit(solution)/shard_map/dot_general | solution.py:314
  105.6 0.7 bitcast_bitcast_fusion
  106.3 0.9 convolution_convert_fusion.1
  107.7 1.5 %convolution_add_fusion.1 = f32[640,1280]{1,0:T(8,128)S(1)} fusion(f32[640,1280]{1,0:T(8,128)S(1)} %convolution_add_fusion.2, bf16[80,8,10,128]{3,2,1,0:T(8,128)(2,1)S(1)} %bitcast.229, bf16[80,8,5,128]{3,2,1,0:T(8,128)(2,1)S(1)} %bitcast.231), kind=kOutput, calls=%fused_computation.1 | convolution fusion | flops 1049395200 | bytes 9011200 | tf_op jit(solution)/shard_map/dot_general | solution.py:314
  109.2 0.9 convolution_convert_fusion
  110.6 2.7 %fusion = bf16[640,1280]{1,0:T(8,128)(2,1)} fusion(f32[640,1280]{1,0:T(8,128)S(1)} %convolution_add_fusion.1, bf16[80,8,10,128]{3,2,1,0:T(8,128)(2,1)S(1)} %bitcast.232, bf16[80,8,5,128]{3,2,1,0:T(8,128)(2,1)S(1)} %bitcast.235), kind=kOutput, calls=%fused_computation.3 | convolution fusion | flops 1050214400 | bytes 7372800 | tf_op jit(solution)/shard_map/dot_general | solution.py:314
  113.3 1.2 %slice.171 = f32[1,1]{1,0:T(1,128)} slice(f32[8,128]{1,0:T(8,128)} %get-tuple-element.83), slice={[0:1], [0:1]} | slice | bytes 8 | tf_op jit(solution)/shard_map/slice | solution.py:315
  (24 shorter events, 2.2 us)
Async XLA Ops:
  6.1 0.6 copy-start.1
  96.2 2.6 %copy-start = (bf16[4,2,8,128,128]{4,3,2,1,0:T(8,128)(2,1)S(1)}, bf16[4,2,8,128,128]{4,3,2,1,0:T(8,128)(2,1)}, u32[]{:S(2)}) copy-start(bf16[4,2,8,128,128]{4,3,2,1,0:T(8,128)(2,1)} %get-tuple-element.82) | copy-start | bytes 6291460

commit v8 on v6

--- a/solution.py
+++ b/solution.py
@@ -26,8 +26,9 @@
     return dense.reshape(nrows * width, ncols * width).astype(pieces.dtype)
 
 
-def exchange_kernel(row_count, col_count, groups,
-                    blocks_ref, meta_ref, recv_l, recv_r, recv_ml, recv_mr, send_sem, recv_sem):
+def exchange_kernel(row_count, col_count, groups, blocks_ref, meta_ref, *refs):
+    recv_l, recv_r, recv_ml, recv_mr = (refs[i * STEPS:(i + 1) * STEPS] for i in range(4))
+    send_sem, recv_sem = refs[4 * STEPS:]
     r = lax.axis_index("row")
     c = lax.axis_index("col")
     a = r // groups
@@ -67,12 +68,12 @@
     pl.semaphore_wait(barrier, peers)
 
     sides = [
-        (left_plan, meta_ref, lambda s: recv_ml.at[s]),
-        (right_plan, meta_ref, lambda s: recv_mr.at[s]),
-        (left_plan, blocks_ref.at[b], lambda s: recv_l.at[s]),
+        (left_plan, meta_ref, lambda s: recv_ml[s]),
+        (right_plan, meta_ref, lambda s: recv_mr[s]),
+        (left_plan, blocks_ref.at[b], lambda s: recv_l[s]),
     ]
     for g in range(groups):
-        sides.append((right_plan, blocks_ref.at[g], lambda s, g=g: recv_r.at[s, g]))
+        sides.append((right_plan, blocks_ref.at[g], lambda s, g=g: recv_r[s].at[g]))
     kinds = len(sides)
 
     def transfer(plan, s, source, target, j):
@@ -144,13 +145,12 @@
     return pl.pallas_call(
         functools.partial(exchange_kernel, row_count, col_count, groups),
         out_shape=(
-            jax.ShapeDtypeStruct((STEPS, slots, width, width), blocks.dtype),
-            jax.ShapeDtypeStruct((STEPS, groups, slots, width, width), blocks.dtype),
-            jax.ShapeDtypeStruct((STEPS,) + meta.shape, meta.dtype),
-            jax.ShapeDtypeStruct((STEPS,) + meta.shape, meta.dtype),
+            [jax.ShapeDtypeStruct((slots, width, width), blocks.dtype)] * STEPS
+            + [jax.ShapeDtypeStruct((groups, slots, width, width), blocks.dtype)] * STEPS
+            + [jax.ShapeDtypeStruct(meta.shape, meta.dtype)] * (2 * STEPS)
         ),
         in_specs=[vmem, vmem],
-        out_specs=(vmem, vmem, vmem, vmem),
+        out_specs=[vmem] * (4 * STEPS),
         scratch_shapes=[
             pltpu.SemaphoreType.DMA(((3 + groups) * STEPS,)),
             pltpu.SemaphoreType.DMA(((3 + groups) * STEPS,)),
@@ -287,12 +287,13 @@
     meta = jnp.zeros((8, 128), jnp.int32)
     meta = meta.at[0, :slot_count].set(left_places)
     meta = meta.at[1, : groups * slot_count].set(right_places)
-    recv_l, recv_r, recv_ml, recv_mr = exchange(blocks[0, 0], meta, row_count, col_count)
+    received = exchange(blocks[0, 0], meta, row_count, col_count)
+    recv_l, recv_r, recv_ml, recv_mr = (received[i * STEPS:(i + 1) * STEPS] for i in range(4))
     totals = jnp.zeros((RB * width, groups * RB * width), jnp.float32)
     for step in range(STEPS):
         rp = recv_r[step].reshape(groups * slot_count, width, width)
-        right_dense = densify(rp, recv_mr[step, 1, : groups * slot_count], RB, groups * RB)
-        left_dense = densify(recv_l[step], recv_ml[step, 0, :slot_count], RB, RB)
+        right_dense = densify(rp, recv_mr[step][1, : groups * slot_count], RB, groups * RB)
+        left_dense = densify(recv_l[step], recv_ml[step][0, :slot_count], RB, RB)
         totals = totals + jnp.dot(left_dense, right_dense, preferred_element_type=jnp.float32)
     shift_amount = row_place - groups * col_place
     valid = (shift_amount >= 0) & (shift_amount < groups)

time: 114 us -> 116 us (1.018)
    eq x2 -> x4, local copies, waits for them, and re-layouts: 1.39 us -> 2.75 us  [densify(): places[None, :] == jnp.arange(nrows * ncols, dtype=jnp.int32)[:, None]]
    unnamed x8 -> x14, local copies, waits for them, and re-layouts: 3.69 us -> 3.28 us
where the time goes in v8:
time: 116 us
  Pallas kernels  87.8 us (76%)
  matrix products  13.6 us (12%)
  local copies, waits for them, and re-layouts  8.27 us (7%)
  between operations  3.27 us (3%)
  other arithmetic  2.92 us (3%)
    pallas_call x1, Pallas kernels, exchange(): pl.pallas_call(functools.partial(exchange_kernel, row_count, col_count, g...  49.9 us
    pallas_call x1, Pallas kernels, trace_total(): pl.pallas_call(functools.partial(trace_kernel, row_count, col_count, grou...  37.9 us
    dot_general x4, matrix products, body(): jnp.dot(left_dense, right_dense, preferred_element_type=jnp.float32)  7.15 us
    dot_general x8, matrix products, densify(): jnp.dot(onehot, pieces.reshape(count, width * width), preferred_element_t...  6.45 us
    unnamed x14, local copies, waits for them, and re-layouts  3.28 us
    eq x4, local copies, waits for them, and re-layouts, densify(): places[None, :] == jnp.arange(nrows * ncols, dtype=jnp.int32)[:, None]  2.75 us

profile of v8, /device:TPU:1, one launch (start us, length us, event | category | flops | bytes accessed | tf_op | source)
XLA Modules:
  0.0 115.8 jit_solution(5917835472520037141)
XLA Ops:
  0.6 0.8 bitcast_select_fusion
  1.4 0.7 iota_compare_fusion.1
  2.4 0.7 multiply_add_fusion.2
  3.3 0.6 copy-done.5
  3.9 49.9 %shard_map.59 = (bf16[8,128,128]{2,1,0:T(8,128)(2,1)}, bf16[8,128,128]{2,1,0:T(8,128)(2,1)}, bf16[8,128,128]{2,1,0:T(8,128)(2,1)}, bf16[8,128,128]{2,1,0:T(8,128...) custom-call(bf16[2,8,128,128]{3,2,1,0:T(8,128)(2,1)} %bitcast.217, ...), custom_call_target="tpu_custom_call" | custom-call | tf_op jit(solution)/shard_map/pallas_call | solution.py:145
  53.8 0.7 slice_bitcast_fusion.5
  54.5 1.5 %convolution_convert_fusion.7 = bf16[5,5,128,128]{3,1,2,0:T(8,128)(2,1)S(1)} fusion(bf16[1,8,128,128]{3,2,1,0:T(8,128)(2,1)} %bitcast.221, s32[5,5]{1,0:T(8,128)S(1)} %multiply_add_fusion.1, s32[8]{0:T(128)S(1)} %get-tuple-element.71), kind=kOutput, calls=%fused_computation.21 | convolution fusion | flops 6963400 | bytes 1081476 | tf_op jit(solution)/shard_map/dot_general | solution.py:22
  56.0 0.7 slice_bitcast_fusion.4
  56.7 1.9 %bitcast_bitcast_fusion.2 = (bf16[2,128,8,128]{3,2,1,0:T(8,128)(2,1)S(1)}, bf16[2,128,8,128]{3,2,1,0:T(8,128)(2,1)S(1)}) fusion(bf16[2,8,128,128]{3,2,1,0:T(8,128)(2,1)} %get-tuple-element.49, bf16[2,8,128,128]{3,2,1,0:T(8,128)(2,1)} %get-tuple-element.45), kind=kLoop, calls=%fused_computation.32 | loop fusion | bytes 2097152
  58.5 0.9 convolution_convert_fusion.3
  59.4 1.5 %fusion.6 = f32[640,1280]{1,0:T(8,128)S(1)} fusion(bf16[80,8,10,128]{3,2,1,0:T(8,128)(2,1)S(1)} %bitcast.215, bf16[80,8,5,128]{3,2,1,0:T(8,128)(2,1)S(1)} %bitcast.216), kind=kOutput, calls=%fused_computation.13 | convolution fusion | flops 1048576000 | bytes 5734400 | tf_op jit(solution)/shard_map/dot_general | solution.py:297
  60.9 0.9 convolution_convert_fusion.2
  62.4 1.5 %convolution_add_fusion.2 = f32[640,1280]{1,0:T(8,128)S(1)} fusion(f32[640,1280]{1,0:T(8,128)S(1)} %fusion.6, bf16[80,8,10,128]{3,2,1,0:T(8,128)(2,1)S(1)} %bitcast.211, bf16[80,8,5,128]{3,2,1,0:T(8,128)(2,1)S(1)} %bitcast.212), kind=kOutput, calls=%fused_computation.2 | convolution fusion | flops 1049395200 | bytes 9011200 | tf_op jit(solution)/shard_map/dot_general | solution.py:297
  63.9 0.7 bitcast_bitcast_fusion
  64.6 0.7 slice_bitcast_fusion
  65.3 0.9 convolution_convert_fusion.1
  66.2 0.7 slice_bitcast_fusion.1
  67.4 1.5 %convolution_add_fusion.1 = f32[640,1280]{1,0:T(8,128)S(1)} fusion(f32[640,1280]{1,0:T(8,128)S(1)} %convolution_add_fusion.2, bf16[80,8,10,128]{3,2,1,0:T(8,128)(2,1)S(1)} %bitcast.210, bf16[80,8,5,128]{3,2,1,0:T(8,128)(2,1)S(1)} %bitcast.213), kind=kOutput, calls=%fused_computation.1 | convolution fusion | flops 1049395200 | bytes 9011200 | tf_op jit(solution)/shard_map/dot_general | solution.py:297
  68.9 0.9 convolution_convert_fusion
  70.4 2.7 %fusion.57 = (bf16[640,1280]{1,0:T(8,128)(2,1)}, f32[640,1280]{1,0:T(8,128)S(1)}) fusion(f32[640,1280]{1,0:T(8,128)S(1)} %convolution_add_fusion.1, bf16[80,8,10,128]{3,2,1,0:T(8,128)(2,1)S(1)} %bitcast.209, bf16[80,8,5,128]{3,2,1,0:T(8,128)(2,1)S(1)} %bitcast.214), kind=kOutput, calls=%fused_computation.98 | convolution fusion | flops 1050214400 | bytes 10649600 | tf_op jit(solution)/shard_map/dot_general | solution.py:297
  73.0 0.7 select_reduce_fusion
  74.4 0.6 broadcast_in_dim.28.term_ref
  75.0 37.9 %shard_map.60 = f32[8,128]{1,0:T(8,128)} custom-call(f32[8,128]{1,0:T(8,128)} %broadcast_in_dim.28.term_ref), custom_call_target="tpu_custom_call" | custom-call | tf_op jit(solution)/shard_map/pallas_call | solution.py:252
  112.8 1.2 %slice.70 = f32[1,1]{1,0:T(1,128)} slice(f32[8,128]{1,0:T(8,128)} %shard_map.60), slice={[0:1], [0:1]} | slice | bytes 8 | tf_op jit(solution)/shard_map/slice | solution.py:267
  (25 shorter events, 2.1 us)
Async XLA Ops:
  3.3 0.6 copy-start.5
  60.9 1.0 copy-start.4
  62.4 1.5 %copy-start = (bf16[2,8,128,128]{3,2,1,0:T(8,128)(2,1)S(1)}, bf16[2,8,128,128]{3,2,1,0:T(8,128)(2,1)}, u32[]{:S(2)}) copy-start(bf16[2,8,128,128]{3,2,1,0:T(8,128)(2,1)} %get-tuple-element.53) | copy-start | bytes 1572868
  62.4 1.5 %copy-start.1 = (bf16[2,8,128,128]{3,2,1,0:T(8,128)(2,1)S(1)}, bf16[2,8,128,128]{3,2,1,0:T(8,128)(2,1)}, u32[]{:S(2)}) copy-start(bf16[2,8,128,128]{3,2,1,0:T(8,128)(2,1)} %get-tuple-element.57) | copy-start | bytes 1572868
  63.9 3.0 %copy-start.3 = (bf16[8,128,128]{2,1,0:T(8,128)(2,1)S(1)}, bf16[8,128,128]{2,1,0:T(8,128)(2,1)}, u32[]{:S(2)}) copy-start(bf16[8,128,128]{2,1,0:T(8,128)(2,1)} %get-tuple-element.51) | copy-start | bytes 786436
  68.9 1.0 copy-start.2

commit v9 on v6

--- a/solution.py
+++ b/solution.py
@@ -288,12 +288,26 @@
     meta = meta.at[0, :slot_count].set(left_places)
     meta = meta.at[1, : groups * slot_count].set(right_places)
     recv_l, recv_r, recv_ml, recv_mr = exchange(blocks[0, 0], meta, row_count, col_count)
-    totals = jnp.zeros((RB * width, groups * RB * width), jnp.float32)
-    for step in range(STEPS):
-        rp = recv_r[step].reshape(groups * slot_count, width, width)
-        right_dense = densify(rp, recv_mr[step, 1, : groups * slot_count], RB, groups * RB)
-        left_dense = densify(recv_l[step], recv_ml[step, 0, :slot_count], RB, RB)
-        totals = totals + jnp.dot(left_dense, right_dense, preferred_element_type=jnp.float32)
+    cells = jnp.arange(RB * RB, dtype=jnp.int32)
+    left_hot = (recv_ml[:, 0, None, :slot_count] == cells[None, :, None]).astype(blocks.dtype)
+    left_dense = jnp.einsum(
+        "sct,stk->sck", left_hot, recv_l.reshape(STEPS, slot_count, width * width),
+        preferred_element_type=jnp.float32,
+    ).astype(blocks.dtype)
+    left_dense = left_dense.reshape(STEPS, RB, RB, width, width).transpose(1, 3, 0, 2, 4)
+    left_dense = left_dense.reshape(RB * width, STEPS * RB * width)
+    cells = jnp.arange(RB * groups * RB, dtype=jnp.int32)
+    right_hot = (
+        recv_mr[:, 1, None, : groups * slot_count] == cells[None, :, None]
+    ).astype(blocks.dtype)
+    right_dense = jnp.einsum(
+        "sct,stk->sck", right_hot,
+        recv_r.reshape(STEPS, groups * slot_count, width * width),
+        preferred_element_type=jnp.float32,
+    ).astype(blocks.dtype)
+    right_dense = right_dense.reshape(STEPS, RB, groups * RB, width, width).transpose(0, 1, 3, 2, 4)
+    right_dense = right_dense.reshape(STEPS * RB * width, groups * RB * width)
+    totals = jnp.dot(left_dense, right_dense, preferred_element_type=jnp.float32)
     shift_amount = row_place - groups * col_place
     valid = (shift_amount >= 0) & (shift_amount < groups)
     start = jnp.clip(shift_amount, 0, groups - 1) * RB * width

time: 114 us -> 158 us (1.39)
  local copies, waits for them, and re-layouts: 7.33 us -> 43.8 us
  matrix products: 12.7 us -> 18.4 us
    reshape x0 -> x5, local copies, waits for them, and re-layouts: none -> 21.9 us  [the longest x1 7.81 us: body(): right_dense.reshape(STEPS, RB, groups * RB, width, width)]
    transpose x0 -> x2, local copies, waits for them, and re-layouts: none -> 17.7 us  [the longest x1 12.9 us: body(): right_dense.reshape(STEPS, RB, groups * RB, width, width)]
    unnamed x8 -> x4, local copies, waits for them, and re-layouts: 3.69 us -> 0.59 us
    dot_general x8 -> x2, matrix products: 5.52 us -> 8.55 us  [the longest x1 5.13 us: body(): jnp.einsum('sct,stk->sck', right_hot, recv_r.reshape(STEPS, groups * slot...]
    dot_general x4 -> x1, matrix products: 7.14 us -> 9.82 us  [body(): jnp.dot(left_dense, right_dense, preferred_element_type=jnp.float32)]
where the time goes in v9:
time: 158 us; the launch traced here: 157 us
  Pallas kernels  87.8 us (56%)
  local copies, waits for them, and re-layouts  43.8 us (28%)
  matrix products  18.4 us (12%)
  other arithmetic  4.33 us (3%)
  between operations  3.15 us (2%)
    pallas_call x1, Pallas kernels, exchange(): pl.pallas_call(functools.partial(exchange_kernel, row_count, col_count, g...  49.9 us
    pallas_call x1, Pallas kernels, trace_total(): pl.pallas_call(functools.partial(trace_kernel, row_count, col_count, grou...  37.9 us
    transpose x1, local copies, waits for them, and re-layouts, body(): right_dense.reshape(STEPS, RB, groups * RB, width, width)  12.9 us
    dot_general x1, matrix products, body(): jnp.dot(left_dense, right_dense, preferred_element_type=jnp.float32)  9.82 us
    reshape x1, local copies, waits for them, and re-layouts, body(): right_dense.reshape(STEPS, RB, groups * RB, width, width)  7.81 us
    reshape x1, local copies, waits for them, and re-layouts, body(): left_dense = left_dense.reshape(RB * width, STEPS * RB * width)  6.81 us
    dot_general x1, matrix products, body(): jnp.einsum('sct,stk->sck', right_hot, recv_r.reshape(STEPS, groups * slot...  5.13 us
    transpose x1, local copies, waits for them, and re-layouts, body(): left_dense.reshape(STEPS, RB, RB, width, width).transpose(1, 3, 0, 2, 4)  4.74 us

profile of v9, /device:TPU:1, one launch (start us, length us, event | category | flops | bytes accessed | tf_op | source)
XLA Modules:
  0.0 157.5 jit_solution(1485791081796153365)
XLA Ops:
  0.6 0.8 bitcast_select_fusion
  1.4 0.7 iota_compare_fusion.5
  2.2 0.1 lt.47
  2.3 0.1 add.60
  2.4 0.7 multiply_add_fusion
  3.2 0.1 scatter.9.meta_ref
  3.3 0.6 copy-done.1
  3.9 49.9 %shard_map.59 = (bf16[4,8,128,128]{3,2,1,0:T(8,128)(2,1)}, bf16[4,2,8,128,128]{4,3,2,1,0:T(8,128)(2,1)}, s32[4,8,128]{2,1,0:T(8,128)}, s32[4,8,128]{2,1,0:T(8,128)}) custom-call(bf16[2,8,128,128]{3,2,1,0:T(8,128)(2,1)} %bitcast.28, s32[8,128]{1,0:T(8,128)} %copy-done.1), custom_call_target="tpu_custom_call" | custom-call | tf_op jit(solution)/shard_map/pallas_call | solution.py:144
  53.8 2.8 %reshape.152 = bf16[4,16,16384]{2,1,0:T(8,128)(2,1)S(1)} reshape(bf16[4,2,8,128,128]{4,3,2,1,0:T(8,128)(2,1)} %get-tuple-element.33) | data formatting | bytes 4194304 | tf_op jit(solution)/shard_map/reshape | solution.py:305
  56.7 0.7 slice.45
  57.4 5.1 %convolution_convert_fusion = bf16[4,50,16384]{2,1,0:T(8,128)(2,1)} fusion(bf16[4,16,16384]{2,1,0:T(8,128)(2,1)S(1)} %reshape.152, s32[4,16]{1,0:T(4,128)S(1)} %bitcast.29), kind=kOutput, calls=%fused_computation | convolution fusion | flops 108137600 | bytes 8651008 | tf_op jit(solution)/shard_map/sct,stk->sck/dot_general | solution.py:303
  62.5 7.8 %reshape.156 = bf16[4,5,10,128,128]{4,3,2,1,0:T(8,128)(2,1)} reshape(bf16[4,50,16384]{2,1,0:T(8,128)(2,1)} %convolution_convert_fusion) | data formatting | bytes 13107200 | tf_op jit(solution)/shard_map/reshape | solution.py:308
  70.3 12.9 %copy.9 = bf16[4,5,128,10,128]{4,3,2,1,0:T(8,128)(2,1)} copy(bf16[4,5,128,10,128]{4,2,3,1,0:T(8,128)(2,1)} %bitcast.25) | data formatting | bytes 13107200 | tf_op jit(solution)/shard_map/transpose | solution.py:308
  83.3 0.5 reshape.149
  83.8 0.7 slice.44
  84.5 3.4 %convolution_convert_fusion.1 = bf16[4,25,16384]{2,1,0:T(8,128)(2,1)} fusion(bf16[4,8,16384]{2,1,0:T(8,128)(2,1)S(1)} %reshape.149, s32[4,8]{1,0:T(4,128)S(1)} %bitcast.30), kind=kOutput, calls=%fused_computation.1 | convolution fusion | flops 27853600 | bytes 4325504 | tf_op jit(solution)/shard_map/sct,stk->sck/dot_general | solution.py:293
  87.9 4.0 %reshape.155 = bf16[4,5,5,128,128]{4,3,2,1,0:T(8,128)(2,1)S(1)} reshape(bf16[4,25,16384]{2,1,0:T(8,128)(2,1)} %convolution_convert_fusion.1) | data formatting | bytes 6553600 | tf_op jit(solution)/shard_map/reshape | solution.py:297
  91.9 4.7 %copy.7 = bf16[5,128,4,5,128]{4,3,2,1,0:T(8,128)(2,1)} copy(bf16[5,128,4,5,128]{4,1,3,0,2:T(8,128)(2,1)S(1)} %bitcast.26) | data formatting | bytes 6553600 | tf_op jit(solution)/shard_map/transpose | solution.py:297
  96.6 6.8 %reshape.151 = bf16[640,2560]{1,0:T(8,128)(2,1)S(1)} reshape(bf16[5,128,4,5,128]{4,3,2,1,0:T(8,128)(2,1)} %copy.7) | data formatting | bytes 6553600 | tf_op jit(solution)/shard_map/reshape | solution.py:298
  103.4 9.8 %fusion.5 = (bf16[640,1280]{1,0:T(8,128)(2,1)}, f32[640,1280]{1,0:T(8,128)}) fusion(bf16[640,2560]{1,0:T(8,128)(2,1)S(1)} %reshape.151, bf16[320,8,10,128]{3,2,1,0:T(8,128)(2,1)} %bitcast.27), kind=kOutput, calls=%fused_computation.17 | convolution fusion | flops 4195123200 | bytes 14745600 | tf_op jit(solution)/shard_map/dot_general | solution.py:310
  113.3 2.1 %select_reduce_fusion = f32[]{:T(128)} fusion(f32[640,1280]{1,0:T(8,128)} %get-tuple-element.35, s32[]{:T(128)S(6)} %select_n.35), kind=kLoop, calls=%fused_computation.5 | loop fusion | flops 1228799 | bytes 1638408 | tf_op jit(solution)/shard_map/jit(trace)/reduce_sum | solution.py:315
  116.0 0.6 broadcast_in_dim.22.term_ref
  116.6 37.9 %shard_map.60 = f32[8,128]{1,0:T(8,128)} custom-call(f32[8,128]{1,0:T(8,128)} %broadcast_in_dim.22.term_ref), custom_call_target="tpu_custom_call" | custom-call | tf_op jit(solution)/shard_map/pallas_call | solution.py:252
  154.5 1.2 slice.46
  (9 shorter events, 0.2 us)
Async XLA Ops:
  3.3 0.6 copy-start.1
  70.3 12.9 %copy-start = (bf16[4,8,128,128]{3,2,1,0:T(8,128)(2,1)S(1)}, bf16[4,8,128,128]{3,2,1,0:T(8,128)(2,1)}, u32[]{:S(2)}) copy-start(bf16[4,8,128,128]{3,2,1,0:T(8,128)(2,1)} %get-tuple-element.31) | copy-start | bytes 3145732

commit v10 on v6

--- a/solution.py
+++ b/solution.py
@@ -32,6 +32,7 @@
     c = lax.axis_index("col")
     a = r // groups
     b = r % groups
+    slots_per_group = blocks_ref.shape[1]
 
     def l_self(s):
         return (a + s) % col_count == 0
@@ -66,13 +67,19 @@
             peers = peers + jnp.where(is_self, 0, 2)
     pl.semaphore_wait(barrier, peers)
 
+    half = slots_per_group // 2
     sides = [
         (left_plan, meta_ref, lambda s: recv_ml.at[s]),
         (right_plan, meta_ref, lambda s: recv_mr.at[s]),
-        (left_plan, blocks_ref.at[b], lambda s: recv_l.at[s]),
     ]
+    for h in range(2):
+        part = pl.ds(h * half, half)
+        sides.append((left_plan, blocks_ref.at[b, part], lambda s, part=part: recv_l.at[s, part]))
     for g in range(groups):
-        sides.append((right_plan, blocks_ref.at[g], lambda s, g=g: recv_r.at[s, g]))
+        for h in range(2):
+            part = pl.ds(h * half, half)
+            sides.append((right_plan, blocks_ref.at[g, part],
+                          lambda s, g=g, part=part: recv_r.at[s, g, part]))
     kinds = len(sides)
 
     def transfer(plan, s, source, target, j):
@@ -152,8 +159,8 @@
         in_specs=[vmem, vmem],
         out_specs=(vmem, vmem, vmem, vmem),
         scratch_shapes=[
-            pltpu.SemaphoreType.DMA(((3 + groups) * STEPS,)),
-            pltpu.SemaphoreType.DMA(((3 + groups) * STEPS,)),
+            pltpu.SemaphoreType.DMA(((4 + 2 * groups) * STEPS,)),
+            pltpu.SemaphoreType.DMA(((4 + 2 * groups) * STEPS,)),
         ],
         compiler_params=pltpu.CompilerParams(collective_id=0, has_side_effects=True),
     )(blocks, meta)

time: 114 us -> 115 us (level)
  no operation moved by 1% of the time
where the time goes in v10:
time: 115 us; the launch traced here: 114 us
  Pallas kernels  88 us (77%)
  matrix products  12.7 us (11%)
  local copies, waits for them, and re-layouts  7.33 us (6%)
  between operations  3.24 us (3%)
  other arithmetic  2.92 us (3%)
    pallas_call x1, Pallas kernels, exchange(): pl.pallas_call(functools.partial(exchange_kernel, row_count, col_count, g...  50.1 us
    pallas_call x1, Pallas kernels, trace_total(): pl.pallas_call(functools.partial(trace_kernel, row_count, col_count, grou...  37.9 us
    dot_general x4, matrix products, body(): jnp.dot(left_dense, right_dense, preferred_element_type=jnp.float32)  7.15 us
    dot_general x8, matrix products, densify(): jnp.dot(onehot, pieces.reshape(count, width * width), preferred_element_t...  5.51 us
    unnamed x8, local copies, waits for them, and re-layouts  3.69 us

profile of v10, /device:TPU:1, one launch (start us, length us, event | category | flops | bytes accessed | tf_op | source)
XLA Modules:
  0.0 114.1 jit_solution(266694292989037724)
XLA Ops:
  0.6 0.8 bitcast_select_fusion
  1.4 0.7 iota_compare_fusion.1
  2.4 0.7 multiply_add_fusion.2
  3.3 0.6 copy-done.1
  3.9 50.1 %shard_map.59 = (bf16[4,8,128,128]{3,2,1,0:T(8,128)(2,1)}, bf16[4,2,8,128,128]{4,3,2,1,0:T(8,128)(2,1)}, s32[4,8,128]{2,1,0:T(8,128)}, s32[4,8,128]{2,1,0:T(8,128)}) custom-call(bf16[2,8,128,128]{3,2,1,0:T(8,128)(2,1)} %bitcast.229, s32[8,128]{1,0:T(8,128)} %copy-done.1), custom_call_target="tpu_custom_call" | custom-call | tf_op jit(solution)/shard_map/pallas_call | solution.py:151
  54.0 1.7 %slice_bitcast_fusion = (bf16[2,8,128,128]{3,2,1,0:T(8,128)(2,1)S(1)}, bf16[2,8,128,128]{3,2,1,0:T(8,128)(2,1)S(1)}, bf16[2,8,128,128]{3,2,1,0:T(8,128)(2,1)S(1)}, bf16[2,8,128,128]{3,2,1,0:T(8,128)(2,1)S(1)}) fusion(bf16[4,2,8,128,128]{4,3,2,1,0:T(8,128)(2,1)} %get-tuple-element.33), kind=kLoop, calls=%fused_computation.42 | loop fusion | bytes 4194304
  55.7 0.7 bitcast_bitcast_fusion.2
  56.4 0.7 slice_bitcast_fusion.8
  57.1 0.9 convolution_convert_fusion.3
  58.1 0.7 slice_bitcast_fusion.9
  58.8 0.5 convolution_convert_fusion.7
  59.3 1.5 %fusion.6 = f32[640,1280]{1,0:T(8,128)S(1)} fusion(bf16[80,8,10,128]{3,2,1,0:T(8,128)(2,1)S(1)} %bitcast.227, bf16[80,8,5,128]{3,2,1,0:T(8,128)(2,1)S(1)} %bitcast.228), kind=kOutput, calls=%fused_computation.13 | convolution fusion | flops 1048576000 | bytes 5734400 | tf_op jit(solution)/shard_map/dot_general | solution.py:303
  60.8 0.9 convolution_convert_fusion.2
  61.7 0.5 convolution_convert_fusion.6
  62.2 1.5 %convolution_add_fusion.2 = f32[640,1280]{1,0:T(8,128)S(1)} fusion(f32[640,1280]{1,0:T(8,128)S(1)} %fusion.6, bf16[80,8,10,128]{3,2,1,0:T(8,128)(2,1)S(1)} %bitcast.222, bf16[80,8,5,128]{3,2,1,0:T(8,128)(2,1)S(1)} %bitcast.224), kind=kOutput, calls=%fused_computation.2 | convolution fusion | flops 1049395200 | bytes 9011200 | tf_op jit(solution)/shard_map/dot_general | solution.py:303
  63.7 0.7 bitcast_bitcast_fusion
  64.4 0.9 convolution_convert_fusion.1
  65.7 1.5 %convolution_add_fusion.1 = f32[640,1280]{1,0:T(8,128)S(1)} fusion(f32[640,1280]{1,0:T(8,128)S(1)} %convolution_add_fusion.2, bf16[80,8,10,128]{3,2,1,0:T(8,128)(2,1)S(1)} %bitcast.223, bf16[80,8,5,128]{3,2,1,0:T(8,128)(2,1)S(1)} %bitcast.225), kind=kOutput, calls=%fused_computation.1 | convolution fusion | flops 1049395200 | bytes 9011200 | tf_op jit(solution)/shard_map/dot_general | solution.py:303
  67.3 0.9 convolution_convert_fusion
  68.7 2.7 %fusion.57 = (bf16[640,1280]{1,0:T(8,128)(2,1)}, f32[640,1280]{1,0:T(8,128)S(1)}) fusion(f32[640,1280]{1,0:T(8,128)S(1)} %convolution_add_fusion.1, bf16[80,8,10,128]{3,2,1,0:T(8,128)(2,1)S(1)} %bitcast.221, bf16[80,8,5,128]{3,2,1,0:T(8,128)(2,1)S(1)} %bitcast.226), kind=kOutput, calls=%fused_computation.106 | convolution fusion | flops 1050214400 | bytes 10649600 | tf_op jit(solution)/shard_map/dot_general | solution.py:303
  71.3 0.7 select_reduce_fusion
  72.7 0.6 broadcast_in_dim.28.term_ref
  73.3 37.9 %shard_map.60 = f32[8,128]{1,0:T(8,128)} custom-call(f32[8,128]{1,0:T(8,128)} %broadcast_in_dim.28.term_ref), custom_call_target="tpu_custom_call" | custom-call | tf_op jit(solution)/shard_map/pallas_call | solution.py:259
  111.1 1.2 %slice.102 = f32[1,1]{1,0:T(1,128)} slice(f32[8,128]{1,0:T(8,128)} %shard_map.60), slice={[0:1], [0:1]} | slice | bytes 8 | tf_op jit(solution)/shard_map/slice | solution.py:274
  (17 shorter events, 1.6 us)
Async XLA Ops:
  3.3 0.6 copy-start.1
  55.7 2.3 %copy-start = (bf16[4,8,128,128]{3,2,1,0:T(8,128)(2,1)S(1)}, bf16[4,8,128,128]{3,2,1,0:T(8,128)(2,1)}, u32[]{:S(2)}) copy-start(bf16[4,8,128,128]{3,2,1,0:T(8,128)(2,1)} %get-tuple-element.31) | copy-start | bytes 3145732

commit v11 on v6

--- a/solution.py
+++ b/solution.py
@@ -159,8 +159,11 @@
     )(blocks, meta)
 
 
-def trace_kernel(row_count, col_count, groups,
-                 term_ref, out_ref, row_buf, col_buf, send_sem, recv_sem, col_send, col_recv):
+def trace_kernel(row_count, col_count, groups, *refs):
+    lefts = refs[:STEPS]
+    rights = refs[STEPS:2 * STEPS]
+    (square_ref, out_ref, term_ref, acc, row_buf, col_buf,
+     send_sem, recv_sem, col_send, col_recv) = refs[2 * STEPS:]
     r = lax.axis_index("row")
     c = lax.axis_index("col")
     diagonal = c == r // groups
@@ -181,6 +184,24 @@
         @pl.when(rr != r)
         def _(rr=rr):
             pl.semaphore_signal(barrier, 1, device_id=(rr, c), device_id_type=MESH)
+
+    rows = lefts[0].shape[0]
+    cols = rights[0].shape[1]
+    tile = 256 if cols % 256 == 0 else cols
+    acc[...] = jnp.zeros(acc.shape, jnp.float32)
+    for s in range(STEPS):
+        @pl.loop(0, cols // tile)
+        def _(j, s=s):
+            span = pl.ds(pl.multiple_of(j * tile, tile), tile)
+            acc[:, span] += jnp.dot(
+                lefts[s][...], rights[s][:, span], preferred_element_type=jnp.float32)
+    square_ref[...] = acc[...].astype(square_ref.dtype)
+    shift = jnp.clip(r - groups * c, 0, groups - 1)
+    window = acc[:, pl.ds(pl.multiple_of(shift * rows, 128), rows)]
+    eye = (lax.broadcasted_iota(jnp.int32, (rows, rows), 0)
+           == lax.broadcasted_iota(jnp.int32, (rows, rows), 1))
+    term = jnp.sum(jnp.where(eye, window, 0.0), keepdims=True)
+    term_ref[...] = jnp.broadcast_to(jnp.where(diagonal, term, 0.0), term_ref.shape)
 
     pl.semaphore_wait(barrier, (row_count - 1) + jnp.where(diagonal, col_count - 1, 1))
 
@@ -246,15 +267,20 @@
     out_ref[...] = total
 
 
-def trace_total(term, row_count, col_count, groups):
-    tile = jnp.broadcast_to(term, (8, 128))
+def finish(lefts, rights, row_count, col_count, groups):
+    rows, cols = lefts[0].shape[0], rights[0].shape[1]
     vmem = pl.BlockSpec(memory_space=pltpu.VMEM)
-    out = pl.pallas_call(
+    square, total = pl.pallas_call(
         functools.partial(trace_kernel, row_count, col_count, groups),
-        out_shape=jax.ShapeDtypeStruct((8, 128), jnp.float32),
-        in_specs=[vmem],
-        out_specs=vmem,
+        out_shape=(
+            jax.ShapeDtypeStruct((rows, cols), lefts[0].dtype),
+            jax.ShapeDtypeStruct((8, 128), jnp.float32),
+        ),
+        in_specs=[vmem] * (2 * STEPS),
+        out_specs=(vmem, vmem),
         scratch_shapes=[
+            pltpu.VMEM((8, 128), jnp.float32),
+            pltpu.VMEM((rows, cols), jnp.float32),
             pltpu.VMEM((8, 128), jnp.float32),
             pltpu.VMEM((row_count, 8, 128), jnp.float32),
             pltpu.SemaphoreType.DMA((col_count,)),
@@ -263,8 +289,8 @@
             pltpu.SemaphoreType.DMA((row_count,)),
         ],
         compiler_params=pltpu.CompilerParams(collective_id=1, has_side_effects=True),
-    )(tile)
-    return out[0, 0]
+    )(*lefts, *rights)
+    return square, total[0, 0]
 
 
 def body(blocks, block_rows, block_cols, counts):
@@ -288,20 +314,14 @@
     meta = meta.at[0, :slot_count].set(left_places)
     meta = meta.at[1, : groups * slot_count].set(right_places)
     recv_l, recv_r, recv_ml, recv_mr = exchange(blocks[0, 0], meta, row_count, col_count)
-    totals = jnp.zeros((RB * width, groups * RB * width), jnp.float32)
+    lefts, rights = [], []
     for step in range(STEPS):
         rp = recv_r[step].reshape(groups * slot_count, width, width)
-        right_dense = densify(rp, recv_mr[step, 1, : groups * slot_count], RB, groups * RB)
-        left_dense = densify(recv_l[step], recv_ml[step, 0, :slot_count], RB, RB)
-        totals = totals + jnp.dot(left_dense, right_dense, preferred_element_type=jnp.float32)
-    shift_amount = row_place - groups * col_place
-    valid = (shift_amount >= 0) & (shift_amount < groups)
-    start = jnp.clip(shift_amount, 0, groups - 1) * RB * width
-    window = lax.dynamic_slice_in_dim(totals, start, RB * width, 1)
-    term = jnp.where(valid, jnp.trace(window), jnp.zeros((), jnp.float32))
-    overall = trace_total(term, row_count, col_count, groups)
+        rights.append(densify(rp, recv_mr[step, 1, : groups * slot_count], RB, groups * RB))
+        lefts.append(densify(recv_l[step], recv_ml[step, 0, :slot_count], RB, RB))
+    square, overall = finish(lefts, rights, row_count, col_count, groups)
     trace_value = overall / math.sqrt(row_count * RB * width)
-    return (totals.astype(jnp.bfloat16), trace_value)
+    return (square, trace_value)
 
 
 def solution(mesh):

time: 114 us -> 128 us (1.12)
  local copies, waits for them, and re-layouts: 7.33 us -> 19.3 us
  Pallas kernels: 87.8 us -> 97.7 us
  matrix products: 12.7 us -> 5.51 us
    pallas_call x1, Pallas kernels: 37.9 us -> 47.8 us  [finish(): pl.pallas_call(functools.partial(trace_kernel, row_count, col_count, grou...]
    unnamed x8 -> x13, local copies, waits for them, and re-layouts: 3.69 us -> 13.1 us
    dot_general x4 -> x0, matrix products: 7.14 us -> none  [body(): jnp.dot(left_dense, right_dense, preferred_element_type=jnp.float32)]
    convert_element_type x0 -> x2, local copies, waits for them, and re-layouts: none -> 3.18 us  [densify(): return dense.reshape(nrows * width, ncols * width).astype(pieces.dtype)]
where the time goes in v11:
time: 128 us; the launch traced here: 127 us
  Pallas kernels  97.7 us (76%)
  local copies, waits for them, and re-layouts  19.3 us (15%)
  matrix products  5.51 us (4%)
  between operations  2.57 us (2%)
  other arithmetic  2.22 us (2%)
    pallas_call x1, Pallas kernels, exchange(): pl.pallas_call(functools.partial(exchange_kernel, row_count, col_count, g...  49.9 us
    pallas_call x1, Pallas kernels, finish(): pl.pallas_call(functools.partial(trace_kernel, row_count, col_count, grou...  47.8 us
    unnamed x13, local copies, waits for them, and re-layouts  13.1 us
    dot_general x8, matrix products, densify(): jnp.dot(onehot, pieces.reshape(count, width * width), preferred_element_t...  5.51 us
    convert_element_type x2, local copies, waits for them, and re-layouts, densify(): return dense.reshape(nrows * width, ncols * width).astype(pieces.dtype)  3.18 us

profile of v11, /device:TPU:1, one launch (start us, length us, event | category | flops | bytes accessed | tf_op | source)
XLA Modules:
  0.0 127.3 jit_solution(4850181210725775030)
XLA Ops:
  0.6 0.7 iota_compare_fusion
  1.6 0.8 bitcast_select_fusion
  2.4 0.7 multiply_add_fusion.2
  3.4 0.6 copy-done.1
  4.0 49.9 %shard_map.59 = (bf16[4,8,128,128]{3,2,1,0:T(8,128)(2,1)}, bf16[4,2,8,128,128]{4,3,2,1,0:T(8,128)(2,1)}, s32[4,8,128]{2,1,0:T(8,128)}, s32[4,8,128]{2,1,0:T(8,128)}) custom-call(bf16[2,8,128,128]{3,2,1,0:T(8,128)(2,1)} %bitcast.225, s32[8,128]{1,0:T(8,128)} %copy-done.1), custom_call_target="tpu_custom_call" | custom-call | tf_op jit(solution)/shard_map/pallas_call | solution.py:144
  53.9 0.7 slice_bitcast_fusion.12
  54.6 0.7 slice_bitcast_fusion.8
  55.3 1.3 slice_bitcast_fusion.4
  57.5 1.6 %copy_bitcast_fusion.4 = (bf16[640,640]{1,0:T(8,128)(2,1)}, bf16[640,640]{1,0:T(8,128)(2,1)}) fusion(bf16[80,8,5,128]{3,2,1,0:T(8,128)(2,1)S(1)} %bitcast.222, bf16[80,8,5,128]{3,2,1,0:T(8,128)(2,1)S(1)} %bitcast.224), kind=kLoop, calls=%fused_computation.12 | loop fusion | bytes 3276800 | tf_op jit(solution)/shard_map/convert_element_type | solution.py:26
  60.2 1.5 %copy_bitcast_fusion.6 = (bf16[640,640]{1,0:T(8,128)(2,1)}, bf16[640,640]{1,0:T(8,128)(2,1)}) fusion(bf16[80,8,5,128]{3,2,1,0:T(8,128)(2,1)S(1)} %bitcast.221, bf16[80,8,5,128]{3,2,1,0:T(8,128)(2,1)S(1)} %bitcast.223), kind=kLoop, calls=%fused_computation.14 | loop fusion | bytes 3276800 | tf_op jit(solution)/shard_map/convert_element_type | solution.py:26
  61.7 0.6 copy-done
  62.5 0.7 bitcast_bitcast_fusion
  63.2 0.7 bitcast_bitcast_fusion.2
  63.9 0.9 convolution_convert_fusion.2
  64.8 1.6 %copy.84 = bf16[80,8,10,128]{3,1,2,0:T(8,128)(2,1)} copy(bf16[80,8,10,128]{3,2,1,0:T(8,128)(2,1)S(1)} %bitcast.214) | data formatting | bytes 3276800
  66.4 0.9 convolution_convert_fusion
  67.3 1.6 %copy.82 = bf16[80,8,10,128]{3,1,2,0:T(8,128)(2,1)} copy(bf16[80,8,10,128]{3,2,1,0:T(8,128)(2,1)S(1)} %bitcast.215) | data formatting | bytes 3276800
  68.9 0.9 convolution_convert_fusion.3
  69.8 1.6 %copy.85 = bf16[80,8,10,128]{3,1,2,0:T(8,128)(2,1)} copy(bf16[80,8,10,128]{3,2,1,0:T(8,128)(2,1)S(1)} %bitcast.216) | data formatting | bytes 3276800
  71.4 0.9 convolution_convert_fusion.1
  72.2 1.6 %copy.83 = bf16[80,8,10,128]{3,1,2,0:T(8,128)(2,1)} copy(bf16[80,8,10,128]{3,2,1,0:T(8,128)(2,1)S(1)} %bitcast.213) | data formatting | bytes 3276800
  73.8 47.8 %shard_map.60 = (bf16[640,1280]{1,0:T(8,128)(2,1)}, f32[8,128]{1,0:T(8,128)}) custom-call(bf16[640,640]{1,0:T(8,128)(2,1)} %get-tuple-element.61.refs_0_, bf16[640,640]{1,0:T(8,128)(2,1)} %get-tuple-element.60.refs_1_, bf16[640,640]{1,0:T(8,128)(2,1)} %get-tuple-element.59.refs_2_, bf16[640,640]{1,0:T(8,128)(2,1)} %get-tuple-element.58.refs_3_, ...), custom_call_target="tpu_custom_call" | custom-call | tf_op jit(solution)/shard_map/pallas_call | solution.py:273
  121.6 1.2 slice.102
  123.5 2.7 %copy.88 = bf16[640,1280]{1,0:T(8,128)(2,1)} copy(bf16[640,1280]{1,0:T(8,128)(2,1)} %get-tuple-element.64) | data formatting | bytes 3276800
  (18 shorter events, 2.7 us)
Async XLA Ops:
  3.4 0.6 copy-start.1
  60.2 2.2 %copy-start = (bf16[4,2,8,128,128]{4,3,2,1,0:T(8,128)(2,1)S(1)}, bf16[4,2,8,128,128]{4,3,2,1,0:T(8,128)(2,1)}, u32[]{:S(2)}) copy-start(bf16[4,2,8,128,128]{4,3,2,1,0:T(8,128)(2,1)} %get-tuple-element.35) | copy-start | bytes 6291460

commit v12 on v6

--- a/solution.py
+++ b/solution.py
@@ -159,7 +159,7 @@
     )(blocks, meta)
 
 
-def trace_kernel(row_count, col_count, groups,
+def trace_kernel(row_count, col_count, groups, scale_width,
                  term_ref, out_ref, row_buf, col_buf, send_sem, recv_sem, col_send, col_recv):
     r = lax.axis_index("row")
     c = lax.axis_index("col")
@@ -240,18 +240,18 @@
             def _(cc=cc):
                 row_copies[cc].wait_send()
 
-    total = jnp.zeros(out_ref.shape, jnp.float32)
+    total = jnp.zeros(col_buf.shape[1:], jnp.float32)
     for rr in range(row_count):
         total = total + col_buf[rr]
-    out_ref[...] = total
-
-
-def trace_total(term, row_count, col_count, groups):
+    out_ref[...] = total[0:1, 0:1] / math.sqrt(row_count * RB * scale_width)
+
+
+def trace_total(term, row_count, col_count, groups, width):
     tile = jnp.broadcast_to(term, (8, 128))
     vmem = pl.BlockSpec(memory_space=pltpu.VMEM)
     out = pl.pallas_call(
-        functools.partial(trace_kernel, row_count, col_count, groups),
-        out_shape=jax.ShapeDtypeStruct((8, 128), jnp.float32),
+        functools.partial(trace_kernel, row_count, col_count, groups, width),
+        out_shape=jax.ShapeDtypeStruct((1, 1), jnp.float32),
         in_specs=[vmem],
         out_specs=vmem,
         scratch_shapes=[
@@ -264,7 +264,7 @@
         ],
         compiler_params=pltpu.CompilerParams(collective_id=1, has_side_effects=True),
     )(tile)
-    return out[0, 0]
+    return out.reshape(())
 
 
 def body(blocks, block_rows, block_cols, counts):
@@ -299,8 +299,7 @@
     start = jnp.clip(shift_amount, 0, groups - 1) * RB * width
     window = lax.dynamic_slice_in_dim(totals, start, RB * width, 1)
     term = jnp.where(valid, jnp.trace(window), jnp.zeros((), jnp.float32))
-    overall = trace_total(term, row_count, col_count, groups)
-    trace_value = overall / math.sqrt(row_count * RB * width)
+    trace_value = trace_total(term, row_count, col_count, groups, width)
     return (totals.astype(jnp.bfloat16), trace_value)
 
 

time: 114 us -> 113 us (level)
  local copies, waits for them, and re-layouts: 7.33 us -> 6.12 us
    slice x1 -> x0, local copies, waits for them, and re-layouts: 1.2 us -> none  [trace_total(): return out[0, 0]]
where the time goes in v12:
time: 113 us
  Pallas kernels  87.7 us (78%)
  matrix products  12.7 us (11%)
  local copies, waits for them, and re-layouts  6.12 us (5%)
  between operations  3.27 us (3%)
  other arithmetic  2.92 us (3%)
    pallas_call x1, Pallas kernels, exchange(): pl.pallas_call(functools.partial(exchange_kernel, row_count, col_count, g...  49.9 us
    pallas_call x1, Pallas kernels, trace_total(): pl.pallas_call(functools.partial(trace_kernel, row_count, col_count, grou...  37.9 us
    dot_general x4, matrix products, body(): jnp.dot(left_dense, right_dense, preferred_element_type=jnp.float32)  7.16 us
    dot_general x8, matrix products, densify(): jnp.dot(onehot, pieces.reshape(count, width * width), preferred_element_t...  5.52 us
    unnamed x8, local copies, waits for them, and re-layouts  3.68 us

profile of v12, /device:TPU:1, one launch (start us, length us, event | category | flops | bytes accessed | tf_op | source)
XLA Modules:
  0.0 112.7 jit_solution(13810947129668533037)
XLA Ops:
  0.6 0.8 bitcast_select_fusion
  1.4 0.7 iota_compare_fusion.1
  2.4 0.7 multiply_add_fusion.2
  3.3 0.6 copy-done.1
  3.9 49.9 %shard_map.59 = (bf16[4,8,128,128]{3,2,1,0:T(8,128)(2,1)}, bf16[4,2,8,128,128]{4,3,2,1,0:T(8,128)(2,1)}, s32[4,8,128]{2,1,0:T(8,128)}, s32[4,8,128]{2,1,0:T(8,128)}) custom-call(bf16[2,8,128,128]{3,2,1,0:T(8,128)(2,1)} %bitcast.229, s32[8,128]{1,0:T(8,128)} %copy-done.1), custom_call_target="tpu_custom_call" | custom-call | tf_op jit(solution)/shard_map/pallas_call | solution.py:144
  53.8 1.7 %slice_bitcast_fusion = (bf16[2,8,128,128]{3,2,1,0:T(8,128)(2,1)S(1)}, bf16[2,8,128,128]{3,2,1,0:T(8,128)(2,1)S(1)}, bf16[2,8,128,128]{3,2,1,0:T(8,128)(2,1)S(1)}, bf16[2,8,128,128]{3,2,1,0:T(8,128)(2,1)S(1)}) fusion(bf16[4,2,8,128,128]{4,3,2,1,0:T(8,128)(2,1)} %get-tuple-element.33), kind=kLoop, calls=%fused_computation.42 | loop fusion | bytes 4194304
  55.5 0.7 bitcast_bitcast_fusion.2
  56.2 0.7 slice_bitcast_fusion.8
  56.9 0.9 convolution_convert_fusion.3
  57.8 0.7 slice_bitcast_fusion.9
  58.5 0.5 convolution_convert_fusion.7
  59.1 1.5 %fusion.6 = f32[640,1280]{1,0:T(8,128)S(1)} fusion(bf16[80,8,10,128]{3,2,1,0:T(8,128)(2,1)S(1)} %bitcast.227, bf16[80,8,5,128]{3,2,1,0:T(8,128)(2,1)S(1)} %bitcast.228), kind=kOutput, calls=%fused_computation.13 | convolution fusion | flops 1048576000 | bytes 5734400 | tf_op jit(solution)/shard_map/dot_general | solution.py:296
  60.5 0.9 convolution_convert_fusion.2
  61.4 0.5 convolution_convert_fusion.6
  61.9 1.5 %convolution_add_fusion.2 = f32[640,1280]{1,0:T(8,128)S(1)} fusion(f32[640,1280]{1,0:T(8,128)S(1)} %fusion.6, bf16[80,8,10,128]{3,2,1,0:T(8,128)(2,1)S(1)} %bitcast.222, bf16[80,8,5,128]{3,2,1,0:T(8,128)(2,1)S(1)} %bitcast.224), kind=kOutput, calls=%fused_computation.2 | convolution fusion | flops 1049395200 | bytes 9011200 | tf_op jit(solution)/shard_map/dot_general | solution.py:296
  63.4 0.7 bitcast_bitcast_fusion
  64.1 0.9 convolution_convert_fusion.1
  65.0 0.5 convolution_convert_fusion.5
  65.5 1.5 %convolution_add_fusion.1 = f32[640,1280]{1,0:T(8,128)S(1)} fusion(f32[640,1280]{1,0:T(8,128)S(1)} %convolution_add_fusion.2, bf16[80,8,10,128]{3,2,1,0:T(8,128)(2,1)S(1)} %bitcast.223, bf16[80,8,5,128]{3,2,1,0:T(8,128)(2,1)S(1)} %bitcast.225), kind=kOutput, calls=%fused_computation.1 | convolution fusion | flops 1049395200 | bytes 9011200 | tf_op jit(solution)/shard_map/dot_general | solution.py:296
  67.0 0.9 convolution_convert_fusion
  68.4 2.7 %fusion.57 = (bf16[640,1280]{1,0:T(8,128)(2,1)}, f32[640,1280]{1,0:T(8,128)S(1)}) fusion(f32[640,1280]{1,0:T(8,128)S(1)} %convolution_add_fusion.1, bf16[80,8,10,128]{3,2,1,0:T(8,128)(2,1)S(1)} %bitcast.221, bf16[80,8,5,128]{3,2,1,0:T(8,128)(2,1)S(1)} %bitcast.226), kind=kOutput, calls=%fused_computation.106 | convolution fusion | flops 1050214400 | bytes 10649600 | tf_op jit(solution)/shard_map/dot_general | solution.py:296
  71.1 0.7 select_reduce_fusion
  72.5 0.6 broadcast_in_dim.28.term_ref
  73.1 37.9 %shard_map.60 = f32[1,1]{1,0:T(1,128)} custom-call(f32[8,128]{1,0:T(8,128)} %broadcast_in_dim.28.term_ref), custom_call_target="tpu_custom_call" | custom-call | tf_op jit(solution)/shard_map/pallas_call | solution.py:252
  (16 shorter events, 1.1 us)
Async XLA Ops:
  3.3 0.6 copy-start.1
  55.5 2.3 %copy-start = (bf16[4,8,128,128]{3,2,1,0:T(8,128)(2,1)S(1)}, bf16[4,8,128,128]{3,2,1,0:T(8,128)(2,1)}, u32[]{:S(2)}) copy-start(bf16[4,8,128,128]{3,2,1,0:T(8,128)(2,1)} %get-tuple-element.31) | copy-start | bytes 3145732

commit v13 on v12

--- a/solution.py
+++ b/solution.py
@@ -247,7 +247,7 @@
 
 
 def trace_total(term, row_count, col_count, groups, width):
-    tile = jnp.broadcast_to(term, (8, 128))
+    tile = term.reshape(1, 1)
     vmem = pl.BlockSpec(memory_space=pltpu.VMEM)
     out = pl.pallas_call(
         functools.partial(trace_kernel, row_count, col_count, groups, width),
@@ -255,8 +255,8 @@
         in_specs=[vmem],
         out_specs=vmem,
         scratch_shapes=[
-            pltpu.VMEM((8, 128), jnp.float32),
-            pltpu.VMEM((row_count, 8, 128), jnp.float32),
+            pltpu.VMEM((1, 1), jnp.float32),
+            pltpu.VMEM((row_count, 1, 1), jnp.float32),
             pltpu.SemaphoreType.DMA((col_count,)),
             pltpu.SemaphoreType.DMA((1,)),
             pltpu.SemaphoreType.DMA((row_count,)),

time: 113 us -> 111 us (0.982)
    pallas_call x1, Pallas kernels: 37.9 us -> 36.7 us  [trace_total(): pl.pallas_call(functools.partial(trace_kernel, row_count, col_count, grou...]
where the time goes in v13:
time: 111 us
  Pallas kernels  86.6 us (78%)
  matrix products  12.7 us (11%)
  local copies, waits for them, and re-layouts  5.54 us (5%)
  between operations  3.15 us (3%)
  other arithmetic  2.92 us (3%)
    pallas_call x1, Pallas kernels, exchange(): pl.pallas_call(functools.partial(exchange_kernel, row_count, col_count, g...  49.9 us
    pallas_call x1, Pallas kernels, trace_total(): pl.pallas_call(functools.partial(trace_kernel, row_count, col_count, grou...  36.7 us
    dot_general x4, matrix products, body(): jnp.dot(left_dense, right_dense, preferred_element_type=jnp.float32)  7.16 us
    dot_general x8, matrix products, densify(): jnp.dot(onehot, pieces.reshape(count, width * width), preferred_element_t...  5.52 us
    unnamed x8, local copies, waits for them, and re-layouts  3.68 us

profile of v13, /device:TPU:1, one launch (start us, length us, event | category | flops | bytes accessed | tf_op | source)
XLA Modules:
  0.0 110.9 jit_solution(1717369722650109278)
XLA Ops:
  0.6 0.8 bitcast_select_fusion
  1.4 0.7 iota_compare_fusion.1
  2.4 0.7 multiply_add_fusion.2
  3.3 0.6 copy-done.1
  3.9 49.9 %shard_map.59 = (bf16[4,8,128,128]{3,2,1,0:T(8,128)(2,1)}, bf16[4,2,8,128,128]{4,3,2,1,0:T(8,128)(2,1)}, s32[4,8,128]{2,1,0:T(8,128)}, s32[4,8,128]{2,1,0:T(8,128)}) custom-call(bf16[2,8,128,128]{3,2,1,0:T(8,128)(2,1)} %bitcast.230, s32[8,128]{1,0:T(8,128)} %copy-done.1), custom_call_target="tpu_custom_call" | custom-call | tf_op jit(solution)/shard_map/pallas_call | solution.py:144
  53.8 1.7 %slice_bitcast_fusion = (bf16[2,8,128,128]{3,2,1,0:T(8,128)(2,1)S(1)}, bf16[2,8,128,128]{3,2,1,0:T(8,128)(2,1)S(1)}, bf16[2,8,128,128]{3,2,1,0:T(8,128)(2,1)S(1)}, bf16[2,8,128,128]{3,2,1,0:T(8,128)(2,1)S(1)}) fusion(bf16[4,2,8,128,128]{4,3,2,1,0:T(8,128)(2,1)} %get-tuple-element.33), kind=kLoop, calls=%fused_computation.42 | loop fusion | bytes 4194304
  55.5 0.7 bitcast_bitcast_fusion.2
  56.2 0.7 slice_bitcast_fusion.8
  56.9 0.9 convolution_convert_fusion.3
  57.8 0.7 slice_bitcast_fusion.9
  58.5 0.5 convolution_convert_fusion.7
  59.1 1.5 %fusion.6 = f32[640,1280]{1,0:T(8,128)S(1)} fusion(bf16[80,8,10,128]{3,2,1,0:T(8,128)(2,1)S(1)} %bitcast.228, bf16[80,8,5,128]{3,2,1,0:T(8,128)(2,1)S(1)} %bitcast.229), kind=kOutput, calls=%fused_computation.13 | convolution fusion | flops 1048576000 | bytes 5734400 | tf_op jit(solution)/shard_map/dot_general | solution.py:296
  60.5 0.9 convolution_convert_fusion.2
  61.4 0.5 convolution_convert_fusion.6
  61.9 1.5 %convolution_add_fusion.2 = f32[640,1280]{1,0:T(8,128)S(1)} fusion(f32[640,1280]{1,0:T(8,128)S(1)} %fusion.6, bf16[80,8,10,128]{3,2,1,0:T(8,128)(2,1)S(1)} %bitcast.223, bf16[80,8,5,128]{3,2,1,0:T(8,128)(2,1)S(1)} %bitcast.225), kind=kOutput, calls=%fused_computation.2 | convolution fusion | flops 1049395200 | bytes 9011200 | tf_op jit(solution)/shard_map/dot_general | solution.py:296
  63.4 0.7 bitcast_bitcast_fusion
  64.1 0.9 convolution_convert_fusion.1
  65.0 0.5 convolution_convert_fusion.5
  65.5 1.5 %convolution_add_fusion.1 = f32[640,1280]{1,0:T(8,128)S(1)} fusion(f32[640,1280]{1,0:T(8,128)S(1)} %convolution_add_fusion.2, bf16[80,8,10,128]{3,2,1,0:T(8,128)(2,1)S(1)} %bitcast.224, bf16[80,8,5,128]{3,2,1,0:T(8,128)(2,1)S(1)} %bitcast.226), kind=kOutput, calls=%fused_computation.1 | convolution fusion | flops 1049395200 | bytes 9011200 | tf_op jit(solution)/shard_map/dot_general | solution.py:296
  67.0 0.9 convolution_convert_fusion
  67.9 0.5 convolution_convert_fusion.4
  68.4 2.7 %fusion.57 = (bf16[640,1280]{1,0:T(8,128)(2,1)}, f32[640,1280]{1,0:T(8,128)S(1)}) fusion(f32[640,1280]{1,0:T(8,128)S(1)} %convolution_add_fusion.1, bf16[80,8,10,128]{3,2,1,0:T(8,128)(2,1)S(1)} %bitcast.222, bf16[80,8,5,128]{3,2,1,0:T(8,128)(2,1)S(1)} %bitcast.227), kind=kOutput, calls=%fused_computation.106 | convolution fusion | flops 1050214400 | bytes 10649600 | tf_op jit(solution)/shard_map/dot_general | solution.py:296
  71.1 0.7 select_reduce_fusion
  72.5 36.7 %shard_map.60 = f32[1,1]{1,0:T(1,128)} custom-call(f32[1,1]{1,0:T(1,128)} %bitcast.55.term_ref), custom_call_target="tpu_custom_call" | custom-call | tf_op jit(solution)/shard_map/pallas_call | solution.py:252
  (15 shorter events, 0.6 us)
Async XLA Ops:
  3.3 0.6 copy-start.1
  55.5 2.3 %copy-start = (bf16[4,8,128,128]{3,2,1,0:T(8,128)(2,1)S(1)}, bf16[4,8,128,128]{3,2,1,0:T(8,128)(2,1)}, u32[]{:S(2)}) copy-start(bf16[4,8,128,128]{3,2,1,0:T(8,128)(2,1)} %get-tuple-element.31) | copy-start | bytes 3145732

commit v14 on v13

--- a/solution.py
+++ b/solution.py
@@ -149,7 +149,7 @@
             jax.ShapeDtypeStruct((STEPS,) + meta.shape, meta.dtype),
             jax.ShapeDtypeStruct((STEPS,) + meta.shape, meta.dtype),
         ),
-        in_specs=[vmem, vmem],
+        in_specs=[pl.BlockSpec(memory_space=pl.ANY), vmem],
         out_specs=(vmem, vmem, vmem, vmem),
         scratch_shapes=[
             pltpu.SemaphoreType.DMA(((3 + groups) * STEPS,)),
@@ -284,9 +284,11 @@
         live, block_rows[0, 0] * (groups * RB) + block_cols[0, 0] + offsets, -1
     ).reshape(-1)
     left_places = lax.dynamic_index_in_dim(left_places_all, lower, 0, keepdims=False)
-    meta = jnp.zeros((8, 128), jnp.int32)
-    meta = meta.at[0, :slot_count].set(left_places)
-    meta = meta.at[1, : groups * slot_count].set(right_places)
+    meta = jnp.stack([
+        jnp.pad(left_places, (0, 128 - slot_count)),
+        jnp.pad(right_places, (0, 128 - groups * slot_count)),
+    ])
+    meta = jnp.pad(meta, ((0, 6), (0, 0)))
     recv_l, recv_r, recv_ml, recv_mr = exchange(blocks[0, 0], meta, row_count, col_count)
     totals = jnp.zeros((RB * width, groups * RB * width), jnp.float32)
     for step in range(STEPS):

time: 111 us -> 109 us (0.982)
  local copies, waits for them, and re-layouts: 5.54 us -> 3.88 us
    unnamed x8 -> x4, local copies, waits for them, and re-layouts: 3.68 us -> 1.55 us
where the time goes in v14:
time: 109 us
  Pallas kernels  86.2 us (79%)
  matrix products  12.7 us (12%)
  local copies, waits for them, and re-layouts  3.88 us (4%)
  between operations  3.12 us (3%)
  other arithmetic  2.93 us (3%)
    pallas_call x1, Pallas kernels, exchange(): pl.pallas_call(functools.partial(exchange_kernel, row_count, col_count, g...  49.8 us
    pallas_call x1, Pallas kernels, trace_total(): pl.pallas_call(functools.partial(trace_kernel, row_count, col_count, grou...  36.4 us
    dot_general x4, matrix products, body(): jnp.dot(left_dense, right_dense, preferred_element_type=jnp.float32)  7.16 us
    dot_general x8, matrix products, densify(): jnp.dot(onehot, pieces.reshape(count, width * width), preferred_element_t...  5.53 us

profile of v14, /device:TPU:1, one launch (start us, length us, event | category | flops | bytes accessed | tf_op | source)
XLA Modules:
  0.0 108.8 jit_solution(7614448442110899366)
XLA Ops:
  0.6 0.8 bitcast_select_fusion
  1.4 0.7 iota_compare_fusion.1
  2.2 0.1 lt.41
  2.4 0.7 multiply_add_fusion.2
  3.2 0.6 pad.14.meta_ref
  3.8 49.8 %shard_map.59 = (bf16[4,8,128,128]{3,2,1,0:T(8,128)(2,1)}, bf16[4,2,8,128,128]{4,3,2,1,0:T(8,128)(2,1)}, s32[4,8,128]{2,1,0:T(8,128)}, s32[4,8,128]{2,1,0:T(8,128)}) custom-call(bf16[2,8,128,128]{3,2,1,0:T(8,128)(2,1)} %bitcast.252, s32[8,128]{1,0:T(8,128)} %pad.14.meta_ref), custom_call_target="tpu_custom_call" | custom-call | tf_op jit(solution)/shard_map/pallas_call | solution.py:144
  53.6 1.4 %slice_bitcast_fusion.4 = (bf16[1,8,128,128]{3,2,1,0:T(8,128)(2,1)S(1)}, bf16[1,8,128,128]{3,2,1,0:T(8,128)(2,1)S(1)}, bf16[1,8,128,128]{3,2,1,0:T(8,128)(2,1)S(1)}, bf16[1,8,128,128]{3,2,1,0:T(8,128)(2,1)S(1)}) fusion(bf16[4,8,128,128]{3,2,1,0:T(8,128)(2,1)} %get-tuple-element.7), kind=kLoop, calls=%fused_computation.54 | loop fusion | bytes 2097152
  55.0 0.7 slice_bitcast_fusion.9
  55.7 0.5 convolution_convert_fusion.7
  56.2 0.1 slice_bitcast_fusion
  56.4 0.7 slice_bitcast_fusion.8
  57.1 0.9 convolution_convert_fusion.3
  58.0 1.5 %fusion.6 = f32[640,1280]{1,0:T(8,128)S(1)} fusion(bf16[80,8,10,128]{3,2,1,0:T(8,128)(2,1)S(1)} %bitcast.250, bf16[80,8,5,128]{3,2,1,0:T(8,128)(2,1)S(1)} %bitcast.251), kind=kOutput, calls=%fused_computation.13 | convolution fusion | flops 1048576000 | bytes 5734400 | tf_op jit(solution)/shard_map/dot_general | solution.py:298
  59.5 0.9 convolution_convert_fusion.2
  60.3 0.5 convolution_convert_fusion.6
  60.9 1.5 %convolution_add_fusion.2 = f32[640,1280]{1,0:T(8,128)S(1)} fusion(f32[640,1280]{1,0:T(8,128)S(1)} %fusion.6, bf16[80,8,10,128]{3,2,1,0:T(8,128)(2,1)S(1)} %bitcast.245, bf16[80,8,5,128]{3,2,1,0:T(8,128)(2,1)S(1)} %bitcast.247), kind=kOutput, calls=%fused_computation.2 | convolution fusion | flops 1049395200 | bytes 9011200 | tf_op jit(solution)/shard_map/dot_general | solution.py:298
  62.4 0.9 convolution_convert_fusion.1
  63.2 0.5 convolution_convert_fusion.5
  63.8 1.5 %convolution_add_fusion.1 = f32[640,1280]{1,0:T(8,128)S(1)} fusion(f32[640,1280]{1,0:T(8,128)S(1)} %convolution_add_fusion.2, bf16[80,8,10,128]{3,2,1,0:T(8,128)(2,1)S(1)} %bitcast.246, bf16[80,8,5,128]{3,2,1,0:T(8,128)(2,1)S(1)} %bitcast.248), kind=kOutput, calls=%fused_computation.1 | convolution fusion | flops 1049395200 | bytes 9011200 | tf_op jit(solution)/shard_map/dot_general | solution.py:298
  65.3 0.9 convolution_convert_fusion
  66.2 0.5 convolution_convert_fusion.4
  66.7 2.7 %fusion.57 = (bf16[640,1280]{1,0:T(8,128)(2,1)}, f32[640,1280]{1,0:T(8,128)S(1)}) fusion(f32[640,1280]{1,0:T(8,128)S(1)} %convolution_add_fusion.1, bf16[80,8,10,128]{3,2,1,0:T(8,128)(2,1)S(1)} %bitcast.244, bf16[80,8,5,128]{3,2,1,0:T(8,128)(2,1)S(1)} %bitcast.249), kind=kOutput, calls=%fused_computation.109 | convolution fusion | flops 1050214400 | bytes 10649600 | tf_op jit(solution)/shard_map/dot_general | solution.py:298
  69.3 0.7 select_reduce_fusion
  70.7 36.4 %shard_map.60 = f32[1,1]{1,0:T(1,128)} custom-call(f32[1,1]{1,0:T(1,128)} %bitcast.58.term_ref), custom_call_target="tpu_custom_call" | custom-call | tf_op jit(solution)/shard_map/pallas_call | solution.py:252
  (12 shorter events, 0.3 us)
Async XLA Ops:
  53.6 2.6 %copy-start = (bf16[4,2,8,128,128]{4,3,2,1,0:T(8,128)(2,1)S(1)}, bf16[4,2,8,128,128]{4,3,2,1,0:T(8,128)(2,1)}, u32[]{:S(2)}) copy-start(bf16[4,2,8,128,128]{4,3,2,1,0:T(8,128)(2,1)} %get-tuple-element.9) | copy-start | bytes 6291460

commit v15 on v14

--- a/solution.py
+++ b/solution.py
@@ -288,7 +288,6 @@
         jnp.pad(left_places, (0, 128 - slot_count)),
         jnp.pad(right_places, (0, 128 - groups * slot_count)),
     ])
-    meta = jnp.pad(meta, ((0, 6), (0, 0)))
     recv_l, recv_r, recv_ml, recv_mr = exchange(blocks[0, 0], meta, row_count, col_count)
     totals = jnp.zeros((RB * width, groups * RB * width), jnp.float32)
     for step in range(STEPS):

time: 109 us -> 108 us (level)
  local copies, waits for them, and re-layouts: 3.88 us -> 2.59 us
where the time goes in v15:
time: 108 us
  Pallas kernels  86 us (80%)
  matrix products  12.7 us (12%)
  other arithmetic  3.49 us (3%)
  between operations  3.27 us (3%)
  local copies, waits for them, and re-layouts  2.59 us (2%)
    pallas_call x1, Pallas kernels, exchange(): pl.pallas_call(functools.partial(exchange_kernel, row_count, col_count, g...  49.6 us
    pallas_call x1, Pallas kernels, trace_total(): pl.pallas_call(functools.partial(trace_kernel, row_count, col_count, grou...  36.4 us
    dot_general x4, matrix products, body(): jnp.dot(left_dense, right_dense, preferred_element_type=jnp.float32)  7.16 us
    dot_general x8, matrix products, densify(): jnp.dot(onehot, pieces.reshape(count, width * width), preferred_element_t...  5.53 us

profile of v15, /device:TPU:1, one launch (start us, length us, event | category | flops | bytes accessed | tf_op | source)
XLA Modules:
  0.0 108.0 jit_solution(15433841301847136390)
XLA Ops:
  0.6 0.8 bitcast_select_fusion
  1.4 0.7 iota_compare_fusion.1
  2.2 0.1 lt.41
  2.3 0.1 add.69
  2.4 0.7 multiply_add_fusion.2
  3.2 0.6 pad_add_fusion.meta_ref
  3.8 49.6 %shard_map.59 = (bf16[4,8,128,128]{3,2,1,0:T(8,128)(2,1)}, bf16[4,2,8,128,128]{4,3,2,1,0:T(8,128)(2,1)}, s32[4,2,128]{2,1,0:T(2,128)}, s32[4,2,128]{2,1,0:T(2,128)}) custom-call(bf16[2,8,128,128]{3,2,1,0:T(8,128)(2,1)} %bitcast.252, s32[2,128]{1,0:T(2,128)} %pad_add_fusion.meta_ref), custom_call_target="tpu_custom_call" | custom-call | tf_op jit(solution)/shard_map/pallas_call | solution.py:144
  53.4 1.4 %slice_bitcast_fusion.4 = (bf16[1,8,128,128]{3,2,1,0:T(8,128)(2,1)S(1)}, bf16[1,8,128,128]{3,2,1,0:T(8,128)(2,1)S(1)}, bf16[1,8,128,128]{3,2,1,0:T(8,128)(2,1)S(1)}, bf16[1,8,128,128]{3,2,1,0:T(8,128)(2,1)S(1)}) fusion(bf16[4,8,128,128]{3,2,1,0:T(8,128)(2,1)} %get-tuple-element.7), kind=kLoop, calls=%fused_computation.54 | loop fusion | bytes 2097152
  54.8 0.7 slice_bitcast_fusion.9
  55.5 0.5 convolution_convert_fusion.7
  56.0 0.1 slice_bitcast_fusion
  56.2 0.9 convolution_convert_fusion.3
  57.1 1.5 %fusion.6 = f32[640,1280]{1,0:T(8,128)S(1)} fusion(bf16[80,8,10,128]{3,2,1,0:T(8,128)(2,1)S(1)} %bitcast.250, bf16[80,8,5,128]{3,2,1,0:T(8,128)(2,1)S(1)} %bitcast.251), kind=kOutput, calls=%fused_computation.13 | convolution fusion | flops 1048576000 | bytes 5734400 | tf_op jit(solution)/shard_map/dot_general | solution.py:297
  58.6 0.9 convolution_convert_fusion.2
  59.4 0.5 convolution_convert_fusion.6
  60.0 1.5 %convolution_add_fusion.2 = f32[640,1280]{1,0:T(8,128)S(1)} fusion(f32[640,1280]{1,0:T(8,128)S(1)} %fusion.6, bf16[80,8,10,128]{3,2,1,0:T(8,128)(2,1)S(1)} %bitcast.245, bf16[80,8,5,128]{3,2,1,0:T(8,128)(2,1)S(1)} %bitcast.247), kind=kOutput, calls=%fused_computation.2 | convolution fusion | flops 1049395200 | bytes 9011200 | tf_op jit(solution)/shard_map/dot_general | solution.py:297
  61.5 0.9 convolution_convert_fusion.1
  62.3 0.5 convolution_convert_fusion.5
  62.9 1.5 %convolution_add_fusion.1 = f32[640,1280]{1,0:T(8,128)S(1)} fusion(f32[640,1280]{1,0:T(8,128)S(1)} %convolution_add_fusion.2, bf16[80,8,10,128]{3,2,1,0:T(8,128)(2,1)S(1)} %bitcast.246, bf16[80,8,5,128]{3,2,1,0:T(8,128)(2,1)S(1)} %bitcast.248), kind=kOutput, calls=%fused_computation.1 | convolution fusion | flops 1049395200 | bytes 9011200 | tf_op jit(solution)/shard_map/dot_general | solution.py:297
  64.4 0.9 convolution_convert_fusion
  65.3 0.5 convolution_convert_fusion.4
  65.8 2.7 %fusion.57 = (bf16[640,1280]{1,0:T(8,128)(2,1)}, f32[640,1280]{1,0:T(8,128)S(1)}) fusion(f32[640,1280]{1,0:T(8,128)S(1)} %convolution_add_fusion.1, bf16[80,8,10,128]{3,2,1,0:T(8,128)(2,1)S(1)} %bitcast.244, bf16[80,8,5,128]{3,2,1,0:T(8,128)(2,1)S(1)} %bitcast.249), kind=kOutput, calls=%fused_computation.109 | convolution fusion | flops 1050214400 | bytes 10649600 | tf_op jit(solution)/shard_map/dot_general | solution.py:297
  68.5 0.7 select_reduce_fusion
  69.8 36.4 %shard_map.60 = f32[1,1]{1,0:T(1,128)} custom-call(f32[1,1]{1,0:T(1,128)} %bitcast.58.term_ref), custom_call_target="tpu_custom_call" | custom-call | tf_op jit(solution)/shard_map/pallas_call | solution.py:252
  (13 shorter events, 0.2 us)
Async XLA Ops:
  53.4 2.6 %copy-start = (bf16[4,2,8,128,128]{4,3,2,1,0:T(8,128)(2,1)S(1)}, bf16[4,2,8,128,128]{4,3,2,1,0:T(8,128)(2,1)}, u32[]{:S(2)}) copy-start(bf16[4,2,8,128,128]{4,3,2,1,0:T(8,128)(2,1)} %get-tuple-element.9) | copy-start | bytes 6291460
  55.5 0.7 copy-start.1

commit v16 on v15

--- a/solution.py
+++ b/solution.py
@@ -285,8 +285,8 @@
     ).reshape(-1)
     left_places = lax.dynamic_index_in_dim(left_places_all, lower, 0, keepdims=False)
     meta = jnp.stack([
-        jnp.pad(left_places, (0, 128 - slot_count)),
-        jnp.pad(right_places, (0, 128 - groups * slot_count)),
+        jnp.pad(left_places, (0, (groups - 1) * slot_count)),
+        right_places,
     ])
     recv_l, recv_r, recv_ml, recv_mr = exchange(blocks[0, 0], meta, row_count, col_count)
     totals = jnp.zeros((RB * width, groups * RB * width), jnp.float32)

time: 108 us -> 109 us (level)
    unnamed x6 -> x10, local copies, waits for them, and re-layouts: 1.56 us -> 3.1 us
where the time goes in v16:
time: 109 us
  Pallas kernels  86 us (79%)
  matrix products  12.7 us (12%)
  other arithmetic  3.49 us (3%)
  local copies, waits for them, and re-layouts  3.45 us (3%)
  between operations  3.31 us (3%)
    pallas_call x1, Pallas kernels, exchange(): pl.pallas_call(functools.partial(exchange_kernel, row_count, col_count, g...  49.6 us
    pallas_call x1, Pallas kernels, trace_total(): pl.pallas_call(functools.partial(trace_kernel, row_count, col_count, grou...  36.4 us
    dot_general x4, matrix products, body(): jnp.dot(left_dense, right_dense, preferred_element_type=jnp.float32)  7.16 us
    dot_general x8, matrix products, densify(): jnp.dot(onehot, pieces.reshape(count, width * width), preferred_element_t...  5.52 us
    unnamed x10, local copies, waits for them, and re-layouts  3.1 us

profile of v16, /device:TPU:1, one launch (start us, length us, event | category | flops | bytes accessed | tf_op | source)
XLA Modules:
  0.0 108.9 jit_solution(15825833745003259672)
XLA Ops:
  0.6 0.8 bitcast_select_fusion
  1.4 0.7 iota_compare_fusion.1
  2.2 0.1 lt.47
  2.3 0.1 add.79
  2.4 0.7 multiply_add_fusion.2
  3.2 0.6 pad_add_fusion.meta_ref
  3.8 49.6 %shard_map.59 = (bf16[4,8,128,128]{3,2,1,0:T(8,128)(2,1)}, bf16[4,2,8,128,128]{4,3,2,1,0:T(8,128)(2,1)}, s32[4,2,16]{2,1,0:T(2,128)}, s32[4,2,16]{2,1,0:T(2,128)}) custom-call(bf16[2,8,128,128]{3,2,1,0:T(8,128)(2,1)} %bitcast.234, s32[2,16]{1,0:T(2,128)} %pad_add_fusion.meta_ref), custom_call_target="tpu_custom_call" | custom-call | tf_op jit(solution)/shard_map/pallas_call | solution.py:144
  53.4 1.7 %slice_bitcast_fusion = (bf16[2,8,128,128]{3,2,1,0:T(8,128)(2,1)S(1)}, bf16[2,8,128,128]{3,2,1,0:T(8,128)(2,1)S(1)}, bf16[2,8,128,128]{3,2,1,0:T(8,128)(2,1)S(1)}, bf16[2,8,128,128]{3,2,1,0:T(8,128)(2,1)S(1)}) fusion(bf16[4,2,8,128,128]{4,3,2,1,0:T(8,128)(2,1)} %get-tuple-element.9), kind=kLoop, calls=%fused_computation.42 | loop fusion | bytes 4194304
  55.0 0.7 bitcast_bitcast_fusion.2
  55.8 0.9 convolution_convert_fusion.3
  56.8 0.5 convolution_convert_fusion.7
  57.3 1.5 %fusion.6 = f32[640,1280]{1,0:T(8,128)S(1)} fusion(bf16[80,8,10,128]{3,2,1,0:T(8,128)(2,1)S(1)} %bitcast.232, bf16[80,8,5,128]{3,2,1,0:T(8,128)(2,1)S(1)} %bitcast.233), kind=kOutput, calls=%fused_computation.13 | convolution fusion | flops 1048576000 | bytes 5734400 | tf_op jit(solution)/shard_map/dot_general | solution.py:297
  58.8 0.9 convolution_convert_fusion.2
  59.7 0.5 convolution_convert_fusion.6
  60.2 1.5 %convolution_add_fusion.2 = f32[640,1280]{1,0:T(8,128)S(1)} fusion(f32[640,1280]{1,0:T(8,128)S(1)} %fusion.6, bf16[80,8,10,128]{3,2,1,0:T(8,128)(2,1)S(1)} %bitcast.227, bf16[80,8,5,128]{3,2,1,0:T(8,128)(2,1)S(1)} %bitcast.229), kind=kOutput, calls=%fused_computation.2 | convolution fusion | flops 1049395200 | bytes 9011200 | tf_op jit(solution)/shard_map/dot_general | solution.py:297
  61.7 0.7 bitcast_bitcast_fusion
  62.4 0.9 convolution_convert_fusion.1
  63.3 0.5 convolution_convert_fusion.5
  63.8 1.5 %convolution_add_fusion.1 = f32[640,1280]{1,0:T(8,128)S(1)} fusion(f32[640,1280]{1,0:T(8,128)S(1)} %convolution_add_fusion.2, bf16[80,8,10,128]{3,2,1,0:T(8,128)(2,1)S(1)} %bitcast.228, bf16[80,8,5,128]{3,2,1,0:T(8,128)(2,1)S(1)} %bitcast.230), kind=kOutput, calls=%fused_computation.1 | convolution fusion | flops 1049395200 | bytes 9011200 | tf_op jit(solution)/shard_map/dot_general | solution.py:297
  65.3 0.9 convolution_convert_fusion
  66.2 0.5 convolution_convert_fusion.4
  66.7 2.7 %fusion.57 = (bf16[640,1280]{1,0:T(8,128)(2,1)}, f32[640,1280]{1,0:T(8,128)S(1)}) fusion(f32[640,1280]{1,0:T(8,128)S(1)} %convolution_add_fusion.1, bf16[80,8,10,128]{3,2,1,0:T(8,128)(2,1)S(1)} %bitcast.226, bf16[80,8,5,128]{3,2,1,0:T(8,128)(2,1)S(1)} %bitcast.231), kind=kOutput, calls=%fused_computation.108 | convolution fusion | flops 1050214400 | bytes 10649600 | tf_op jit(solution)/shard_map/dot_general | solution.py:297
  69.3 0.7 select_reduce_fusion
  70.7 36.4 %shard_map.60 = f32[1,1]{1,0:T(1,128)} custom-call(f32[1,1]{1,0:T(1,128)} %bitcast.57.term_ref), custom_call_target="tpu_custom_call" | custom-call | tf_op jit(solution)/shard_map/pallas_call | solution.py:252
  (17 shorter events, 0.3 us)
Async XLA Ops:
  53.4 2.4 %copy-start.2 = (s32[4,2,16]{2,1,0:T(2,128)S(1)}, s32[4,2,16]{2,1,0:T(2,128)}, u32[]{:S(2)}) copy-start(s32[4,2,16]{2,1,0:T(2,128)} %get-tuple-element.8) | copy-start | bytes 1540
  55.0 1.6 %copy-start = (bf16[4,8,128,128]{3,2,1,0:T(8,128)(2,1)S(1)}, bf16[4,8,128,128]{3,2,1,0:T(8,128)(2,1)}, u32[]{:S(2)}) copy-start(bf16[4,8,128,128]{3,2,1,0:T(8,128)(2,1)} %get-tuple-element.7) | copy-start | bytes 3145732
  55.8 1.0 copy-start.1
